TPU v7x, 32 devices: a whole 2x2x4 slice. The times are simulated.
32 devices in a mesh: groups: 2 (over y), row: 4 (over z), col: 2 (over x), sub: 2 (over core).
Axes of the slice: x: 2, y: 2, z: 4, core: 2. Of those that a mesh axis runs over, the one named last changes fastest.
Arguments:
- pixels: bfloat16 [4, 4096, 2048], P('groups', ('row', 'col', 'sub')), parts along dimension 0, may hold values from 0.019897461 to 1
Outputs:
- phase: float32 [4, 512, 256], P(('groups', 'sub'), 'row', 'col'), parts along dimension 0
- mean_flux: float32 [4, 512, 256], P(('groups', 'sub'), 'row', 'col'), parts along dimension 0
- spot_size: float32 [4, 512, 256], P(('groups', 'sub'), 'row', 'col'), parts along dimension 0
There are 2 independent parts, one for each index of `groups`. A program takes and returns all parts, laid end to end along the dimension named above; each array names one. Nothing has to cross between parts.
All inputs are finite; a program needn't handle non-finite values.
Results may differ from a plain program's by a relative error of at most 0.0011.
Values sent between devices are 32-bit elements; how exact they have to be, the bound alone decides.
No kernel may reach another device: no remote copies, remote signals or barrier semaphores. Data moves between devices by JAX's collectives and lax.ppermute only.
A program may use at most 128 MiB of HBM per device.

v0:
```python
import math

import jax
import jax.numpy as jnp
from jax import lax
from jax.sharding import PartitionSpec as P

PIX = 8
SUBN = 128
MARGIN = 8


damping = 2e-05


def with_halo(cells, sides, width):
    for axis, dim in sides:
        count = lax.axis_size(axis)
        ends = count - 1
        head = lax.slice_in_dim(cells, 0, width, axis=dim)
        tail = lax.slice_in_dim(cells, cells.shape[dim] - width, cells.shape[dim], axis=dim)
        cells = jnp.concatenate(
            [
                lax.ppermute(tail, axis, [(i, (i + 1) % count) for i in range(ends)]),
                cells,
                lax.ppermute(head, axis, [((i + 1) % count, i) for i in range(ends)]),
            ],
            axis=dim,
        )
    return cells


def moment_table():
    offset = jnp.arange(PIX, dtype=jnp.float32) - (PIX - 1) / 2.0
    table = jnp.stack([jnp.ones_like(offset), offset, offset * offset], 1)
    return (table, offset)


def make_basis(count):
    order = jnp.arange(1, count + 1, dtype=jnp.float32)
    angles = math.pi * order[:, None] * order[None, :] / (count + 1)
    vectors = jnp.sqrt(2.0 / (count + 1)) * jnp.sin(angles)
    spectrum = 2.0 - 2.0 * jnp.cos(math.pi * order / (count + 1))
    return (vectors, spectrum[:, None] + spectrum[None, :] + damping)


def coarse_matrix(blocks_down, blocks_across):
    number = blocks_down * blocks_across
    labels = jnp.arange(number, dtype=jnp.int32)
    block_row = labels // blocks_across
    block_col = labels % blocks_across
    apart = jnp.abs(block_row[:, None] - block_row[None, :]) + jnp.abs(
        block_col[:, None] - block_col[None, :]
    )
    touching = (apart == 1).astype(jnp.float32)
    laplace = jnp.diag(jnp.sum(touching, 1)) - touching
    return SUBN * laplace + damping * SUBN * SUBN * jnp.eye(number, dtype=jnp.float32)


def solve_windows(source, vectors, denominator):
    highest = lax.Precision.HIGHEST
    inner = jnp.einsum("ij,fjk->fik", vectors, source, precision=highest)
    inner = jnp.einsum("fik,kl->fil", inner, vectors, precision=highest) / denominator
    outer = jnp.einsum("ij,fjk->fik", vectors, inner, precision=highest)
    return jnp.einsum("fik,kl->fil", outer, vectors, precision=highest)


def split_columns(values, parts):
    frame_count, kind_count, stripe, grid_cols = values.shape
    return values.reshape(frame_count, kind_count, stripe, parts, grid_cols // parts)


def to_pieces(values, core_count):
    frame_count, kind_count, stripe, parts, piece_width = values.shape
    frame_half = frame_count // core_count
    grouped = values.reshape(core_count, frame_half, kind_count, stripe, parts, piece_width)
    grouped = jnp.transpose(grouped, (4, 0, 1, 2, 3, 5))
    return grouped.reshape(parts * core_count * frame_half, kind_count, stripe, piece_width)


def pack_rims(values, axis_dim):
    block_side = values.shape[axis_dim] - 2 * MARGIN
    head_part = lax.slice_in_dim(values, 0, MARGIN, axis=axis_dim)
    middle = lax.slice_in_dim(values, 2 * MARGIN, block_side, axis=axis_dim)
    tail_part = lax.slice_in_dim(
        values, block_side + MARGIN, block_side + 2 * MARGIN, axis=axis_dim
    )
    return jnp.concatenate([head_part, middle, tail_part], axis_dim)


def add_rims(values, extended, axis_dim):
    block_side = values.shape[axis_dim] - 2 * MARGIN
    own_part = lax.slice_in_dim(values, MARGIN, block_side + MARGIN, axis=axis_dim)
    first_part = lax.slice_in_dim(own_part, 0, MARGIN, axis=axis_dim) + lax.slice_in_dim(
        extended, 0, MARGIN, axis=axis_dim
    )
    middle = lax.slice_in_dim(own_part, MARGIN, block_side - MARGIN, axis=axis_dim)
    last_part = lax.slice_in_dim(
        own_part, block_side - MARGIN, block_side, axis=axis_dim
    ) + lax.slice_in_dim(extended, block_side + MARGIN, block_side + 2 * MARGIN, axis=axis_dim)
    return jnp.concatenate([first_part, middle, last_part], axis_dim)


def fold_columns(values):
    extended = with_halo(pack_rims(values, 2), (("col", 2),), MARGIN)
    return add_rims(values, extended, 2)


def fold_rowwise(values):
    extended = with_halo(pack_rims(values, 1), (("row", 1),), MARGIN)
    return add_rims(values, extended, 1)


def from_border(border):
    border_x = border[:, 0]
    border_y = border[:, 1]
    return (
        border_x[:, 1:-1, :-2]
        - border_x[:, 1:-1, 1:-1]
        + border_y[:, :-2, 1:-1]
        - border_y[:, 1:-1, 1:-1]
    )


def body(pixels):
    frame_count, pixel_rows, pixel_cols = pixels.shape
    stripe = pixel_rows // PIX
    grid_cols = pixel_cols // PIX
    block_rows = lax.axis_size("row")
    block_cols = lax.axis_size("col")
    core_count = lax.axis_size("sub")
    block_side = grid_cols // block_cols
    grid_rows = block_side * block_rows
    rim_width = MARGIN + 1
    table, offset = moment_table()
    blocks = pixels.reshape(frame_count, stripe, PIX, grid_cols, PIX)
    partial_value = jnp.einsum(
        "fiajb,bk->fkiaj", blocks, table.astype(jnp.bfloat16), preferred_element_type=jnp.float32
    )
    intensity = jnp.sum(partial_value[:, 0], 2)
    moment_x = jnp.sum(partial_value[:, 1], 2)
    moment_y = jnp.sum(partial_value[:, 0] * offset[None, None, :, None], 2)
    moment_two = jnp.sum(partial_value[:, 2], 2) + jnp.sum(
        partial_value[:, 0] * (offset * offset)[None, None, :, None], 2
    )
    slope_x = moment_x / intensity
    slope_y = moment_y / intensity
    spot_size = moment_two / intensity - slope_x * slope_x - slope_y * slope_y
    mean_flux = intensity / (PIX * PIX)
    position = lax.axis_index(("row", "col", "sub"))
    global_row = position * stripe + jnp.arange(stripe, dtype=jnp.int32)
    column = jnp.arange(grid_cols, dtype=jnp.int32)
    flow_x = jnp.where(column[None, None, :] < grid_cols - 1, slope_x, 0.0)
    flow_y = jnp.where(global_row[None, :, None] < grid_rows - 1, slope_y, 0.0)
    stacked = jnp.stack([flow_x, flow_y, mean_flux, spot_size], 1)
    received = lax.all_to_all(
        to_pieces(split_columns(stacked, block_cols), core_count),
        ("col", "sub"),
        split_axis=0,
        concat_axis=2,
        tiled=True,
    )
    flows = received[:, 0:2]
    extras = received[:, 2:4]
    border = with_halo(flows, (("row", 2), ("col", 3)), rim_width)
    source = from_border(border)
    own_sum = jnp.sum(source[:, MARGIN : MARGIN + block_side, MARGIN : MARGIN + block_side], (1, 2))
    right_hand = lax.all_gather(own_sum[None, :], ("row", "col"), axis=0, tiled=True)
    vectors, denominator = make_basis(block_side + 2 * MARGIN)
    solved = solve_windows(source, vectors, denominator)
    folded = fold_rowwise(fold_columns(solved))
    factor = jnp.linalg.cholesky(coarse_matrix(block_rows, block_cols))
    coarse_phase = jax.scipy.linalg.cho_solve((factor, True), right_hand)
    own_phase = lax.dynamic_slice_in_dim(coarse_phase, lax.axis_index(("row", "col")), 1, 0)[0]
    phase = folded + own_phase[:, None, None]
    return (phase, extras[:, 0], extras[:, 1])


def solution(mesh):
    placed = (P("groups", ("row", "col", "sub"), None),)
    return jax.shard_map(
        body,
        mesh=mesh,
        in_specs=placed,
        out_specs=(
            P(("groups", "sub"), "row", "col"),
            P(("groups", "sub"), "row", "col"),
            P(("groups", "sub"), "row", "col"),
        ),
        check_vma=False,
    )
```

profile of v0, /device:TPU:0, one launch (start us, length us, event | category | flops | bytes accessed | tf_op | source)
XLA Modules:
  0.0 133.9 jit_solution(6467780394615393911)
XLA Ops:
  0.7 42.1 %reshape.316 = bf16[2,32,8,256,8]{4,3,2,1,0:T(8,128)(2,1)} reshape(bf16[2,256,2048]{2,1,0:T(8,128)(2,1)} %param.1) | data formatting | bytes 4194304 | tf_op jit(solution)/shard_map/reshape | solution.py:136
  42.7 14.6 %convolution_bitcast_fusion = f32[2,3,32,8,256]{4,1,3,2,0:T(4,128)S(1)} fusion(bf16[2,32,8,256,8]{4,3,2,1,0:T(8,128)(2,1)} %reshape.316, bf16[8,1]{0,1:T(2,128)(2,1)S(1)} %get-tuple-element.40, bf16[8,1]{0,1:T(2,128)(2,1)S(1)} %get-tuple-element.41, bf16[3]{0:T(256)(128)(2,1)S(1)} %pad.18.clone), kind=kOutput, calls=%fused_computation | convolution fusion | flops 6291600 | bytes 3670054 | tf_op jit(solution)/shard_map/fiajb,bk->fkiaj/dot_general | solution.py:137
  57.3 3.2 %slice_reduce_fusion.1 = (f32[2,32,256]{2,1,0:T(8,128)S(1)}, f32[2,32,256]{2,1,0:T(8,128)S(1)}, f32[2,32,256]{2,1,0:T(8,128)S(1)}, f32[2,1,32,8,256]{4,1,3,2,0:T(1,128)S(1)}) fusion(f32[2,3,32,8,256]{4,1,3,2,0:T(4,128)S(1)} %convolution_bitcast_fusion), kind=kLoop, calls=%fused_computation.8 | loop fusion | flops 344064 | bytes 2293760 | tf_op jit(solution)/shard_map/reduce_sum | solution.py:141
  62.1 4.2 %all-to-all-start = ((f32[4,4,32,128]{3,2,1,0:T(8,128)}), f32[4,4,32,128]{3,2,1,0:T(8,128)S(1)}, u32[]{:S(2)}, u32[]{:S(2)}) async-start(f32[4,4,32,128]{3,2,1,0:T(8,128)} %bitcast.4), calls=%async_computation | async-start | bytes 524288 | tf_op jit(solution)/shard_map/all_to_all | solution.py:156
  68.6 3.7 %all-to-all-done = f32[4,4,32,128]{3,2,1,0:T(8,128)S(1)} async-done(((f32[4,4,32,128]{3,2,1,0:T(8,128)}), f32[4,4,32,128]{3,2,1,0:T(8,128)S(1)}, u32[]{:S(2)}, u32[]{:S(2)}) %all-to-all-start) | async-done | bytes 262176 | tf_op jit(solution)/shard_map/all_to_all | solution.py:156
  72.4 4.1 %collective-permute-start = (f32[1,2,9,128]{3,2,1,0:T(8,128)S(1)}, f32[1,2,9,128]{3,2,1,0:T(8,128)S(1)}, u32[]{:S(2)}, u32[]{:S(2)}) collective-permute-start(f32[1,2,9,128]{3,2,1,0:T(8,128)S(1)} %get-tuple-element.25), channel_id=1, source_target_pairs={{0,4},{4,8},{8,12},{1,5},{5,9},{9,13},{2,6},{6,10},{10,14},{3,7},{... | collective-permute-start | bytes 27656 | tf_op jit(solution)/shard_map/ppermute | solution.py:24
  76.5 1.3 collective-permute-start.1
  77.9 4.2 %collective-permute-done.1 = f32[1,2,9,128]{3,2,1,0:T(8,128)S(1)} collective-permute-done((f32[1,2,9,128]{3,2,1,0:T(8,128)S(1)}, f32[1,2,9,128]{3,2,1,0:T(8,128)S(1)}, u32[]{:S(2)}, u32[]{:S(2)}) %collective-permute-start.1) | collective-permute-done | bytes 9248 | tf_op jit(solution)/shard_map/ppermute | solution.py:26
  82.2 2.3 %collective-permute-start.2 = (f32[1,2,146,9]{3,2,1,0:T(8,128)S(1)}, f32[1,2,146,9]{3,2,1,0:T(8,128)S(1)}, u32[]{:S(2)}, u32[]{:S(2)}) collective-permute-start(f32[1,2,146,9]{3,2,1,0:T(8,128)S(1)} %get-tuple-element.27), channel_id=1, source_target_pairs={{0,2},{1,3},{4,6},{5,7},{8,10},{9,11},{12,14},{13,15},{16,18},{17,... | collective-permute-start | bytes 31544 | tf_op jit(solution)/shard_map/ppermute | solution.py:24
  84.5 1.3 collective-permute-start.3
  87.2 4.4 %collective-permute-done.3 = f32[1,2,146,9]{3,2,1,0:T(8,128)S(1)} collective-permute-done((f32[1,2,146,9]{3,2,1,0:T(8,128)S(1)}, f32[1,2,146,9]{3,2,1,0:T(8,128)S(1)}, u32[]{:S(2)}, u32[]{:S(2)}) %collective-permute-start.3) | collective-permute-done | bytes 10544 | tf_op jit(solution)/shard_map/ppermute | solution.py:26
  92.1 0.9 convolution_bitcast_fusion.3
  93.0 0.9 convolution_divide_fusion
  93.9 0.9 convolution_bitcast_fusion.2
  94.8 1.0 convolution_bitcast_fusion.1
  95.9 1.4 %collective-permute-start.4 = (f32[1,144,8]{1,2,0:T(8,128)S(1)}, f32[1,144,8]{1,2,0:T(8,128)S(1)}, u32[]{:S(2)}, u32[]{:S(2)}) collective-permute-start(f32[1,144,8]{1,2,0:T(8,128)S(1)} %slice.156), channel_id=1, source_target_pairs={{0,2},{1,3},{4,6},{5,7},{8,10},{9,11},{12,14},{13,15},{16,18},{17,... | collective-permute-start | bytes 13832 | tf_op jit(solution)/shard_map/ppermute | solution.py:24
  98.0 1.4 %dynamic-update-slice.3 = f32[8]{0:T(128)S(1)} dynamic-update-slice(f32[8]{0:T(128)S(1)} %broadcast.336, f32[1]{0:T(128)} %bitcast.20, u32[]{:T(128)} %bitcast.21) | dynamic-update-slice | bytes 12
  99.4 1.3 collective-permute-start.5
  101.4 21.1 %all-reduce = f32[8]{0:T(128)S(1)} all-reduce(f32[8]{0:T(128)S(1)} %dynamic-update-slice.3), channel_id=1, replica_groups=mesh['groups'=2,'row'=4,'col'=2,'sub'=2] {'row','col'}, use_global_device_ids=true, to_apply=%add | all-reduce | flops 8 | bytes 64 | tf_op jit(solution)/shard_map/reshape.25
  122.6 1.3 collective-permute-start.6
  124.1 1.8 %collective-permute-done.6 = f32[1,8,128]{1,2,0:T(8,128)S(1)} collective-permute-done((f32[1,8,128]{1,2,0:T(8,128)S(1)}, f32[1,8,128]{1,2,0:T(8,128)S(1)}, u32[]{:S(2)}, u32[]{:S(2)}) %collective-permute-start.6) | collective-permute-done | bytes 4128 | tf_op jit(solution)/shard_map/ppermute | solution.py:24
  125.9 1.3 collective-permute-start.7
  128.0 4.4 %collective-permute-done.7 = f32[1,8,128]{1,2,0:T(8,128)S(1)} collective-permute-done((f32[1,8,128]{1,2,0:T(8,128)S(1)}, f32[1,8,128]{1,2,0:T(8,128)S(1)}, u32[]{:S(2)}, u32[]{:S(2)}) %collective-permute-start.7) | collective-permute-done | bytes 4128 | tf_op jit(solution)/shard_map/ppermute | solution.py:26
  132.4 0.7 maximum_add_fusion
  (55 shorter events, 9.2 us)
Async XLA Ops:
  0.7 85.8 %copy-start = (u32[32]{0:T(128)S(1)}, u32[32]{0:T(128)}, u32[]{:S(2)}) copy-start(u32[32]{0:T(128)} %constant.146) | copy-start | bytes 388
  62.1 10.2 %all-to-all-start = ((f32[4,4,32,128]{3,2,1,0:T(8,128)}), f32[4,4,32,128]{3,2,1,0:T(8,128)S(1)}, u32[]{:S(2)}, u32[]{:S(2)}) async-start(f32[4,4,32,128]{3,2,1,0:T(8,128)} %bitcast.4), calls=%async_computation | async-start | bytes 524288 | tf_op jit(solution)/shard_map/all_to_all | solution.py:156
  72.4 5.5 %collective-permute-start = (f32[1,2,9,128]{3,2,1,0:T(8,128)S(1)}, f32[1,2,9,128]{3,2,1,0:T(8,128)S(1)}, u32[]{:S(2)}, u32[]{:S(2)}) collective-permute-start(f32[1,2,9,128]{3,2,1,0:T(8,128)S(1)} %get-tuple-element.25), channel_id=1, source_target_pairs={{0,4},{4,8},{8,12},{1,5},{5,9},{9,13},{2,6},{6,10},{10,14},{3,7},{... | collective-permute-start | bytes 27656 | tf_op jit(solution)/shard_map/ppermute | solution.py:24
  76.5 5.6 %collective-permute-start.1 = (f32[1,2,9,128]{3,2,1,0:T(8,128)S(1)}, f32[1,2,9,128]{3,2,1,0:T(8,128)S(1)}, u32[]{:S(2)}, u32[]{:S(2)}) collective-permute-start(f32[1,2,9,128]{3,2,1,0:T(8,128)S(1)} %get-tuple-element.26), channel_id=1, source_target_pairs={{4,0},{8,4},{12,8},{5,1},{9,5},{13,9},{6,2},{10,6},{14,10},{7,3},{... | collective-permute-start | bytes 27656 | tf_op jit(solution)/shard_map/ppermute | solution.py:26
  82.2 5.0 %collective-permute-start.2 = (f32[1,2,146,9]{3,2,1,0:T(8,128)S(1)}, f32[1,2,146,9]{3,2,1,0:T(8,128)S(1)}, u32[]{:S(2)}, u32[]{:S(2)}) collective-permute-start(f32[1,2,146,9]{3,2,1,0:T(8,128)S(1)} %get-tuple-element.27), channel_id=1, source_target_pairs={{0,2},{1,3},{4,6},{5,7},{8,10},{9,11},{12,14},{13,15},{16,18},{17,... | collective-permute-start | bytes 31544 | tf_op jit(solution)/shard_map/ppermute | solution.py:24
  84.5 7.1 %collective-permute-start.3 = (f32[1,2,146,9]{3,2,1,0:T(8,128)S(1)}, f32[1,2,146,9]{3,2,1,0:T(8,128)S(1)}, u32[]{:S(2)}, u32[]{:S(2)}) collective-permute-start(f32[1,2,146,9]{3,2,1,0:T(8,128)S(1)} %get-tuple-element.28), channel_id=1, source_target_pairs={{2,0},{3,1},{6,4},{7,5},{10,8},{11,9},{14,12},{15,13},{18,16},{19,... | collective-permute-start | bytes 31544 | tf_op jit(solution)/shard_map/ppermute | solution.py:26
  95.9 3.5 %collective-permute-start.4 = (f32[1,144,8]{1,2,0:T(8,128)S(1)}, f32[1,144,8]{1,2,0:T(8,128)S(1)}, u32[]{:S(2)}, u32[]{:S(2)}) collective-permute-start(f32[1,144,8]{1,2,0:T(8,128)S(1)} %slice.156), channel_id=1, source_target_pairs={{0,2},{1,3},{4,6},{5,7},{8,10},{9,11},{12,14},{13,15},{16,18},{17,... | collective-permute-start | bytes 13832 | tf_op jit(solution)/shard_map/ppermute | solution.py:24
  99.4 23.1 %collective-permute-start.5 = (f32[1,144,8]{1,2,0:T(8,128)S(1)}, f32[1,144,8]{1,2,0:T(8,128)S(1)}, u32[]{:S(2)}, u32[]{:S(2)}) collective-permute-start(f32[1,144,8]{1,2,0:T(8,128)S(1)} %get-tuple-element.30), channel_id=1, source_target_pairs={{2,0},{3,1},{6,4},{7,5},{10,8},{11,9},{14,12},{15,13},{18,16},{19,... | collective-permute-start | bytes 13832 | tf_op jit(solution)/shard_map/ppermute | solution.py:26
  122.6 3.2 %collective-permute-start.6 = (f32[1,8,128]{1,2,0:T(8,128)S(1)}, f32[1,8,128]{1,2,0:T(8,128)S(1)}, u32[]{:S(2)}, u32[]{:S(2)}) collective-permute-start(f32[1,8,128]{1,2,0:T(8,128)S(1)} %slice.161), channel_id=1, source_target_pairs={{0,4},{4,8},{8,12},{1,5},{5,9},{9,13},{2,6},{6,10},{10,14},{3,7},{... | collective-permute-start | bytes 12296 | tf_op jit(solution)/shard_map/ppermute | solution.py:24
  125.9 6.5 %collective-permute-start.7 = (f32[1,8,128]{1,2,0:T(8,128)S(1)}, f32[1,8,128]{1,2,0:T(8,128)S(1)}, u32[]{:S(2)}, u32[]{:S(2)}) collective-permute-start(f32[1,8,128]{1,2,0:T(8,128)S(1)} %get-tuple-element.32), channel_id=1, source_target_pairs={{4,0},{8,4},{12,8},{5,1},{9,5},{13,9},{6,2},{10,6},{14,10},{7,3},{... | collective-permute-start | bytes 12296 | tf_op jit(solution)/shard_map/ppermute | solution.py:26
where the time goes:
time: 134 us
  local copies, waits for them, and re-layouts  47.2 us (35%)
  blocking collectives  21.1 us (16%)
  waiting for transfers between devices  18.7 us (14%)
  matrix products  18.6 us (14%)
  starting transfers between devices  18.5 us (14%)
  other arithmetic  8.81 us (7%)
    reshape x1, local copies, waits for them, and re-layouts, body(): blocks = pixels.reshape(frame_count, stripe, PIX, grid_cols, PIX)  42.1 us
    another operation x1, blocking collectives  21.1 us
    dot_general x1, matrix products, body(): jnp.einsum('fiajb,bk->fkiaj', blocks, table.astype(jnp.bfloat16), preferr...  14.6 us
    ppermute x4, waiting for transfers between devices, with_halo(): lax.ppermute(head, axis, [((i + 1) % count, i) for i in range(ends)])  13 us
    ppermute x4, starting transfers between devices, with_halo(): lax.ppermute(tail, axis, [(i, (i + 1) % count) for i in range(ends)])  9.11 us
    ppermute x4, starting transfers between devices, with_halo(): lax.ppermute(head, axis, [((i + 1) % count, i) for i in range(ends)])  5.16 us
    all_to_all x1, starting transfers between devices, body(): lax.all_to_all(to_pieces(split_columns(stacked, block_cols), core_count),...  4.21 us
    all_to_all x1, waiting for transfers between devices, body(): lax.all_to_all(to_pieces(split_columns(stacked, block_cols), core_count),...  3.7 us
  transfers between devices with their start and end apart: 9, of which 7 were waited for; matrix products, arithmetic and copies ran while one was open for 5% of the time, Pallas kernels for 0%

commit v1 on v0

v1 whole, which is shorter than its diff:
```python
import functools
import math

import jax
import jax.numpy as jnp
import numpy as np
from jax import lax
from jax.experimental import pallas as pl
from jax.experimental.pallas import tpu as pltpu
from jax.sharding import PartitionSpec as P

PIX = 8
SUBN = 128
MARGIN = 8
WIN = SUBN + 2 * MARGIN
CHUNK = 256
LANES = 128
GROUP = CHUNK // PIX
DAMPING = 2e-05
F32 = jnp.float32
BF16 = jnp.bfloat16


def split_const(values):
    high = np.asarray(values).astype(jnp.bfloat16)
    return high, (values - high.astype(np.float64)).astype(jnp.bfloat16)


def sine_basis():
    order = np.arange(1, WIN + 1, dtype=np.float64)
    vectors = np.sqrt(2.0 / (WIN + 1)) * np.sin(math.pi * order[:, None] * order[None, :] / (WIN + 1))
    spectrum = 2.0 - 2.0 * np.cos(math.pi * order / (WIN + 1))
    return vectors, 1.0 / (spectrum[:, None] + spectrum[None, :] + DAMPING)


def column_basis(blocks):
    vectors, _ = sine_basis()
    table = np.zeros((blocks * SUBN, blocks * WIN))
    for block in range(blocks):
        low = max(block * SUBN - MARGIN, 0)
        high = min((block + 1) * SUBN + MARGIN, blocks * SUBN)
        start = low - (block * SUBN - MARGIN)
        table[low:high, block * WIN : (block + 1) * WIN] = vectors[start : start + high - low]
    return table


def coarse_inverse(blocks_down, blocks_across):
    number = blocks_down * blocks_across
    row, col = np.divmod(np.arange(number), blocks_across)
    apart = np.abs(row[:, None] - row[None, :]) + np.abs(col[:, None] - col[None, :])
    touching = (apart == 1).astype(np.float64)
    laplace = np.diag(touching.sum(1)) - touching
    return np.linalg.inv(SUBN * laplace + DAMPING * SUBN * SUBN * np.eye(number))


def row_moments(stripe):
    offset = np.arange(PIX) - (PIX - 1) / 2.0
    table = np.zeros((3, stripe, stripe * PIX))
    for row in range(stripe):
        for kind in range(3):
            table[kind, row, row * PIX : (row + 1) * PIX] = offset**kind
    return table.reshape(3 * stripe, stripe * PIX).astype(jnp.bfloat16)


def column_moments():
    offset = np.arange(PIX) - (PIX - 1) / 2.0
    places = LANES // GROUP
    table = np.zeros((places, CHUNK, LANES))
    for chunk in range(places):
        for kind in range(3):
            lane = GROUP * ((kind + chunk) % places)
            for cell in range(GROUP):
                table[chunk, cell * PIX : (cell + 1) * PIX, lane + cell] = offset**kind
    return table.astype(jnp.bfloat16)


def halves(values):
    high = values.astype(BF16)
    return high, (values - high.astype(F32)).astype(BF16)


def dot(left, right):
    return jnp.dot(left, right, preferred_element_type=F32)


def dot_three(left, right):
    return dot(left[0], right[0]) + (dot(left[0], right[1]) + dot(left[1], right[0]))


def iota(shape, axis):
    return lax.broadcasted_iota(jnp.int32, shape, axis)


def moments_kernel(sizes, pixels, row_table, col_table, field, extras, held, arrived):
    frames, stripe, blocks, cores, stripes = sizes
    width = blocks * SUBN
    places = LANES // GROUP
    span = LANES * PIX

    def copy(frame, part):
        where = (frame, slice(None), pl.ds(part * span, span))
        return pltpu.make_async_copy(pixels.at[where], held.at[where], arrived.at[frame, part])

    for frame in range(frames):
        for part in range(blocks):
            copy(frame, part).start()
    position = (lax.axis_index("row") * blocks + lax.axis_index("col")) * cores + lax.axis_index("sub")
    group = iota((stripe, LANES), 1) // GROUP

    def gather(pieces, kind):
        total = pieces[-1]
        for chunk in range(places - 1):
            total = jnp.where(group == (kind + chunk) % places, pieces[chunk], total)
        return pltpu.roll(total, LANES - GROUP * kind, 1) if kind else total

    row = iota((stripe, width), 0)
    column = iota((stripe, width), 1)
    for frame in range(frames):
        intensity, moment_x, moment_y, moment_two = [], [], [], []
        for part in range(blocks):
            copy(frame, part).wait()
            lines = dot(row_table[...], held[frame, :, pl.ds(part * span, span)])
            high, low = halves(lines)
            pieces = []
            for chunk in range(places):
                cut = slice(chunk * CHUNK, (chunk + 1) * CHUNK)
                weights = col_table[chunk]
                pieces.append(dot(high[:, cut], weights) + dot(low[:, cut], weights))
            plain = [piece[:stripe] for piece in pieces]
            tilted = [piece[stripe : 2 * stripe] for piece in pieces]
            bent = [piece[2 * stripe :] for piece in pieces]
            intensity.append(gather(plain, 0))
            moment_x.append(gather(plain, 1))
            moment_y.append(gather(tilted, 0))
            moment_two.append(gather(plain, 2) + gather(bent, 0))
        intensity = jnp.concatenate(intensity, 1)
        inverse = 1.0 / intensity
        slope_x = jnp.concatenate(moment_x, 1) * inverse
        slope_y = jnp.concatenate(moment_y, 1) * inverse
        spot_size = jnp.concatenate(moment_two, 1) * inverse - slope_x * slope_x - slope_y * slope_y
        mean_flux = intensity * (1.0 / (PIX * PIX))
        flow_x = jnp.where(column < width - 1, slope_x, 0.0)
        flow_y = jnp.where(position * stripe + row < stripes * stripe - 1, slope_y, 0.0)
        left = jnp.where(column > 0, pltpu.roll(flow_x, 1, 1), 0.0)
        above = pltpu.roll(flow_y, 1, 0)
        source = left - flow_x + jnp.where(row > 0, above, 0.0) - flow_y
        spill = jnp.where(row[:8] == 0, above[:8], 0.0)
        for block in range(blocks):
            target = block * cores + frame
            own = slice(block * SUBN, (block + 1) * SUBN)
            field[target, :stripe, :] = source
            field[target, stripe:, :] = spill
            extras[target, :stripe, :] = mean_flux[:, own]
            extras[target, stripe:, :] = spot_size[:, own]


def rims_kernel(
    sizes, field, basis_high, basis_low, back_high, back_low, drive_high, drive_low, edge_high, edge_low, scale,
    sent, spread, near,
):
    stripe, pieces, blocks, rows = sizes
    width = blocks * SUBN
    mine = lax.axis_index("row")
    side = lax.axis_index("col")
    parts = []
    for piece in range(pieces):
        block = field[piece, :stripe, :]
        if piece:
            head = block[:8] + field[piece - 1, stripe:, :]
            block = head if stripe == 8 else jnp.concatenate([head, block[8:]], 0)
        parts.append(block)
    spill = field[pieces - 1, stripe:, :]
    parts.append(spill)
    source = jnp.concatenate(parts, 0)
    across = dot_three(halves(source), (basis_high[...], basis_low[...]))
    driven = dot_three((drive_high[...], drive_low[...]), halves(across))
    factor = scale[...]
    responses = [driven[k * WIN : (k + 1) * WIN] * factor for k in range(3)]
    response = jnp.concatenate(responses, 0)
    back = (back_high[side], back_low[side])
    reach = dot_three(halves(response), back)
    spread[...] = reach[:WIN]
    edge = (edge_high[...], edge_low[...])
    high, low = halves(reach)
    rims = [
        dot_three(edge, (high[k * WIN : (k + 1) * WIN], low[k * WIN : (k + 1) * WIN])) for k in range(3)
    ]
    near[:8, :] = jnp.where(mine > 0, rims[1][8:], 0.0)
    near[8:, :] = jnp.where(mine < rows - 1, rims[2][:8], 0.0)
    base = 8 * blocks
    tail = sent.shape[1] - base - 8
    total = jnp.sum(source[:SUBN], 0, keepdims=True)
    place = iota((tail, LANES), 0)
    sums = jnp.zeros((tail, LANES), F32)
    for block in range(blocks):
        cut = slice(block * SUBN, (block + 1) * SUBN)
        sums = jnp.where(place == block, total[:, cut], sums)
        sums = jnp.where(place == blocks + block, spill[:1, cut], sums)
    for target in range(rows):
        sent[target, : base + 8, :] = jnp.zeros((base + 8, LANES), F32)
        sent[target, base + 8 :, :] = sums

    def put(target, rim, raw):
        sent[target, base : base + 8, :] = rim
        if raw is not None:
            for block in range(blocks):
                sent[target, 8 * block : 8 * block + 8, :] = raw[:, block * SUBN : (block + 1) * SUBN]

    @pl.when(mine >= 1)
    def _():
        put(mine - 1, rims[0][:8], source[:8])

    @pl.when(mine >= 2)
    def _():
        put(mine - 2, rims[1][:8], None)

    @pl.when(mine + 1 < rows)
    def _():
        put(mine + 1, rims[0][8:], source[SUBN - 8 : SUBN])

    @pl.when(mine + 2 < rows)
    def _():
        put(mine + 2, rims[2][8:], None)


def phase_kernel(
    sizes, received, spread, near, basis_high, basis_low, back_high, back_low, halo_high, halo_low,
    out_high, out_low, scale, coarse, phase,
):
    blocks, rows = sizes
    mine = lax.axis_index("row")
    side = lax.axis_index("col")
    base = 8 * blocks
    tail = received.shape[1] - base - 8
    above = jnp.maximum(mine - 1, 0)
    below = jnp.minimum(mine + 1, rows - 1)
    has_above = mine > 0
    has_below = mine < rows - 1
    first = iota((8, LANES), 0) == 0
    top, bottom, spilt = [], [], []
    for block in range(blocks):
        top.append(jnp.where(has_above, received[above, 8 * block : 8 * block + 8, :], 0.0))
        bottom.append(jnp.where(has_below, received[below, 8 * block : 8 * block + 8, :], 0.0))
        line = received[above, pl.ds(base + 8 + blocks + block, 1), :]
        spilt.append(jnp.where(jnp.logical_and(first, has_above), line, 0.0))
    halo = jnp.concatenate(
        [jnp.concatenate(top, 1), jnp.concatenate(spilt, 1), jnp.concatenate(bottom, 1)], 0
    )
    across = dot_three(halves(halo), (basis_high[...], basis_low[...]))
    driven = dot_three((halo_high[...], halo_low[...]), halves(across))
    reach = dot_three(halves(driven * scale[...]), (back_high[side], back_low[side]))
    solved = dot_three((out_high[...], out_low[...]), halves(spread[...] + reach))
    weighted = jnp.zeros((tail, LANES), F32)
    for origin in range(rows):
        count = jnp.sum(received[origin, base + 8 :, :], 1, keepdims=True)
        weighted = weighted + count * coarse[origin]
    own = iota((tail, LANES), 1) == mine * blocks + side
    level = jnp.sum(jnp.where(own, weighted, 0.0), keepdims=True)
    solved = solved + level
    head = near[:8, :] + jnp.where(has_above, received[above, base : base + 8, :], 0.0)
    head = head + jnp.where(mine > 1, received[jnp.maximum(mine - 2, 0), base : base + 8, :], 0.0)
    foot = near[8:, :] + jnp.where(has_below, received[below, base : base + 8, :], 0.0)
    foot = foot + jnp.where(
        mine < rows - 2, received[jnp.minimum(mine + 2, rows - 1), base : base + 8, :], 0.0
    )
    phase[0, :8, :] = solved[:8] + head
    phase[0, 8 : SUBN - 8, :] = solved[8 : SUBN - 8]
    phase[0, SUBN - 8 :, :] = solved[SUBN - 8 :] + foot


def coarse_table(blocks_down, blocks_across, tail):
    inverse = coarse_inverse(blocks_down, blocks_across)
    number = blocks_down * blocks_across
    lanes = -(-number // LANES) * LANES
    table = np.zeros((blocks_down, tail, lanes), np.float32)
    for row in range(blocks_down):
        for block in range(blocks_across):
            table[row, block, :number] = inverse[row * blocks_across + block]
            if row + 1 < blocks_down:
                table[row, blocks_across + block, :number] = inverse[(row + 1) * blocks_across + block]
    return table


def in_vmem(count):
    return [pl.BlockSpec(memory_space=pltpu.VMEM)] * count


PARAMS = pltpu.CompilerParams(vmem_limit_bytes=48 * 1024 * 1024)


def body(pixels):
    frames, pixel_rows, pixel_cols = pixels.shape
    stripe = pixel_rows // PIX
    width = pixel_cols // PIX
    rows = lax.axis_size("row")
    blocks = lax.axis_size("col")
    cores = lax.axis_size("sub")
    pieces = blocks * cores
    assert frames == cores and width == blocks * SUBN and stripe * pieces == SUBN

    field, extras = pl.pallas_call(
        functools.partial(moments_kernel, (frames, stripe, blocks, cores, rows * pieces)),
        out_shape=(
            jax.ShapeDtypeStruct((pieces, stripe + 8, width), F32),
            jax.ShapeDtypeStruct((pieces, 2 * stripe, SUBN), F32),
        ),
        in_specs=[pl.BlockSpec(memory_space=pl.ANY)] + in_vmem(2),
        out_specs=tuple(in_vmem(2)),
        scratch_shapes=[
            pltpu.VMEM((frames, pixel_rows, pixel_cols), BF16),
            pltpu.SemaphoreType.DMA((frames, blocks)),
        ],
        compiler_params=PARAMS,
        name="moments",
    )(pixels, jnp.asarray(row_moments(stripe)), jnp.asarray(column_moments()))

    field = lax.all_to_all(field, ("col", "sub"), split_axis=0, concat_axis=0, tiled=True)
    extras = lax.all_to_all(extras, ("col", "sub"), split_axis=0, concat_axis=0, tiled=True)

    vectors, scale = sine_basis()
    basis = column_basis(blocks)
    basis_pair = [jnp.asarray(part) for part in split_const(basis)]
    back = basis.T.reshape(blocks * WIN, blocks, SUBN).transpose(1, 0, 2)
    back_pair = [jnp.asarray(part) for part in split_const(back)]
    scale_wide = jnp.asarray(np.tile(scale, (1, blocks)).astype(np.float32))
    reached = SUBN + 8
    drive = np.zeros((3, WIN, reached))
    drive[0] = vectors[:, MARGIN:]
    drive[1, :, :8] = vectors[:, WIN - 8 :]
    drive[2, :, SUBN - 8 : SUBN + 1] = vectors[:, :9]
    drive_pair = [jnp.asarray(part) for part in split_const(drive.reshape(3 * WIN, reached))]
    edge = np.concatenate([vectors[:8], vectors[WIN - 8 :]], 0)
    edge_pair = [jnp.asarray(part) for part in split_const(edge)]
    tail = -(-2 * blocks // 8) * 8
    height = 8 * blocks + 8 + tail

    sent, spread, near = pl.pallas_call(
        functools.partial(rims_kernel, (stripe, pieces, blocks, rows)),
        out_shape=(
            jax.ShapeDtypeStruct((rows, height, LANES), F32),
            jax.ShapeDtypeStruct((WIN, SUBN), F32),
            jax.ShapeDtypeStruct((16, SUBN), F32),
        ),
        in_specs=in_vmem(10),
        out_specs=tuple(in_vmem(3)),
        compiler_params=PARAMS,
        name="rims",
    )(field, *basis_pair, *back_pair, *drive_pair, *edge_pair, scale_wide)

    received = lax.all_to_all(sent, "row", split_axis=0, concat_axis=0, tiled=True)

    halo = np.zeros((WIN, 24))
    halo[:, :9] = vectors[:, :9]
    halo[:, 16:] = vectors[:, WIN - 8 :]
    halo_pair = [jnp.asarray(part) for part in split_const(halo)]
    out_pair = [jnp.asarray(part) for part in split_const(vectors[MARGIN : MARGIN + SUBN])]
    phase = pl.pallas_call(
        functools.partial(phase_kernel, (blocks, rows)),
        out_shape=jax.ShapeDtypeStruct((1, SUBN, SUBN), F32),
        in_specs=in_vmem(13),
        out_specs=pl.BlockSpec(memory_space=pltpu.VMEM),
        compiler_params=PARAMS,
        name="phase",
    )(
        received, spread, near, *basis_pair, *back_pair, *halo_pair, *out_pair, scale_wide,
        jnp.asarray(coarse_table(rows, blocks, tail)),
    )
    mean_flux = extras[:, :stripe].reshape(1, SUBN, SUBN)
    spot_size = extras[:, stripe:].reshape(1, SUBN, SUBN)
    return phase, mean_flux, spot_size


def solution(mesh):
    placed = P(("groups", "sub"), "row", "col")
    return jax.shard_map(
        body,
        mesh=mesh,
        in_specs=(P("groups", ("row", "col", "sub"), None),),
        out_specs=(placed, placed, placed),
        check_vma=False,
    )
```

time: 134 us -> 36.7 us (0.27)
  local copies, waits for them, and re-layouts: 47.2 us -> 4.08 us
  matrix products: 18.6 us -> 0 us
  blocking collectives: 21.1 us -> 9 us
  waiting for transfers between devices: 18.7 us -> 7.11 us
  starting transfers between devices: 18.5 us -> 8.19 us
  other arithmetic: 8.81 us -> 0 us
  Pallas kernels: 0 us -> 6.98 us
    reshape x1 -> x0, local copies, waits for them, and re-layouts: 42.1 us -> none  [body(): blocks = pixels.reshape(frame_count, stripe, PIX, grid_cols, PIX)]
    another operation x1 -> x0, blocking collectives: 21.1 us -> none
    dot_general x5 -> x0, matrix products: 18.3 us -> none  [the longest x1 14.6 us: body(): jnp.einsum('fiajb,bk->fkiaj', blocks, table.astype(jnp.bfloat16), preferr...]
    ppermute x8 -> x0, waiting for transfers between devices: 15 us -> none  [the longest x4 13 us: with_halo(): lax.ppermute(head, axis, [((i + 1) % count, i) for i in range(ends)])]
    ppermute x8 -> x0, starting transfers between devices: 14.3 us -> none  [the longest x4 9.11 us: with_halo(): lax.ppermute(tail, axis, [(i, (i + 1) % count) for i in range(ends)])]
    all_to_all x0 -> x1, blocking collectives: none -> 9 us  [body(): lax.all_to_all(field, ('col', 'sub'), split_axis=0, concat_axis=0, tiled=...]
    pallas_call x0 -> x3, Pallas kernels: none -> 6.98 us  [the longest x1 2.85 us: body(): pl.pallas_call(functools.partial(moments_kernel, (frames, stripe, blocks,...]
    reduce_sum x4 -> x0, other arithmetic: 4.44 us -> none  [the longest x1 3.18 us: body(): moment_x = jnp.sum(partial_value[:, 1], 2)]
  transfers between devices with their start and end apart: 9 -> 2, of which waited for: 7 -> 2; matrix products, arithmetic and copies ran while one was open for 5% -> 2% of each run, Pallas kernels for 0% -> 7%
where the time goes in v1:
time: 36.7 us; the launch traced here: 36.2 us
  blocking collectives  9 us (25%)
  starting transfers between devices  8.19 us (22%)
  waiting for transfers between devices  7.11 us (19%)
  Pallas kernels  6.98 us (19%)
  local copies, waits for them, and re-layouts  4.08 us (11%)
  between operations  0.83 us (2%)
    all_to_all x1, blocking collectives, body(): lax.all_to_all(field, ('col', 'sub'), split_axis=0, concat_axis=0, tiled=...  9 us
    all_to_all x1, waiting for transfers between devices, body(): lax.all_to_all(sent, 'row', split_axis=0, concat_axis=0, tiled=True)  5.09 us
    all_to_all x1, starting transfers between devices, body(): lax.all_to_all(sent, 'row', split_axis=0, concat_axis=0, tiled=True)  4.87 us
    unnamed x34, local copies, waits for them, and re-layouts  3.42 us
    all_to_all x1, starting transfers between devices, body(): lax.all_to_all(extras, ('col', 'sub'), split_axis=0, concat_axis=0, tiled...  3.32 us
    pallas_call x1, Pallas kernels, body(): pl.pallas_call(functools.partial(moments_kernel, (frames, stripe, blocks,...  2.85 us
    pallas_call x1, Pallas kernels, body(): pl.pallas_call(functools.partial(rims_kernel, (stripe, pieces, blocks, ro...  2.48 us
    all_to_all x1, waiting for transfers between devices, body(): lax.all_to_all(extras, ('col', 'sub'), split_axis=0, concat_axis=0, tiled...  2.03 us
  transfers between devices with their start and end apart: 2, of which 2 were waited for; matrix products, arithmetic and copies ran while one was open for 2% of the time, Pallas kernels for 7%

profile of v1, /device:TPU:0, one launch (start us, length us, event | category | flops | bytes accessed | tf_op | source)
XLA Modules:
  0.0 36.2 jit_solution(12388237393303533639)
XLA Ops:
  0.6 0.0 copy-start.15
  0.6 0.0 copy-start
  0.7 1.6 %copy-done = bf16[2,256,2048]{2,1,0:T(8,128)(2,1)S(1)} copy-done((bf16[2,256,2048]{2,1,0:T(8,128)(2,1)S(1)}, bf16[2,256,2048]{2,1,0:T(8,128)(2,1)}, u32[]{:S(2)}) %copy-start) | copy-done | bytes 2097176
  2.2 0.9 %copy-done.6 = bf16[4,256,128]{2,1,0:T(8,128)(2,1)S(1)} copy-done((bf16[4,256,128]{2,1,0:T(8,128)(2,1)S(1)}, bf16[4,256,128]{2,1,0:T(8,128)(2,1)}, u32[]{:S(2)}) %copy-start.6) | copy-done | bytes 262168
  3.2 0.8 %copy-done.11 = bf16[96,256]{1,0:T(8,128)(2,1)S(1)} copy-done((bf16[96,256]{1,0:T(8,128)(2,1)S(1)}, bf16[96,256]{1,0:T(8,128)(2,1)}, u32[]{:S(2)}) %copy-start.11) | copy-done | bytes 49176
  4.0 0.0 copy-start.5
  4.0 0.0 copy-start.7
  4.0 0.0 copy-start.8
  4.0 0.0 copy-start.16
  4.1 0.0 copy-start.9
  4.1 0.0 copy-start.10
  4.1 0.0 copy-start.12
  4.1 0.0 copy-start.13
  4.1 0.0 copy-start.14
  4.1 2.8 %moments.1 = (f32[4,40,256]{2,1,0:T(8,128)S(1)}, f32[4,64,128]{2,1,0:T(8,128)}) custom-call(bf16[2,256,2048]{2,1,0:T(8,128)(2,1)S(1)} %copy-done, bf16[96,256]{1,0:T(8,128)(2,1)S(1)} %copy-done.11, bf16[4,256,128]{2,1,0:T(8,128)(2,1)S(1)} %copy-done.6), custom_call_target="tpu_custom_call" | custom-call | tf_op jit(solution)/shard_map/moments/pallas_call | solution.py:301
  7.0 9.0 %all_to_all.15.field = f32[4,40,256]{2,1,0:T(8,128)S(1)} all-to-all(f32[4,40,256]{2,1,0:T(8,128)S(1)} %get-tuple-element.8), channel_id=1, replica_groups=mesh['groups'=2,'row'=4,'col'=2,'sub'=2] {'col','sub'}, dimensions={0} | all-to-all | bytes 327680 | tf_op jit(solution)/shard_map/all_to_all | solution.py:317
  16.0 3.3 %all-to-all-start.2 = ((f32[4,64,128]{2,1,0:T(8,128)}), f32[4,64,128]{2,1,0:T(8,128)S(1)}, u32[]{:S(2)}, u32[]{:S(2)}) async-start(f32[4,64,128]{2,1,0:T(8,128)} %get-tuple-element.12), calls=%async_computation.2 | async-start | bytes 262144 | tf_op jit(solution)/shard_map/all_to_all | solution.py:318
  19.4 2.5 %rims.1 = (f32[4,32,128]{2,1,0:T(8,128)}, f32[144,128]{1,0:T(8,128)S(1)}, f32[16,128]{1,0:T(8,128)S(1)}) custom-call(f32[4,40,256]{2,1,0:T(8,128)S(1)} %all_to_all.15.field, bf16[256,288]{1,0:T(8,128)(2,1)S(1)} %copy-done.3, bf16[256,288]{1,0:T(8,128)(2,1)S(1)} %copy-done.2, bf16[2,288,128]{2,1,0:T(8,128)(2,1)S(1)} %copy-done.5, ...), custom_call_target="tpu_custom_call" | custom-call | tf_op jit(solution)/shard_map/rims/pallas_call | solution.py:337
  21.9 2.0 %all-to-all-done.2 = f32[4,64,128]{2,1,0:T(8,128)S(1)} async-done(((f32[4,64,128]{2,1,0:T(8,128)}), f32[4,64,128]{2,1,0:T(8,128)S(1)}, u32[]{:S(2)}, u32[]{:S(2)}) %all-to-all-start.2) | async-done | bytes 131104 | tf_op jit(solution)/shard_map/all_to_all | solution.py:318
  23.9 4.9 %all-to-all-start.1 = ((f32[4,32,128]{2,1,0:T(8,128)}), f32[4,32,128]{2,1,0:T(8,128)S(1)}, u32[]{:S(2)}, u32[]{:S(2)}) async-start(f32[4,32,128]{2,1,0:T(8,128)} %get-tuple-element.9), calls=%async_computation.1 | async-start | bytes 131072 | tf_op jit(solution)/shard_map/all_to_all | solution.py:350
  28.8 0.7 %fusion = (f32[4,32,128]{2,1,0:T(8,128)}, f32[4,32,128]{2,1,0:T(8,128)}) fusion(f32[4,64,128]{2,1,0:T(8,128)S(1)} %all-to-all-done.2), kind=kLoop, calls=%fused_computation | loop fusion | bytes 262144 | tf_op jit(solution)/shard_map/slice | solution.py:369
  29.4 5.1 %all-to-all-done.1.received = f32[4,32,128]{2,1,0:T(8,128)S(1)} async-done(((f32[4,32,128]{2,1,0:T(8,128)}), f32[4,32,128]{2,1,0:T(8,128)S(1)}, u32[]{:S(2)}, u32[]{:S(2)}) %all-to-all-start.1) | async-done | bytes 65568 | tf_op jit(solution)/shard_map/all_to_all | solution.py:350
  34.5 0.0 copy-done.9
  34.5 1.7 %phase.1 = f32[1,128,128]{2,1,0:T(8,128)} custom-call(f32[4,32,128]{2,1,0:T(8,128)S(1)} %all-to-all-done.1.received, f32[144,128]{1,0:T(8,128)S(1)} %get-tuple-element.10.spread, f32[16,128]{1,0:T(8,128)S(1)} %get-tuple-element.11.near, bf16[256,288]{1,0:T(8,128)(2,1)S(1)} %copy-done.3, bf16[256,288]{1,0:T(8,128)(2,1)S(1)} %copy-done.2, ...), custom_call_target="tpu_custom_call" | custom-call | tf_op jit(solution)/shard_map/phase/pallas_call | solution.py:357
  (19 shorter events, 0.0 us)
Async XLA Ops:
  0.6 18.7 %copy-start.15 = (bf16[16,144]{1,0:T(8,128)(2,1)S(1)}, bf16[16,144]{1,0:T(8,128)(2,1)}, u32[]{:S(2)}) copy-start(bf16[16,144]{1,0:T(8,128)(2,1)} %constant.42.clone.edge_low) | copy-start | bytes 13828
  0.6 1.6 %copy-start = (bf16[2,256,2048]{2,1,0:T(8,128)(2,1)S(1)}, bf16[2,256,2048]{2,1,0:T(8,128)(2,1)}, u32[]{:S(2)}) copy-start(bf16[2,256,2048]{2,1,0:T(8,128)(2,1)} %pixels.1) | copy-start | bytes 6291460
  2.2 0.9 %copy-start.6 = (bf16[4,256,128]{2,1,0:T(8,128)(2,1)S(1)}, bf16[4,256,128]{2,1,0:T(8,128)(2,1)}, u32[]{:S(2)}) copy-start(bf16[4,256,128]{2,1,0:T(8,128)(2,1)} %constant.33.clone.col_table) | copy-start | bytes 786436
  3.2 0.8 %copy-start.11 = (bf16[96,256]{1,0:T(8,128)(2,1)S(1)}, bf16[96,256]{1,0:T(8,128)(2,1)}, u32[]{:S(2)}) copy-start(bf16[96,256]{1,0:T(8,128)(2,1)} %constant.32.clone.row_table) | copy-start | bytes 147460
  4.0 15.3 %copy-start.1 = (f32[144,288]{1,0:T(8,128)S(1)}, f32[144,288]{1,0:T(8,128)}, u32[]{:S(2)}) copy-start(f32[144,288]{1,0:T(8,128)} %constant.38.clone.scale) | copy-start | bytes 497668
  4.0 15.3 %copy-start.2 = (bf16[256,288]{1,0:T(8,128)(2,1)S(1)}, bf16[256,288]{1,0:T(8,128)(2,1)}, u32[]{:S(2)}) copy-start(bf16[256,288]{1,0:T(8,128)(2,1)} %constant.35.clone.basis_low) | copy-start | bytes 442372
  4.0 15.3 %copy-start.3 = (bf16[256,288]{1,0:T(8,128)(2,1)S(1)}, bf16[256,288]{1,0:T(8,128)(2,1)}, u32[]{:S(2)}) copy-start(bf16[256,288]{1,0:T(8,128)(2,1)} %constant.34.clone.basis_high) | copy-start | bytes 442372
  4.0 15.3 %copy-start.4 = (bf16[2,288,128]{2,1,0:T(8,128)(2,1)S(1)}, bf16[2,288,128]{2,1,0:T(8,128)(2,1)}, u32[]{:S(2)}) copy-start(bf16[2,288,128]{2,1,0:T(8,128)(2,1)} %constant.37.clone.back_low) | copy-start | bytes 442372
  4.0 15.3 %copy-start.5 = (bf16[2,288,128]{2,1,0:T(8,128)(2,1)S(1)}, bf16[2,288,128]{2,1,0:T(8,128)(2,1)}, u32[]{:S(2)}) copy-start(bf16[2,288,128]{2,1,0:T(8,128)(2,1)} %constant.36.clone.back_high) | copy-start | bytes 442372
  4.0 15.3 %copy-start.7 = (bf16[432,136]{1,0:T(8,128)(2,1)S(1)}, bf16[432,136]{1,0:T(8,128)(2,1)}, u32[]{:S(2)}) copy-start(bf16[432,136]{1,0:T(8,128)(2,1)} %constant.40.clone.drive_low) | copy-start | bytes 352516
  4.0 15.3 %copy-start.8 = (bf16[432,136]{1,0:T(8,128)(2,1)S(1)}, bf16[432,136]{1,0:T(8,128)(2,1)}, u32[]{:S(2)}) copy-start(bf16[432,136]{1,0:T(8,128)(2,1)} %constant.39.clone.drive_high) | copy-start | bytes 352516
  4.0 15.3 %copy-start.16 = (bf16[16,144]{1,0:T(8,128)(2,1)S(1)}, bf16[16,144]{1,0:T(8,128)(2,1)}, u32[]{:S(2)}) copy-start(bf16[16,144]{1,0:T(8,128)(2,1)} %constant.41.clone.edge_high) | copy-start | bytes 13828
  4.1 30.5 %copy-start.9 = (bf16[128,144]{1,0:T(8,128)(2,1)S(1)}, bf16[128,144]{1,0:T(8,128)(2,1)}, u32[]{:S(2)}) copy-start(bf16[128,144]{1,0:T(8,128)(2,1)} %constant.46.clone.out_low) | copy-start | bytes 110596
  4.1 30.5 %copy-start.10 = (bf16[128,144]{1,0:T(8,128)(2,1)S(1)}, bf16[128,144]{1,0:T(8,128)(2,1)}, u32[]{:S(2)}) copy-start(bf16[128,144]{1,0:T(8,128)(2,1)} %constant.45.clone.out_high) | copy-start | bytes 110596
  4.1 30.4 %copy-start.12 = (bf16[144,24]{1,0:T(8,128)(2,1)S(1)}, bf16[144,24]{1,0:T(8,128)(2,1)}, u32[]{:S(2)}) copy-start(bf16[144,24]{1,0:T(8,128)(2,1)} %constant.44.clone.halo_low) | copy-start | bytes 20740
  4.1 30.4 %copy-start.13 = (bf16[144,24]{1,0:T(8,128)(2,1)S(1)}, bf16[144,24]{1,0:T(8,128)(2,1)}, u32[]{:S(2)}) copy-start(bf16[144,24]{1,0:T(8,128)(2,1)} %constant.43.clone.halo_high) | copy-start | bytes 20740
  4.1 30.4 %copy-start.14 = (f32[4,8,128]{2,1,0:T(8,128)S(1)}, f32[4,8,128]{2,1,0:T(8,128)}, u32[]{:S(2)}) copy-start(f32[4,8,128]{2,1,0:T(8,128)} %constant.47.clone.coarse) | copy-start | bytes 49156
  16.0 7.9 %all-to-all-start.2 = ((f32[4,64,128]{2,1,0:T(8,128)}), f32[4,64,128]{2,1,0:T(8,128)S(1)}, u32[]{:S(2)}, u32[]{:S(2)}) async-start(f32[4,64,128]{2,1,0:T(8,128)} %get-tuple-element.12), calls=%async_computation.2 | async-start | bytes 262144 | tf_op jit(solution)/shard_map/all_to_all | solution.py:318
  23.9 10.6 %all-to-all-start.1 = ((f32[4,32,128]{2,1,0:T(8,128)}), f32[4,32,128]{2,1,0:T(8,128)S(1)}, u32[]{:S(2)}, u32[]{:S(2)}) async-start(f32[4,32,128]{2,1,0:T(8,128)} %get-tuple-element.9), calls=%async_computation.1 | async-start | bytes 131072 | tf_op jit(solution)/shard_map/all_to_all | solution.py:350

commit v2 on v1

--- a/solution.py
+++ b/solution.py
@@ -53,27 +53,6 @@
     return np.linalg.inv(SUBN * laplace + DAMPING * SUBN * SUBN * np.eye(number))
 
 
-def row_moments(stripe):
-    offset = np.arange(PIX) - (PIX - 1) / 2.0
-    table = np.zeros((3, stripe, stripe * PIX))
-    for row in range(stripe):
-        for kind in range(3):
-            table[kind, row, row * PIX : (row + 1) * PIX] = offset**kind
-    return table.reshape(3 * stripe, stripe * PIX).astype(jnp.bfloat16)
-
-
-def column_moments():
-    offset = np.arange(PIX) - (PIX - 1) / 2.0
-    places = LANES // GROUP
-    table = np.zeros((places, CHUNK, LANES))
-    for chunk in range(places):
-        for kind in range(3):
-            lane = GROUP * ((kind + chunk) % places)
-            for cell in range(GROUP):
-                table[chunk, cell * PIX : (cell + 1) * PIX, lane + cell] = offset**kind
-    return table.astype(jnp.bfloat16)
-
-
 def halves(values):
     high = values.astype(BF16)
     return high, (values - high.astype(F32)).astype(BF16)
@@ -91,7 +70,31 @@
     return lax.broadcasted_iota(jnp.int32, shape, axis)
 
 
-def moments_kernel(sizes, pixels, row_table, col_table, field, extras, held, arrived):
+def power(offset, kind):
+    return jnp.where(kind == 0, 1.0, jnp.where(kind == 1, offset, offset * offset))
+
+
+def offset_of(place):
+    return (place % PIX).astype(F32) - (PIX - 1) / 2.0
+
+
+def row_moments(stripe):
+    shape = (3 * stripe, stripe * PIX)
+    row, place = iota(shape, 0), iota(shape, 1)
+    hit = place // PIX == row % stripe
+    return jnp.where(hit, power(offset_of(place), row // stripe), 0.0).astype(BF16)
+
+
+def column_moments(chunk):
+    places = LANES // GROUP
+    shape = (CHUNK, LANES)
+    place, lane = iota(shape, 0), iota(shape, 1)
+    kind = (lane // GROUP + (places - chunk)) % places
+    hit = jnp.logical_and(place // PIX == lane % GROUP, kind < 3)
+    return jnp.where(hit, power(offset_of(place), kind), 0.0).astype(BF16)
+
+
+def moments_kernel(sizes, pixels, field, held, arrived):
     frames, stripe, blocks, cores, stripes = sizes
     width = blocks * SUBN
     places = LANES // GROUP
@@ -104,6 +107,8 @@
     for frame in range(frames):
         for part in range(blocks):
             copy(frame, part).start()
+    row_table = row_moments(stripe)
+    col_tables = [column_moments(chunk) for chunk in range(places)]
     position = (lax.axis_index("row") * blocks + lax.axis_index("col")) * cores + lax.axis_index("sub")
     group = iota((stripe, LANES), 1) // GROUP
 
@@ -119,12 +124,12 @@
         intensity, moment_x, moment_y, moment_two = [], [], [], []
         for part in range(blocks):
             copy(frame, part).wait()
-            lines = dot(row_table[...], held[frame, :, pl.ds(part * span, span)])
+            lines = dot(row_table, held[frame, :, pl.ds(part * span, span)])
             high, low = halves(lines)
             pieces = []
             for chunk in range(places):
                 cut = slice(chunk * CHUNK, (chunk + 1) * CHUNK)
-                weights = col_table[chunk]
+                weights = col_tables[chunk]
                 pieces.append(dot(high[:, cut], weights) + dot(low[:, cut], weights))
             plain = [piece[:stripe] for piece in pieces]
             tilted = [piece[stripe : 2 * stripe] for piece in pieces]
@@ -149,9 +154,9 @@
             target = block * cores + frame
             own = slice(block * SUBN, (block + 1) * SUBN)
             field[target, :stripe, :] = source
-            field[target, stripe:, :] = spill
-            extras[target, :stripe, :] = mean_flux[:, own]
-            extras[target, stripe:, :] = spot_size[:, own]
+            field[target, stripe : stripe + 8, :] = spill
+            field[target, stripe + 8 :, :SUBN] = mean_flux[:, own]
+            field[target, stripe + 8 :, SUBN : 2 * SUBN] = spot_size[:, own]
 
 
 def rims_kernel(
@@ -166,10 +171,10 @@
     for piece in range(pieces):
         block = field[piece, :stripe, :]
         if piece:
-            head = block[:8] + field[piece - 1, stripe:, :]
+            head = block[:8] + field[piece - 1, stripe : stripe + 8, :]
             block = head if stripe == 8 else jnp.concatenate([head, block[8:]], 0)
         parts.append(block)
-    spill = field[pieces - 1, stripe:, :]
+    spill = field[pieces - 1, stripe : stripe + 8, :]
     parts.append(spill)
     source = jnp.concatenate(parts, 0)
     across = dot_three(halves(source), (basis_high[...], basis_low[...]))
@@ -298,24 +303,20 @@
     pieces = blocks * cores
     assert frames == cores and width == blocks * SUBN and stripe * pieces == SUBN
 
-    field, extras = pl.pallas_call(
+    field = pl.pallas_call(
         functools.partial(moments_kernel, (frames, stripe, blocks, cores, rows * pieces)),
-        out_shape=(
-            jax.ShapeDtypeStruct((pieces, stripe + 8, width), F32),
-            jax.ShapeDtypeStruct((pieces, 2 * stripe, SUBN), F32),
-        ),
-        in_specs=[pl.BlockSpec(memory_space=pl.ANY)] + in_vmem(2),
-        out_specs=tuple(in_vmem(2)),
+        out_shape=jax.ShapeDtypeStruct((pieces, 2 * stripe + 8, width), F32),
+        in_specs=[pl.BlockSpec(memory_space=pltpu.HBM)],
+        out_specs=pl.BlockSpec(memory_space=pltpu.VMEM),
         scratch_shapes=[
             pltpu.VMEM((frames, pixel_rows, pixel_cols), BF16),
             pltpu.SemaphoreType.DMA((frames, blocks)),
         ],
         compiler_params=PARAMS,
         name="moments",
-    )(pixels, jnp.asarray(row_moments(stripe)), jnp.asarray(column_moments()))
+    )(pltpu.with_memory_space_constraint(pixels, pltpu.HBM))
 
     field = lax.all_to_all(field, ("col", "sub"), split_axis=0, concat_axis=0, tiled=True)
-    extras = lax.all_to_all(extras, ("col", "sub"), split_axis=0, concat_axis=0, tiled=True)
 
     vectors, scale = sine_basis()
     basis = column_basis(blocks)
@@ -365,8 +366,8 @@
         received, spread, near, *basis_pair, *back_pair, *halo_pair, *out_pair, scale_wide,
         jnp.asarray(coarse_table(rows, blocks, tail)),
     )
-    mean_flux = extras[:, :stripe].reshape(1, SUBN, SUBN)
-    spot_size = extras[:, stripe:].reshape(1, SUBN, SUBN)
+    mean_flux = field[:, stripe + 8 :, :SUBN].reshape(1, SUBN, SUBN)
+    spot_size = field[:, stripe + 8 :, SUBN : 2 * SUBN].reshape(1, SUBN, SUBN)
     return phase, mean_flux, spot_size
 
 

time: 36.7 us -> 29.7 us (0.81)
  local copies, waits for them, and re-layouts: 4.08 us -> 0.75 us
  starting transfers between devices: 8.19 us -> 4.87 us
  waiting for transfers between devices: 7.11 us -> 5.09 us
  blocking collectives: 9 us -> 10.4 us
  Pallas kernels: 6.98 us -> 7.41 us
    unnamed x34 -> x28, local copies, waits for them, and re-layouts: 3.42 us -> 0.1 us
    all_to_all x1 -> x0, starting transfers between devices: 3.32 us -> none  [body(): lax.all_to_all(extras, ('col', 'sub'), split_axis=0, concat_axis=0, tiled...]
    all_to_all x1 -> x0, waiting for transfers between devices: 2.03 us -> none  [body(): lax.all_to_all(extras, ('col', 'sub'), split_axis=0, concat_axis=0, tiled...]
    all_to_all x1, blocking collectives: 9 us -> 10.4 us  [body(): lax.all_to_all(field, ('col', 'sub'), split_axis=0, concat_axis=0, tiled=...]
    pallas_call x1, Pallas kernels: 2.85 us -> 3.27 us  [body(): pl.pallas_call(functools.partial(moments_kernel, (frames, stripe, blocks,...]
  transfers between devices with their start and end apart: 2 -> 1, of which waited for: 2 -> 1; matrix products, arithmetic and copies ran while one was open for 2% -> 2% of each run, Pallas kernels for 7% -> 0%
where the time goes in v2:
time: 29.7 us; the launch traced here: 29.3 us
  blocking collectives  10.4 us (35%)
  Pallas kernels  7.41 us (25%)
  waiting for transfers between devices  5.09 us (17%)
  starting transfers between devices  4.87 us (16%)
  between operations  0.82 us (3%)
  local copies, waits for them, and re-layouts  0.75 us (3%)
    all_to_all x1, blocking collectives, body(): lax.all_to_all(field, ('col', 'sub'), split_axis=0, concat_axis=0, tiled=...  10.4 us
    all_to_all x1, waiting for transfers between devices, body(): lax.all_to_all(sent, 'row', split_axis=0, concat_axis=0, tiled=True)  5.09 us
    all_to_all x1, starting transfers between devices, body(): lax.all_to_all(sent, 'row', split_axis=0, concat_axis=0, tiled=True)  4.87 us
    pallas_call x1, Pallas kernels, body(): pl.pallas_call(functools.partial(moments_kernel, (frames, stripe, blocks,...  3.27 us
    pallas_call x1, Pallas kernels, body(): pl.pallas_call(functools.partial(rims_kernel, (stripe, pieces, blocks, ro...  2.49 us
    pallas_call x1, Pallas kernels, body(): pl.pallas_call(functools.partial(phase_kernel, (blocks, rows)), out_shape...  1.65 us
    slice x1, local copies, waits for them, and re-layouts, body(): spot_size = field[:, stripe + 8:, SUBN:2 * SUBN].reshape(1, SUBN, SUBN)  0.66 us
  transfers between devices with their start and end apart: 1, of which 1 were waited for; matrix products, arithmetic and copies ran while one was open for 2% of the time, Pallas kernels for 0%

profile of v2, /device:TPU:0, one launch (start us, length us, event | category | flops | bytes accessed | tf_op | source)
XLA Modules:
  0.0 29.3 jit_solution(570061038323999669)
XLA Ops:
  0.6 0.0 copy-start
  0.6 0.0 copy-start.3
  0.7 0.0 copy-start.4
  0.7 0.0 copy-start.1
  0.7 0.0 copy-start.2
  0.7 0.0 copy-start.12
  0.7 0.0 copy-start.13
  0.7 0.0 copy-start.5
  0.7 0.0 copy-start.6
  0.7 0.0 copy-start.7
  0.8 0.0 copy-start.8
  0.8 0.0 copy-start.9
  0.8 0.0 copy-start.10
  0.8 0.0 copy-start.11
  0.8 3.3 %moments.1 = f32[4,72,256]{2,1,0:T(8,128)S(1)} custom-call(bf16[2,256,2048]{2,1,0:T(8,128)(2,1)} %pixels.1), custom_call_target="tpu_custom_call" | custom-call | tf_op jit(solution)/shard_map/moments/pallas_call | solution.py:306
  4.1 10.4 %all_to_all.10.field = f32[4,72,256]{2,1,0:T(8,128)S(1)} all-to-all(f32[4,72,256]{2,1,0:T(8,128)S(1)} %moments.1), channel_id=1, replica_groups=mesh['groups'=2,'row'=4,'col'=2,'sub'=2] {'col','sub'}, dimensions={0} | all-to-all | bytes 589824 | tf_op jit(solution)/shard_map/all_to_all | solution.py:319
  14.5 0.0 copy-done
  14.6 2.5 %rims.1 = (f32[4,32,128]{2,1,0:T(8,128)}, f32[144,128]{1,0:T(8,128)S(1)}, f32[16,128]{1,0:T(8,128)S(1)}) custom-call(f32[4,72,256]{2,1,0:T(8,128)S(1)} %all_to_all.10.field, bf16[256,288]{1,0:T(8,128)(2,1)S(1)} %copy-done.2, bf16[256,288]{1,0:T(8,128)(2,1)S(1)} %copy-done.1, bf16[2,288,128]{2,1,0:T(8,128)(2,1)S(1)} %copy-done.4, ...), custom_call_target="tpu_custom_call" | custom-call | tf_op jit(solution)/shard_map/rims/pallas_call | solution.py:338
  17.0 4.9 %all-to-all-start.1 = ((f32[4,32,128]{2,1,0:T(8,128)}), f32[4,32,128]{2,1,0:T(8,128)S(1)}, u32[]{:S(2)}, u32[]{:S(2)}) async-start(f32[4,32,128]{2,1,0:T(8,128)} %get-tuple-element.6), calls=%async_computation.1 | async-start | bytes 131072 | tf_op jit(solution)/shard_map/all_to_all | solution.py:351
  21.9 0.7 %fusion = (f32[4,32,128]{2,1,0:T(8,128)}, f32[4,32,128]{2,1,0:T(8,128)}) fusion(f32[4,72,256]{2,1,0:T(8,128)S(1)} %all_to_all.10.field), kind=kLoop, calls=%fused_computation | loop fusion | bytes 262144 | tf_op jit(solution)/shard_map/slice | solution.py:370
  22.6 5.1 %all-to-all-done.1.received = f32[4,32,128]{2,1,0:T(8,128)S(1)} async-done(((f32[4,32,128]{2,1,0:T(8,128)}), f32[4,32,128]{2,1,0:T(8,128)S(1)}, u32[]{:S(2)}, u32[]{:S(2)}) %all-to-all-start.1) | async-done | bytes 65568 | tf_op jit(solution)/shard_map/all_to_all | solution.py:351
  27.7 0.0 copy-done.9
  27.7 0.0 copy-done.10
  27.7 1.7 %phase.1 = f32[1,128,128]{2,1,0:T(8,128)} custom-call(f32[4,32,128]{2,1,0:T(8,128)S(1)} %all-to-all-done.1.received, f32[144,128]{1,0:T(8,128)S(1)} %get-tuple-element.7.spread, f32[16,128]{1,0:T(8,128)S(1)} %get-tuple-element.8.near, bf16[256,288]{1,0:T(8,128)(2,1)S(1)} %copy-done.2, bf16[256,288]{1,0:T(8,128)(2,1)S(1)} %copy-done.1, ...), custom_call_target="tpu_custom_call" | custom-call | tf_op jit(solution)/shard_map/phase/pallas_call | solution.py:358
  (11 shorter events, 0.0 us)
Async XLA Ops:
  0.6 13.9 %copy-start = (f32[144,288]{1,0:T(8,128)S(1)}, f32[144,288]{1,0:T(8,128)}, u32[]{:S(2)}) copy-start(f32[144,288]{1,0:T(8,128)} %constant.32.clone.scale) | copy-start | bytes 497668
  0.6 13.8 %copy-start.3 = (bf16[2,288,128]{2,1,0:T(8,128)(2,1)S(1)}, bf16[2,288,128]{2,1,0:T(8,128)(2,1)}, u32[]{:S(2)}) copy-start(bf16[2,288,128]{2,1,0:T(8,128)(2,1)} %constant.31.clone.back_low) | copy-start | bytes 442372
  0.7 13.8 %copy-start.4 = (bf16[2,288,128]{2,1,0:T(8,128)(2,1)S(1)}, bf16[2,288,128]{2,1,0:T(8,128)(2,1)}, u32[]{:S(2)}) copy-start(bf16[2,288,128]{2,1,0:T(8,128)(2,1)} %constant.30.clone.back_high) | copy-start | bytes 442372
  0.7 13.8 %copy-start.1 = (bf16[256,288]{1,0:T(8,128)(2,1)S(1)}, bf16[256,288]{1,0:T(8,128)(2,1)}, u32[]{:S(2)}) copy-start(bf16[256,288]{1,0:T(8,128)(2,1)} %constant.29.clone.basis_low) | copy-start | bytes 442372
  0.7 13.8 %copy-start.2 = (bf16[256,288]{1,0:T(8,128)(2,1)S(1)}, bf16[256,288]{1,0:T(8,128)(2,1)}, u32[]{:S(2)}) copy-start(bf16[256,288]{1,0:T(8,128)(2,1)} %constant.28.clone.basis_high) | copy-start | bytes 442372
  0.7 13.8 %copy-start.12 = (bf16[16,144]{1,0:T(8,128)(2,1)S(1)}, bf16[16,144]{1,0:T(8,128)(2,1)}, u32[]{:S(2)}) copy-start(bf16[16,144]{1,0:T(8,128)(2,1)} %constant.36.clone.edge_low) | copy-start | bytes 13828
  0.7 13.8 %copy-start.13 = (bf16[16,144]{1,0:T(8,128)(2,1)S(1)}, bf16[16,144]{1,0:T(8,128)(2,1)}, u32[]{:S(2)}) copy-start(bf16[16,144]{1,0:T(8,128)(2,1)} %constant.35.clone.edge_high) | copy-start | bytes 13828
  0.7 13.8 %copy-start.5 = (bf16[432,136]{1,0:T(8,128)(2,1)S(1)}, bf16[432,136]{1,0:T(8,128)(2,1)}, u32[]{:S(2)}) copy-start(bf16[432,136]{1,0:T(8,128)(2,1)} %constant.34.clone.drive_low) | copy-start | bytes 352516
  0.7 13.8 %copy-start.6 = (bf16[432,136]{1,0:T(8,128)(2,1)S(1)}, bf16[432,136]{1,0:T(8,128)(2,1)}, u32[]{:S(2)}) copy-start(bf16[432,136]{1,0:T(8,128)(2,1)} %constant.33.clone.drive_high) | copy-start | bytes 352516
  0.7 26.9 %copy-start.7 = (bf16[128,144]{1,0:T(8,128)(2,1)S(1)}, bf16[128,144]{1,0:T(8,128)(2,1)}, u32[]{:S(2)}) copy-start(bf16[128,144]{1,0:T(8,128)(2,1)} %constant.40.clone.out_low) | copy-start | bytes 110596
  0.8 26.9 %copy-start.8 = (bf16[128,144]{1,0:T(8,128)(2,1)S(1)}, bf16[128,144]{1,0:T(8,128)(2,1)}, u32[]{:S(2)}) copy-start(bf16[128,144]{1,0:T(8,128)(2,1)} %constant.39.clone.out_high) | copy-start | bytes 110596
  0.8 26.9 %copy-start.9 = (bf16[144,24]{1,0:T(8,128)(2,1)S(1)}, bf16[144,24]{1,0:T(8,128)(2,1)}, u32[]{:S(2)}) copy-start(bf16[144,24]{1,0:T(8,128)(2,1)} %constant.38.clone.halo_low) | copy-start | bytes 20740
  0.8 26.9 %copy-start.10 = (bf16[144,24]{1,0:T(8,128)(2,1)S(1)}, bf16[144,24]{1,0:T(8,128)(2,1)}, u32[]{:S(2)}) copy-start(bf16[144,24]{1,0:T(8,128)(2,1)} %constant.37.clone.halo_high) | copy-start | bytes 20740
  0.8 26.9 %copy-start.11 = (f32[4,8,128]{2,1,0:T(8,128)S(1)}, f32[4,8,128]{2,1,0:T(8,128)}, u32[]{:S(2)}) copy-start(f32[4,8,128]{2,1,0:T(8,128)} %constant.41.clone.coarse) | copy-start | bytes 49156
  17.0 10.6 %all-to-all-start.1 = ((f32[4,32,128]{2,1,0:T(8,128)}), f32[4,32,128]{2,1,0:T(8,128)S(1)}, u32[]{:S(2)}, u32[]{:S(2)}) async-start(f32[4,32,128]{2,1,0:T(8,128)} %get-tuple-element.6), calls=%async_computation.1 | async-start | bytes 131072 | tf_op jit(solution)/shard_map/all_to_all | solution.py:351

commit v3 on v2

--- a/solution.py
+++ b/solution.py
@@ -21,9 +21,10 @@
 BF16 = jnp.bfloat16
 
 
-def split_const(values):
+def constant_pair(values):
     high = np.asarray(values).astype(jnp.bfloat16)
-    return high, (values - high.astype(np.float64)).astype(jnp.bfloat16)
+    low = (values - high.astype(np.float64)).astype(jnp.bfloat16)
+    return jnp.asarray(high), jnp.asarray(low)
 
 
 def sine_basis():
@@ -33,15 +34,33 @@
     return vectors, 1.0 / (spectrum[:, None] + spectrum[None, :] + DAMPING)
 
 
+def padded(blocks):
+    return -(-blocks * WIN // LANES) * LANES
+
+
 def column_basis(blocks):
     vectors, _ = sine_basis()
-    table = np.zeros((blocks * SUBN, blocks * WIN))
+    table = np.zeros((blocks * SUBN, padded(blocks)))
     for block in range(blocks):
         low = max(block * SUBN - MARGIN, 0)
         high = min((block + 1) * SUBN + MARGIN, blocks * SUBN)
         start = low - (block * SUBN - MARGIN)
         table[low:high, block * WIN : (block + 1) * WIN] = vectors[start : start + high - low]
     return table
+
+
+def widened(table, blocks):
+    wide = np.zeros(table.shape[:-1] + (padded(blocks),), np.float32)
+    wide[..., : blocks * WIN] = np.tile(table, (1,) * (table.ndim - 1) + (blocks,))
+    return wide
+
+
+def edge_tables():
+    vectors, scale = sine_basis()
+    ends = np.concatenate([vectors[:8], vectors[WIN - 8 :]], 0)
+    def driven_by(rows):
+        return np.einsum("oa,ai,ab->iob", ends, vectors[:, rows], scale)
+    return driven_by(slice(WIN - 8, WIN)), driven_by(slice(0, 9))
 
 
 def coarse_inverse(blocks_down, blocks_across):
@@ -120,29 +139,25 @@
 
     row = iota((stripe, width), 0)
     column = iota((stripe, width), 1)
-    for frame in range(frames):
-        intensity, moment_x, moment_y, moment_two = [], [], [], []
-        for part in range(blocks):
-            copy(frame, part).wait()
-            lines = dot(row_table, held[frame, :, pl.ds(part * span, span)])
-            high, low = halves(lines)
-            pieces = []
-            for chunk in range(places):
-                cut = slice(chunk * CHUNK, (chunk + 1) * CHUNK)
-                weights = col_tables[chunk]
-                pieces.append(dot(high[:, cut], weights) + dot(low[:, cut], weights))
-            plain = [piece[:stripe] for piece in pieces]
-            tilted = [piece[stripe : 2 * stripe] for piece in pieces]
-            bent = [piece[2 * stripe :] for piece in pieces]
-            intensity.append(gather(plain, 0))
-            moment_x.append(gather(plain, 1))
-            moment_y.append(gather(tilted, 0))
-            moment_two.append(gather(plain, 2) + gather(bent, 0))
-        intensity = jnp.concatenate(intensity, 1)
+
+    def columns_of(lines):
+        high, low = halves(lines)
+        pieces = []
+        for chunk in range(places):
+            cut = slice(chunk * CHUNK, (chunk + 1) * CHUNK)
+            weights = col_tables[chunk]
+            pieces.append(dot(high[:, cut], weights) + dot(low[:, cut], weights))
+        plain = [piece[:stripe] for piece in pieces]
+        tilted = [piece[stripe : 2 * stripe] for piece in pieces]
+        bent = [piece[2 * stripe :] for piece in pieces]
+        return gather(plain, 0), gather(plain, 1), gather(tilted, 0), gather(plain, 2) + gather(bent, 0)
+
+    def finish(frame, parts):
+        intensity, moment_x, moment_y, moment_two = [jnp.concatenate(kind, 1) for kind in zip(*parts)]
         inverse = 1.0 / intensity
-        slope_x = jnp.concatenate(moment_x, 1) * inverse
-        slope_y = jnp.concatenate(moment_y, 1) * inverse
-        spot_size = jnp.concatenate(moment_two, 1) * inverse - slope_x * slope_x - slope_y * slope_y
+        slope_x = moment_x * inverse
+        slope_y = moment_y * inverse
+        spot_size = moment_two * inverse - slope_x * slope_x - slope_y * slope_y
         mean_flux = intensity * (1.0 / (PIX * PIX))
         flow_x = jnp.where(column < width - 1, slope_x, 0.0)
         flow_y = jnp.where(position * stripe + row < stripes * stripe - 1, slope_y, 0.0)
@@ -158,13 +173,31 @@
             field[target, stripe + 8 :, :SUBN] = mean_flux[:, own]
             field[target, stripe + 8 :, SUBN : 2 * SUBN] = spot_size[:, own]
 
+    waiting, parts = None, []
+
+    def advance():
+        frame, lines = waiting
+        parts.append(columns_of(lines))
+        if len(parts) == blocks:
+            finish(frame, parts)
+            parts.clear()
+
+    for frame in range(frames):
+        for part in range(blocks):
+            copy(frame, part).wait()
+            lines = dot(row_table, held[frame, :, pl.ds(part * span, span)])
+            if waiting is not None:
+                advance()
+            waiting = (frame, lines)
+    advance()
+
 
 def rims_kernel(
     sizes, field, basis_high, basis_low, back_high, back_low, drive_high, drive_low, edge_high, edge_low, scale,
-    sent, spread, near,
+    above_table, below_table, sent, spectrum, near,
 ):
     stripe, pieces, blocks, rows = sizes
-    width = blocks * SUBN
+    tiles = padded(blocks) // LANES
     mine = lax.axis_index("row")
     side = lax.axis_index("col")
     parts = []
@@ -179,20 +212,18 @@
     source = jnp.concatenate(parts, 0)
     across = dot_three(halves(source), (basis_high[...], basis_low[...]))
     driven = dot_three((drive_high[...], drive_low[...]), halves(across))
-    factor = scale[...]
-    responses = [driven[k * WIN : (k + 1) * WIN] * factor for k in range(3)]
-    response = jnp.concatenate(responses, 0)
-    back = (back_high[side], back_low[side])
-    reach = dot_three(halves(response), back)
-    spread[...] = reach[:WIN]
-    edge = (edge_high[...], edge_low[...])
-    high, low = halves(reach)
-    rims = [
-        dot_three(edge, (high[k * WIN : (k + 1) * WIN], low[k * WIN : (k + 1) * WIN])) for k in range(3)
-    ]
-    near[:8, :] = jnp.where(mine > 0, rims[1][8:], 0.0)
-    near[8:, :] = jnp.where(mine < rows - 1, rims[2][:8], 0.0)
-    base = 8 * blocks
+    response = driven * scale[...]
+    spectrum[...] = response
+    edges = [dot_three((edge_high[...], edge_low[...]), halves(response))]
+    for table, start, count in ((above_table, 0, 8), (below_table, SUBN - 8, 9)):
+        total = across[start : start + 1] * table[0]
+        for step in range(1, count):
+            total = total + across[start + step : start + step + 1] * table[step]
+        edges.append(total)
+    rims = dot_three(halves(jnp.concatenate(edges, 0)), (back_high[side], back_low[side]))
+    near[:8, :] = jnp.where(mine > 0, rims[24:32], 0.0)
+    near[8:, :] = jnp.where(mine < rows - 1, rims[32:40], 0.0)
+    base = 8 * tiles
     tail = sent.shape[1] - base - 8
     total = jnp.sum(source[:SUBN], 0, keepdims=True)
     place = iota((tail, LANES), 0)
@@ -201,41 +232,45 @@
         cut = slice(block * SUBN, (block + 1) * SUBN)
         sums = jnp.where(place == block, total[:, cut], sums)
         sums = jnp.where(place == blocks + block, spill[:1, cut], sums)
+    for tile in range(tiles):
+        cut = slice(tile * LANES, (tile + 1) * LANES)
+        sums = jnp.where(place == 2 * blocks + tile, across[SUBN : SUBN + 1, cut], sums)
     for target in range(rows):
         sent[target, : base + 8, :] = jnp.zeros((base + 8, LANES), F32)
         sent[target, base + 8 :, :] = sums
 
-    def put(target, rim, raw):
+    def put(target, rim, lines):
         sent[target, base : base + 8, :] = rim
-        if raw is not None:
-            for block in range(blocks):
-                sent[target, 8 * block : 8 * block + 8, :] = raw[:, block * SUBN : (block + 1) * SUBN]
+        if lines is not None:
+            for tile in range(tiles):
+                sent[target, 8 * tile : 8 * tile + 8, :] = lines[:, tile * LANES : (tile + 1) * LANES]
 
     @pl.when(mine >= 1)
     def _():
-        put(mine - 1, rims[0][:8], source[:8])
+        put(mine - 1, rims[:8], across[:8])
 
     @pl.when(mine >= 2)
     def _():
-        put(mine - 2, rims[1][:8], None)
+        put(mine - 2, rims[16:24], None)
 
     @pl.when(mine + 1 < rows)
     def _():
-        put(mine + 1, rims[0][8:], source[SUBN - 8 : SUBN])
+        put(mine + 1, rims[8:16], across[SUBN - 8 : SUBN])
 
     @pl.when(mine + 2 < rows)
     def _():
-        put(mine + 2, rims[2][8:], None)
+        put(mine + 2, rims[40:], None)
 
 
 def phase_kernel(
-    sizes, received, spread, near, basis_high, basis_low, back_high, back_low, halo_high, halo_low,
-    out_high, out_low, scale, coarse, phase,
+    sizes, received, spectrum, near, back_high, back_low, halo_high, halo_low, out_high, out_low, scale, coarse,
+    phase,
 ):
     blocks, rows = sizes
+    tiles = padded(blocks) // LANES
     mine = lax.axis_index("row")
     side = lax.axis_index("col")
-    base = 8 * blocks
+    base = 8 * tiles
     tail = received.shape[1] - base - 8
     above = jnp.maximum(mine - 1, 0)
     below = jnp.minimum(mine + 1, rows - 1)
@@ -243,23 +278,23 @@
     has_below = mine < rows - 1
     first = iota((8, LANES), 0) == 0
     top, bottom, spilt = [], [], []
-    for block in range(blocks):
-        top.append(jnp.where(has_above, received[above, 8 * block : 8 * block + 8, :], 0.0))
-        bottom.append(jnp.where(has_below, received[below, 8 * block : 8 * block + 8, :], 0.0))
-        line = received[above, pl.ds(base + 8 + blocks + block, 1), :]
+    for tile in range(tiles):
+        top.append(jnp.where(has_above, received[above, 8 * tile : 8 * tile + 8, :], 0.0))
+        bottom.append(jnp.where(has_below, received[below, 8 * tile : 8 * tile + 8, :], 0.0))
+        line = received[above, pl.ds(base + 8 + 2 * blocks + tile, 1), :]
         spilt.append(jnp.where(jnp.logical_and(first, has_above), line, 0.0))
-    halo = jnp.concatenate(
+    across = jnp.concatenate(
         [jnp.concatenate(top, 1), jnp.concatenate(spilt, 1), jnp.concatenate(bottom, 1)], 0
     )
-    across = dot_three(halves(halo), (basis_high[...], basis_low[...]))
     driven = dot_three((halo_high[...], halo_low[...]), halves(across))
-    reach = dot_three(halves(driven * scale[...]), (back_high[side], back_low[side]))
-    solved = dot_three((out_high[...], out_low[...]), halves(spread[...] + reach))
-    weighted = jnp.zeros((tail, LANES), F32)
+    response = spectrum[...] + driven * scale[...]
+    reach = dot_three(halves(response), (back_high[side], back_low[side]))
+    solved = dot_three((out_high[...], out_low[...]), halves(reach))
+    weighted = jnp.zeros((tail, coarse.shape[2]), F32)
     for origin in range(rows):
         count = jnp.sum(received[origin, base + 8 :, :], 1, keepdims=True)
         weighted = weighted + count * coarse[origin]
-    own = iota((tail, LANES), 1) == mine * blocks + side
+    own = iota(weighted.shape, 1) == mine * blocks + side
     level = jnp.sum(jnp.where(own, weighted, 0.0), keepdims=True)
     solved = solved + level
     head = near[:8, :] + jnp.where(has_above, received[above, base : base + 8, :], 0.0)
@@ -320,50 +355,46 @@
 
     vectors, scale = sine_basis()
     basis = column_basis(blocks)
-    basis_pair = [jnp.asarray(part) for part in split_const(basis)]
-    back = basis.T.reshape(blocks * WIN, blocks, SUBN).transpose(1, 0, 2)
-    back_pair = [jnp.asarray(part) for part in split_const(back)]
-    scale_wide = jnp.asarray(np.tile(scale, (1, blocks)).astype(np.float32))
-    reached = SUBN + 8
-    drive = np.zeros((3, WIN, reached))
-    drive[0] = vectors[:, MARGIN:]
-    drive[1, :, :8] = vectors[:, WIN - 8 :]
-    drive[2, :, SUBN - 8 : SUBN + 1] = vectors[:, :9]
-    drive_pair = [jnp.asarray(part) for part in split_const(drive.reshape(3 * WIN, reached))]
-    edge = np.concatenate([vectors[:8], vectors[WIN - 8 :]], 0)
-    edge_pair = [jnp.asarray(part) for part in split_const(edge)]
-    tail = -(-2 * blocks // 8) * 8
-    height = 8 * blocks + 8 + tail
-
-    sent, spread, near = pl.pallas_call(
+    full = padded(blocks)
+    tiles = full // LANES
+    basis_pair = constant_pair(basis)
+    back_pair = constant_pair(basis.T.reshape(full, blocks, SUBN).transpose(1, 0, 2))
+    scale_wide = jnp.asarray(widened(scale, blocks))
+    drive_pair = constant_pair(vectors[:, MARGIN:])
+    edge_pair = constant_pair(np.concatenate([vectors[:8], vectors[WIN - 8 :]], 0))
+    side_tables = [jnp.asarray(widened(table, blocks)) for table in edge_tables()]
+    tail = -(-(2 * blocks + tiles) // 8) * 8
+    height = 8 * tiles + 8 + tail
+
+    sent, spectrum, near = pl.pallas_call(
         functools.partial(rims_kernel, (stripe, pieces, blocks, rows)),
         out_shape=(
             jax.ShapeDtypeStruct((rows, height, LANES), F32),
-            jax.ShapeDtypeStruct((WIN, SUBN), F32),
+            jax.ShapeDtypeStruct((WIN, full), F32),
             jax.ShapeDtypeStruct((16, SUBN), F32),
         ),
-        in_specs=in_vmem(10),
+        in_specs=in_vmem(12),
         out_specs=tuple(in_vmem(3)),
         compiler_params=PARAMS,
         name="rims",
-    )(field, *basis_pair, *back_pair, *drive_pair, *edge_pair, scale_wide)
+    )(field, *basis_pair, *back_pair, *drive_pair, *edge_pair, scale_wide, *side_tables)
 
     received = lax.all_to_all(sent, "row", split_axis=0, concat_axis=0, tiled=True)
 
     halo = np.zeros((WIN, 24))
     halo[:, :9] = vectors[:, :9]
     halo[:, 16:] = vectors[:, WIN - 8 :]
-    halo_pair = [jnp.asarray(part) for part in split_const(halo)]
-    out_pair = [jnp.asarray(part) for part in split_const(vectors[MARGIN : MARGIN + SUBN])]
+    halo_pair = constant_pair(halo)
+    out_pair = constant_pair(vectors[MARGIN : MARGIN + SUBN])
     phase = pl.pallas_call(
         functools.partial(phase_kernel, (blocks, rows)),
         out_shape=jax.ShapeDtypeStruct((1, SUBN, SUBN), F32),
-        in_specs=in_vmem(13),
+        in_specs=in_vmem(11),
         out_specs=pl.BlockSpec(memory_space=pltpu.VMEM),
         compiler_params=PARAMS,
         name="phase",
     )(
-        received, spread, near, *basis_pair, *back_pair, *halo_pair, *out_pair, scale_wide,
+        received, spectrum, near, *back_pair, *halo_pair, *out_pair, scale_wide,
         jnp.asarray(coarse_table(rows, blocks, tail)),
     )
     mean_flux = field[:, stripe + 8 :, :SUBN].reshape(1, SUBN, SUBN)

time: 29.7 us -> 28 us (0.943)
  Pallas kernels: 7.41 us -> 5.77 us
    pallas_call x1, Pallas kernels: 2.49 us -> 1.49 us  [body(): pl.pallas_call(functools.partial(rims_kernel, (stripe, pieces, blocks, ro...]
    pallas_call x1, Pallas kernels: 1.65 us -> 1.32 us  [body(): pl.pallas_call(functools.partial(phase_kernel, (blocks, rows)), out_shape...]
    pallas_call x1, Pallas kernels: 3.27 us -> 2.96 us  [body(): pl.pallas_call(functools.partial(moments_kernel, (frames, stripe, blocks,...]
where the time goes in v3:
time: 28 us; the launch traced here: 27.8 us
  blocking collectives  10.4 us (37%)
  Pallas kernels  5.77 us (21%)
  waiting for transfers between devices  5.13 us (18%)
  starting transfers between devices  4.88 us (17%)
  between operations  0.85 us (3%)
  local copies, waits for them, and re-layouts  0.77 us (3%)
    all_to_all x1, blocking collectives, body(): lax.all_to_all(field, ('col', 'sub'), split_axis=0, concat_axis=0, tiled=...  10.4 us
    all_to_all x1, waiting for transfers between devices, body(): lax.all_to_all(sent, 'row', split_axis=0, concat_axis=0, tiled=True)  5.13 us
    all_to_all x1, starting transfers between devices, body(): lax.all_to_all(sent, 'row', split_axis=0, concat_axis=0, tiled=True)  4.88 us
    pallas_call x1, Pallas kernels, body(): pl.pallas_call(functools.partial(moments_kernel, (frames, stripe, blocks,...  2.96 us
    pallas_call x1, Pallas kernels, body(): pl.pallas_call(functools.partial(rims_kernel, (stripe, pieces, blocks, ro...  1.49 us
    pallas_call x1, Pallas kernels, body(): pl.pallas_call(functools.partial(phase_kernel, (blocks, rows)), out_shape...  1.32 us
    slice x1, local copies, waits for them, and re-layouts, body(): spot_size = field[:, stripe + 8:, SUBN:2 * SUBN].reshape(1, SUBN, SUBN)  0.66 us
  transfers between devices with their start and end apart: 1, of which 1 were waited for; matrix products, arithmetic and copies ran while one was open for 2% of the time, Pallas kernels for 0%

profile of v3, /device:TPU:0, one launch (start us, length us, event | category | flops | bytes accessed | tf_op | source)
XLA Modules:
  0.0 27.8 jit_solution(1209978507992010453)
XLA Ops:
  0.6 0.0 copy-start.4
  0.6 0.0 copy-start.5
  0.7 0.0 copy-start.1
  0.7 0.0 copy-start.2
  0.7 0.0 copy-start
  0.7 0.0 copy-start.7
  0.7 0.0 copy-start.8
  0.7 0.0 copy-start.14
  0.7 0.0 copy-start.15
  0.7 0.0 copy-start.6
  0.8 0.0 copy-start.3
  0.8 0.0 copy-start.9
  0.8 0.0 copy-start.10
  0.8 0.0 copy-start.11
  0.8 0.0 copy-start.12
  0.8 0.0 copy-start.13
  0.8 3.0 %moments.1 = f32[4,72,256]{2,1,0:T(8,128)S(1)} custom-call(bf16[2,256,2048]{2,1,0:T(8,128)(2,1)} %pixels.1), custom_call_target="tpu_custom_call" | custom-call | tf_op jit(solution)/shard_map/moments/pallas_call | solution.py:341
  3.8 10.4 %all_to_all.10.field = f32[4,72,256]{2,1,0:T(8,128)S(1)} all-to-all(f32[4,72,256]{2,1,0:T(8,128)S(1)} %moments.1), channel_id=1, replica_groups=mesh['groups'=2,'row'=4,'col'=2,'sub'=2] {'col','sub'}, dimensions={0} | all-to-all | bytes 589824 | tf_op jit(solution)/shard_map/all_to_all | solution.py:354
  14.2 0.0 copy-done.1
  14.3 1.5 %rims.1 = (f32[4,40,128]{2,1,0:T(8,128)}, f32[144,384]{1,0:T(8,128)S(1)}, f32[16,128]{1,0:T(8,128)S(1)}) custom-call(f32[4,72,256]{2,1,0:T(8,128)S(1)} %all_to_all.10.field, bf16[256,384]{1,0:T(8,128)(2,1)S(1)} %copy-done.4, bf16[256,384]{1,0:T(8,128)(2,1)S(1)} %copy-done.5, bf16[2,384,128]{2,1,0:T(8,128)(2,1)S(1)} %copy-done.1, ...), custom_call_target="tpu_custom_call" | custom-call | tf_op jit(solution)/shard_map/rims/pallas_call | solution.py:369
  15.8 4.9 %all-to-all-start.1 = ((f32[4,40,128]{2,1,0:T(8,128)}), f32[4,40,128]{2,1,0:T(8,128)S(1)}, u32[]{:S(2)}, u32[]{:S(2)}) async-start(f32[4,40,128]{2,1,0:T(8,128)} %get-tuple-element.6), calls=%async_computation.1 | async-start | bytes 163840 | tf_op jit(solution)/shard_map/all_to_all | solution.py:382
  20.7 0.7 %fusion = (f32[4,32,128]{2,1,0:T(8,128)}, f32[4,32,128]{2,1,0:T(8,128)}) fusion(f32[4,72,256]{2,1,0:T(8,128)S(1)} %all_to_all.10.field), kind=kLoop, calls=%fused_computation | loop fusion | bytes 262144 | tf_op jit(solution)/shard_map/slice | solution.py:401
  21.3 5.1 %all-to-all-done.1.received = f32[4,40,128]{2,1,0:T(8,128)S(1)} async-done(((f32[4,40,128]{2,1,0:T(8,128)}), f32[4,40,128]{2,1,0:T(8,128)S(1)}, u32[]{:S(2)}, u32[]{:S(2)}) %all-to-all-start.1) | async-done | bytes 81952 | tf_op jit(solution)/shard_map/all_to_all | solution.py:382
  26.5 1.3 %phase.1 = f32[1,128,128]{2,1,0:T(8,128)} custom-call(f32[4,40,128]{2,1,0:T(8,128)S(1)} %all-to-all-done.1.received, f32[144,384]{1,0:T(8,128)S(1)} %get-tuple-element.7.spectrum, f32[16,128]{1,0:T(8,128)S(1)} %get-tuple-element.8.near, bf16[2,384,128]{2,1,0:T(8,128)(2,1)S(1)} %copy-done.1, bf16[2,384,128]{2,1,0:T(8,128)(2,1)S(1)} %copy-done.2, ...), custom_call_target="tpu_custom_call" | custom-call | tf_op jit(solution)/shard_map/phase/pallas_call | solution.py:389
  (15 shorter events, 0.0 us)
Async XLA Ops:
  0.6 13.6 %copy-start.4 = (bf16[256,384]{1,0:T(8,128)(2,1)S(1)}, bf16[256,384]{1,0:T(8,128)(2,1)}, u32[]{:S(2)}) copy-start(bf16[256,384]{1,0:T(8,128)(2,1)} %constant.32.clone.basis_high) | copy-start | bytes 589828
  0.6 13.6 %copy-start.5 = (bf16[256,384]{1,0:T(8,128)(2,1)S(1)}, bf16[256,384]{1,0:T(8,128)(2,1)}, u32[]{:S(2)}) copy-start(bf16[256,384]{1,0:T(8,128)(2,1)} %constant.33.clone.basis_low) | copy-start | bytes 589828
  0.7 13.6 %copy-start.1 = (bf16[2,384,128]{2,1,0:T(8,128)(2,1)S(1)}, bf16[2,384,128]{2,1,0:T(8,128)(2,1)}, u32[]{:S(2)}) copy-start(bf16[2,384,128]{2,1,0:T(8,128)(2,1)} %constant.34.clone.back_high) | copy-start | bytes 589828
  0.7 13.5 %copy-start.2 = (bf16[2,384,128]{2,1,0:T(8,128)(2,1)S(1)}, bf16[2,384,128]{2,1,0:T(8,128)(2,1)}, u32[]{:S(2)}) copy-start(bf16[2,384,128]{2,1,0:T(8,128)(2,1)} %constant.35.clone.back_low) | copy-start | bytes 589828
  0.7 13.5 %copy-start = (f32[144,384]{1,0:T(8,128)S(1)}, f32[144,384]{1,0:T(8,128)}, u32[]{:S(2)}) copy-start(f32[144,384]{1,0:T(8,128)} %constant.36.clone.scale) | copy-start | bytes 663556
  0.7 13.5 %copy-start.7 = (bf16[144,136]{1,0:T(8,128)(2,1)S(1)}, bf16[144,136]{1,0:T(8,128)(2,1)}, u32[]{:S(2)}) copy-start(bf16[144,136]{1,0:T(8,128)(2,1)} %constant.37.clone.drive_high) | copy-start | bytes 117508
  0.7 13.5 %copy-start.8 = (bf16[144,136]{1,0:T(8,128)(2,1)S(1)}, bf16[144,136]{1,0:T(8,128)(2,1)}, u32[]{:S(2)}) copy-start(bf16[144,136]{1,0:T(8,128)(2,1)} %constant.38.clone.drive_low) | copy-start | bytes 117508
  0.7 13.5 %copy-start.14 = (bf16[16,144]{1,0:T(8,128)(2,1)S(1)}, bf16[16,144]{1,0:T(8,128)(2,1)}, u32[]{:S(2)}) copy-start(bf16[16,144]{1,0:T(8,128)(2,1)} %constant.39.clone.edge_high) | copy-start | bytes 13828
  0.7 13.5 %copy-start.15 = (bf16[16,144]{1,0:T(8,128)(2,1)S(1)}, bf16[16,144]{1,0:T(8,128)(2,1)}, u32[]{:S(2)}) copy-start(bf16[16,144]{1,0:T(8,128)(2,1)} %constant.40.clone.edge_low) | copy-start | bytes 13828
  0.7 13.5 %copy-start.6 = (f32[8,16,384]{2,1,0:T(8,128)S(1)}, f32[8,16,384]{2,1,0:T(8,128)}, u32[]{:S(2)}) copy-start(f32[8,16,384]{2,1,0:T(8,128)} %constant.41.clone.above_table) | copy-start | bytes 589828
  0.8 13.5 %copy-start.3 = (f32[9,16,384]{2,1,0:T(8,128)S(1)}, f32[9,16,384]{2,1,0:T(8,128)}, u32[]{:S(2)}) copy-start(f32[9,16,384]{2,1,0:T(8,128)} %constant.42.clone.below_table) | copy-start | bytes 663556
  0.8 25.7 %copy-start.9 = (bf16[128,144]{1,0:T(8,128)(2,1)S(1)}, bf16[128,144]{1,0:T(8,128)(2,1)}, u32[]{:S(2)}) copy-start(bf16[128,144]{1,0:T(8,128)(2,1)} %constant.45.clone.out_high) | copy-start | bytes 110596
  0.8 25.7 %copy-start.10 = (bf16[128,144]{1,0:T(8,128)(2,1)S(1)}, bf16[128,144]{1,0:T(8,128)(2,1)}, u32[]{:S(2)}) copy-start(bf16[128,144]{1,0:T(8,128)(2,1)} %constant.46.clone.out_low) | copy-start | bytes 110596
  0.8 25.7 %copy-start.11 = (bf16[144,24]{1,0:T(8,128)(2,1)S(1)}, bf16[144,24]{1,0:T(8,128)(2,1)}, u32[]{:S(2)}) copy-start(bf16[144,24]{1,0:T(8,128)(2,1)} %constant.43.clone.halo_high) | copy-start | bytes 20740
  0.8 25.7 %copy-start.12 = (bf16[144,24]{1,0:T(8,128)(2,1)S(1)}, bf16[144,24]{1,0:T(8,128)(2,1)}, u32[]{:S(2)}) copy-start(bf16[144,24]{1,0:T(8,128)(2,1)} %constant.44.clone.halo_low) | copy-start | bytes 20740
  0.8 25.6 %copy-start.13 = (f32[4,8,128]{2,1,0:T(8,128)S(1)}, f32[4,8,128]{2,1,0:T(8,128)}, u32[]{:S(2)}) copy-start(f32[4,8,128]{2,1,0:T(8,128)} %constant.47.clone.coarse) | copy-start | bytes 49156
  15.8 10.7 %all-to-all-start.1 = ((f32[4,40,128]{2,1,0:T(8,128)}), f32[4,40,128]{2,1,0:T(8,128)S(1)}, u32[]{:S(2)}, u32[]{:S(2)}) async-start(f32[4,40,128]{2,1,0:T(8,128)} %get-tuple-element.6), calls=%async_computation.1 | async-start | bytes 163840 | tf_op jit(solution)/shard_map/all_to_all | solution.py:382

commit v4 on v3

--- a/solution.py
+++ b/solution.py
@@ -173,23 +173,14 @@
             field[target, stripe + 8 :, :SUBN] = mean_flux[:, own]
             field[target, stripe + 8 :, SUBN : 2 * SUBN] = spot_size[:, own]
 
-    waiting, parts = None, []
-
-    def advance():
-        frame, lines = waiting
-        parts.append(columns_of(lines))
-        if len(parts) == blocks:
-            finish(frame, parts)
-            parts.clear()
-
-    for frame in range(frames):
+    def lines_of(frame):
         for part in range(blocks):
             copy(frame, part).wait()
-            lines = dot(row_table, held[frame, :, pl.ds(part * span, span)])
-            if waiting is not None:
-                advance()
-            waiting = (frame, lines)
-    advance()
+        return [dot(row_table, held[frame, :, pl.ds(part * span, span)]) for part in range(blocks)]
+
+    lines = [lines_of(frame) for frame in range(frames)]
+    for frame in range(frames):
+        finish(frame, [columns_of(part) for part in lines[frame]])
 
 
 def rims_kernel(
@@ -263,10 +254,14 @@
 
 
 def phase_kernel(
-    sizes, received, spectrum, near, back_high, back_low, halo_high, halo_low, out_high, out_low, scale, coarse,
-    phase,
+    sizes, received, field, spectrum, near, back_high, back_low, halo_high, halo_low, out_high, out_low, scale,
+    coarse, phase, mean_flux, spot_size,
 ):
-    blocks, rows = sizes
+    stripe, pieces, blocks, rows = sizes
+    for piece in range(pieces):
+        where = slice(piece * stripe, (piece + 1) * stripe)
+        mean_flux[0, where, :] = field[piece, stripe + 8 :, :SUBN]
+        spot_size[0, where, :] = field[piece, stripe + 8 :, SUBN : 2 * SUBN]
     tiles = padded(blocks) // LANES
     mine = lax.axis_index("row")
     side = lax.axis_index("col")
@@ -386,21 +381,17 @@
     halo[:, 16:] = vectors[:, WIN - 8 :]
     halo_pair = constant_pair(halo)
     out_pair = constant_pair(vectors[MARGIN : MARGIN + SUBN])
-    phase = pl.pallas_call(
-        functools.partial(phase_kernel, (blocks, rows)),
-        out_shape=jax.ShapeDtypeStruct((1, SUBN, SUBN), F32),
-        in_specs=in_vmem(11),
-        out_specs=pl.BlockSpec(memory_space=pltpu.VMEM),
+    return pl.pallas_call(
+        functools.partial(phase_kernel, (stripe, pieces, blocks, rows)),
+        out_shape=(jax.ShapeDtypeStruct((1, SUBN, SUBN), F32),) * 3,
+        in_specs=in_vmem(12),
+        out_specs=tuple(in_vmem(3)),
         compiler_params=PARAMS,
         name="phase",
     )(
-        received, spectrum, near, *back_pair, *halo_pair, *out_pair, scale_wide,
+        received, field, spectrum, near, *back_pair, *halo_pair, *out_pair, scale_wide,
         jnp.asarray(coarse_table(rows, blocks, tail)),
     )
-    mean_flux = field[:, stripe + 8 :, :SUBN].reshape(1, SUBN, SUBN)
-    spot_size = field[:, stripe + 8 :, SUBN : 2 * SUBN].reshape(1, SUBN, SUBN)
-    return phase, mean_flux, spot_size
-
 
 def solution(mesh):
     placed = P(("groups", "sub"), "row", "col")

time: 28 us -> 26.9 us (0.961)
  blocking collectives: 10.4 us -> 20.9 us
  waiting for transfers between devices: 5.13 us -> 0 us
  starting transfers between devices: 4.88 us -> 0 us
  Pallas kernels: 5.77 us -> 4.81 us
  local copies, waits for them, and re-layouts: 0.77 us -> 0.11 us
    all_to_all x0 -> x1, blocking collectives: none -> 10.5 us  [body(): lax.all_to_all(sent, 'row', split_axis=0, concat_axis=0, tiled=True)]
    all_to_all x1 -> x0, waiting for transfers between devices: 5.13 us -> none  [body(): lax.all_to_all(sent, 'row', split_axis=0, concat_axis=0, tiled=True)]
    all_to_all x1 -> x0, starting transfers between devices: 4.88 us -> none  [body(): lax.all_to_all(sent, 'row', split_axis=0, concat_axis=0, tiled=True)]
    slice x1 -> x0, local copies, waits for them, and re-layouts: 0.66 us -> none  [body(): spot_size = field[:, stripe + 8:, SUBN:2 * SUBN].reshape(1, SUBN, SUBN)]
    pallas_call x1, Pallas kernels: 1.49 us -> 0.86 us  [body(): pl.pallas_call(functools.partial(rims_kernel, (stripe, pieces, blocks, ro...]
    pallas_call x1, Pallas kernels: 2.96 us -> 2.62 us  [body(): pl.pallas_call(functools.partial(moments_kernel, (frames, stripe, blocks,...]
  transfers between devices with their start and end apart: 1 -> 0, of which waited for: 1 -> 0; matrix products, arithmetic and copies ran while one was open for 2% -> 0% of each run, Pallas kernels for 0% -> 0%
where the time goes in v4:
time: 26.9 us; the launch traced here: 26.6 us
  blocking collectives  20.9 us (78%)
  Pallas kernels  4.81 us (18%)
  between operations  0.86 us (3%)
    all_to_all x1, blocking collectives, body(): lax.all_to_all(sent, 'row', split_axis=0, concat_axis=0, tiled=True)  10.5 us
    all_to_all x1, blocking collectives, body(): lax.all_to_all(field, ('col', 'sub'), split_axis=0, concat_axis=0, tiled=...  10.4 us
    pallas_call x1, Pallas kernels, body(): pl.pallas_call(functools.partial(moments_kernel, (frames, stripe, blocks,...  2.62 us
    pallas_call x1, Pallas kernels, body(): pl.pallas_call(functools.partial(phase_kernel, (stripe, pieces, blocks, r...  1.33 us
    pallas_call x1, Pallas kernels, body(): pl.pallas_call(functools.partial(rims_kernel, (stripe, pieces, blocks, ro...  0.86 us

profile of v4, /device:TPU:0, one launch (start us, length us, event | category | flops | bytes accessed | tf_op | source)
XLA Modules:
  0.0 26.6 jit_solution(9098047518982739082)
XLA Ops:
  0.6 0.0 copy-start
  0.6 0.0 copy-start.1
  0.7 0.0 copy-start.2
  0.7 0.0 copy-start.3
  0.7 0.0 copy-start.4
  0.7 0.0 copy-start.14
  0.7 0.0 copy-start.15
  0.7 0.0 copy-start.7
  0.7 0.0 copy-start.8
  0.7 0.0 copy-start.5
  0.8 0.0 copy-start.6
  0.8 0.0 copy-start.9
  0.8 0.0 copy-start.10
  0.8 0.0 copy-start.11
  0.8 0.0 copy-start.12
  0.8 0.0 copy-start.13
  0.8 2.6 %moments.1 = f32[4,72,256]{2,1,0:T(8,128)S(1)} custom-call(bf16[2,256,2048]{2,1,0:T(8,128)(2,1)} %pixels.1), custom_call_target="tpu_custom_call" | custom-call | tf_op jit(solution)/shard_map/moments/pallas_call | solution.py:336
  3.5 10.4 %all_to_all.10.field = f32[4,72,256]{2,1,0:T(8,128)S(1)} all-to-all(f32[4,72,256]{2,1,0:T(8,128)S(1)} %moments.1), channel_id=1, replica_groups=mesh['groups'=2,'row'=4,'col'=2,'sub'=2] {'col','sub'}, dimensions={0} | all-to-all | bytes 589824 | tf_op jit(solution)/shard_map/all_to_all | solution.py:349
  13.9 0.0 copy-done.3
  13.9 0.0 copy-done.4
  13.9 0.0 copy-done.14
  13.9 0.9 %rims.1 = (f32[4,40,128]{2,1,0:T(8,128)S(1)}, f32[144,384]{1,0:T(8,128)S(1)}, f32[16,128]{1,0:T(8,128)S(1)}) custom-call(f32[4,72,256]{2,1,0:T(8,128)S(1)} %all_to_all.10.field, bf16[256,384]{1,0:T(8,128)(2,1)S(1)} %copy-done.6, bf16[256,384]{1,0:T(8,128)(2,1)S(1)} %copy-done.5, bf16[2,384,128]{2,1,0:T(8,128)(2,1)S(1)} %copy-done.2, ...), custom_call_target="tpu_custom_call" | custom-call | tf_op jit(solution)/shard_map/rims/pallas_call | solution.py:364
  14.8 10.5 %all_to_all.11.received = f32[4,40,128]{2,1,0:T(8,128)S(1)} all-to-all(f32[4,40,128]{2,1,0:T(8,128)S(1)} %get-tuple-element.6), channel_id=1, replica_groups=mesh['groups'=2,'row'=4,'col'=2,'sub'=2] {'row'}, dimensions={0} | all-to-all | bytes 163840 | tf_op jit(solution)/shard_map/all_to_all | solution.py:377
  25.3 1.3 %phase.1 = (f32[1,128,128]{2,1,0:T(8,128)}, f32[1,128,128]{2,1,0:T(8,128)}, f32[1,128,128]{2,1,0:T(8,128)}) custom-call(f32[4,40,128]{2,1,0:T(8,128)S(1)} %all_to_all.11.received, f32[4,72,256]{2,1,0:T(8,128)S(1)} %all_to_all.10.field, f32[144,384]{1,0:T(8,128)S(1)} %get-tuple-element.7.spectrum, f32[16,128]{1,0:T(8,128)S(1)} %get-tuple-element.8.near, ...), custom_call_target="tpu_custom_call" | custom-call | tf_op jit(solution)/shard_map/phase/pallas_call | solution.py:384
  (13 shorter events, 0.0 us)
Async XLA Ops:
  0.6 13.2 %copy-start = (f32[144,384]{1,0:T(8,128)S(1)}, f32[144,384]{1,0:T(8,128)}, u32[]{:S(2)}) copy-start(f32[144,384]{1,0:T(8,128)} %constant.36.clone.scale) | copy-start | bytes 663556
  0.6 13.2 %copy-start.1 = (bf16[2,384,128]{2,1,0:T(8,128)(2,1)S(1)}, bf16[2,384,128]{2,1,0:T(8,128)(2,1)}, u32[]{:S(2)}) copy-start(bf16[2,384,128]{2,1,0:T(8,128)(2,1)} %constant.35.clone.back_low) | copy-start | bytes 589828
  0.7 13.2 %copy-start.2 = (bf16[2,384,128]{2,1,0:T(8,128)(2,1)S(1)}, bf16[2,384,128]{2,1,0:T(8,128)(2,1)}, u32[]{:S(2)}) copy-start(bf16[2,384,128]{2,1,0:T(8,128)(2,1)} %constant.34.clone.back_high) | copy-start | bytes 589828
  0.7 13.2 %copy-start.3 = (f32[9,16,384]{2,1,0:T(8,128)S(1)}, f32[9,16,384]{2,1,0:T(8,128)}, u32[]{:S(2)}) copy-start(f32[9,16,384]{2,1,0:T(8,128)} %constant.42.clone.below_table) | copy-start | bytes 663556
  0.7 13.2 %copy-start.4 = (f32[8,16,384]{2,1,0:T(8,128)S(1)}, f32[8,16,384]{2,1,0:T(8,128)}, u32[]{:S(2)}) copy-start(f32[8,16,384]{2,1,0:T(8,128)} %constant.41.clone.above_table) | copy-start | bytes 589828
  0.7 13.2 %copy-start.14 = (bf16[16,144]{1,0:T(8,128)(2,1)S(1)}, bf16[16,144]{1,0:T(8,128)(2,1)}, u32[]{:S(2)}) copy-start(bf16[16,144]{1,0:T(8,128)(2,1)} %constant.40.clone.edge_low) | copy-start | bytes 13828
  0.7 13.2 %copy-start.15 = (bf16[16,144]{1,0:T(8,128)(2,1)S(1)}, bf16[16,144]{1,0:T(8,128)(2,1)}, u32[]{:S(2)}) copy-start(bf16[16,144]{1,0:T(8,128)(2,1)} %constant.39.clone.edge_high) | copy-start | bytes 13828
  0.7 13.2 %copy-start.7 = (bf16[144,136]{1,0:T(8,128)(2,1)S(1)}, bf16[144,136]{1,0:T(8,128)(2,1)}, u32[]{:S(2)}) copy-start(bf16[144,136]{1,0:T(8,128)(2,1)} %constant.38.clone.drive_low) | copy-start | bytes 117508
  0.7 13.2 %copy-start.8 = (bf16[144,136]{1,0:T(8,128)(2,1)S(1)}, bf16[144,136]{1,0:T(8,128)(2,1)}, u32[]{:S(2)}) copy-start(bf16[144,136]{1,0:T(8,128)(2,1)} %constant.37.clone.drive_high) | copy-start | bytes 117508
  0.7 13.2 %copy-start.5 = (bf16[256,384]{1,0:T(8,128)(2,1)S(1)}, bf16[256,384]{1,0:T(8,128)(2,1)}, u32[]{:S(2)}) copy-start(bf16[256,384]{1,0:T(8,128)(2,1)} %constant.33.clone.basis_low) | copy-start | bytes 589828
  0.8 13.2 %copy-start.6 = (bf16[256,384]{1,0:T(8,128)(2,1)S(1)}, bf16[256,384]{1,0:T(8,128)(2,1)}, u32[]{:S(2)}) copy-start(bf16[256,384]{1,0:T(8,128)(2,1)} %constant.32.clone.basis_high) | copy-start | bytes 589828
  0.8 24.5 %copy-start.9 = (bf16[128,144]{1,0:T(8,128)(2,1)S(1)}, bf16[128,144]{1,0:T(8,128)(2,1)}, u32[]{:S(2)}) copy-start(bf16[128,144]{1,0:T(8,128)(2,1)} %constant.46.clone.out_low) | copy-start | bytes 110596
  0.8 24.5 %copy-start.10 = (bf16[128,144]{1,0:T(8,128)(2,1)S(1)}, bf16[128,144]{1,0:T(8,128)(2,1)}, u32[]{:S(2)}) copy-start(bf16[128,144]{1,0:T(8,128)(2,1)} %constant.45.clone.out_high) | copy-start | bytes 110596
  0.8 24.5 %copy-start.11 = (bf16[144,24]{1,0:T(8,128)(2,1)S(1)}, bf16[144,24]{1,0:T(8,128)(2,1)}, u32[]{:S(2)}) copy-start(bf16[144,24]{1,0:T(8,128)(2,1)} %constant.44.clone.halo_low) | copy-start | bytes 20740
  0.8 24.5 %copy-start.12 = (bf16[144,24]{1,0:T(8,128)(2,1)S(1)}, bf16[144,24]{1,0:T(8,128)(2,1)}, u32[]{:S(2)}) copy-start(bf16[144,24]{1,0:T(8,128)(2,1)} %constant.43.clone.halo_high) | copy-start | bytes 20740
  0.8 24.5 %copy-start.13 = (f32[4,8,128]{2,1,0:T(8,128)S(1)}, f32[4,8,128]{2,1,0:T(8,128)}, u32[]{:S(2)}) copy-start(f32[4,8,128]{2,1,0:T(8,128)} %constant.47.clone.coarse) | copy-start | bytes 49156

commit v5 on v4

--- a/solution.py
+++ b/solution.py
@@ -113,8 +113,37 @@
     return jnp.where(hit, power(offset_of(place), kind), 0.0).astype(BF16)
 
 
-def moments_kernel(sizes, pixels, field, held, arrived):
+def swapped(count):
+    return count <= 4 and count & (count - 1) == 0
+
+
+def exchange(pieces, axes, count):
+    if not swapped(count):
+        return [lax.all_to_all(pieces[0], axes, split_axis=0, concat_axis=0, tiled=True)]
+    return [pieces[0]] + [
+        lax.ppermute(pieces[k], axes, [(i, i ^ k) for i in range(count)]) for k in range(1, count)
+    ]
+
+
+def piece_shapes(count, shape):
+    if swapped(count):
+        return [jax.ShapeDtypeStruct(shape, F32)] * count
+    return [jax.ShapeDtypeStruct((count,) + shape, F32)]
+
+
+def pick(index, values):
+    total = values[-1]
+    for step in range(len(values) - 1):
+        total = jnp.where(index == step, values[step], total)
+    return total
+
+
+def moments_kernel(sizes, pixels, *refs):
     frames, stripe, blocks, cores, stripes = sizes
+    pieces = blocks * cores
+    slots = pieces if swapped(pieces) else 1
+    fields, extras = refs[:slots], refs[slots : 2 * slots]
+    held, arrived = refs[2 * slots :]
     width = blocks * SUBN
     places = LANES // GROUP
     span = LANES * PIX
@@ -128,7 +157,8 @@
             copy(frame, part).start()
     row_table = row_moments(stripe)
     col_tables = [column_moments(chunk) for chunk in range(places)]
-    position = (lax.axis_index("row") * blocks + lax.axis_index("col")) * cores + lax.axis_index("sub")
+    slot = lax.axis_index("col") * cores + lax.axis_index("sub")
+    position = lax.axis_index("row") * pieces + slot
     group = iota((stripe, LANES), 1) // GROUP
 
     def gather(pieces, kind):
@@ -165,13 +195,9 @@
         above = pltpu.roll(flow_y, 1, 0)
         source = left - flow_x + jnp.where(row > 0, above, 0.0) - flow_y
         spill = jnp.where(row[:8] == 0, above[:8], 0.0)
-        for block in range(blocks):
-            target = block * cores + frame
-            own = slice(block * SUBN, (block + 1) * SUBN)
-            field[target, :stripe, :] = source
-            field[target, stripe : stripe + 8, :] = spill
-            field[target, stripe + 8 :, :SUBN] = mean_flux[:, own]
-            field[target, stripe + 8 :, SUBN : 2 * SUBN] = spot_size[:, own]
+        fluxes = [mean_flux[:, block * SUBN : (block + 1) * SUBN] for block in range(blocks)]
+        spots = [spot_size[:, block * SUBN : (block + 1) * SUBN] for block in range(blocks)]
+        return source, spill, fluxes, spots
 
     def lines_of(frame):
         for part in range(blocks):
@@ -179,28 +205,51 @@
         return [dot(row_table, held[frame, :, pl.ds(part * span, span)]) for part in range(blocks)]
 
     lines = [lines_of(frame) for frame in range(frames)]
-    for frame in range(frames):
-        finish(frame, [columns_of(part) for part in lines[frame]])
-
-
-def rims_kernel(
-    sizes, field, basis_high, basis_low, back_high, back_low, drive_high, drive_low, edge_high, edge_low, scale,
-    above_table, below_table, sent, spectrum, near,
-):
-    stripe, pieces, blocks, rows = sizes
+    found = [finish(frame, [columns_of(part) for part in lines[frame]]) for frame in range(frames)]
+    for piece in range(pieces):
+        if slots > 1:
+            target = slot ^ piece
+            frame, block = target % cores, target // cores
+            source, spill = [pick(frame, [one[kind] for one in found]) for kind in range(2)]
+            flux, spot = [pick(frame, [pick(block, one[kind]) for one in found]) for kind in range(2, 4)]
+            field, extra = fields[piece], extras[piece]
+        else:
+            frame, block = piece % cores, piece // cores
+            source, spill, flux, spot = found[frame]
+            flux, spot = flux[block], spot[block]
+            field, extra = fields[0].at[piece], extras[0].at[piece]
+        field[:stripe, :] = source
+        field[stripe:, :] = spill
+        extra[:stripe, :] = flux
+        extra[stripe:, :] = spot
+
+
+def pieces_of(refs, slots, count, mine):
+    if slots > 1:
+        return [(mine ^ step, refs[step]) for step in range(count)]
+    return [(step, refs[0].at[step]) for step in range(count)]
+
+
+def rims_kernel(sizes, *refs):
+    stripe, pieces, blocks, cores, rows = sizes
+    slots = pieces if swapped(pieces) else 1
+    outs = rows if swapped(rows) else 1
+    fields, refs = refs[:slots], refs[slots:]
+    basis_high, basis_low, back_high, back_low, drive_high, drive_low, edge_high, edge_low = refs[:8]
+    scale, above_table, below_table = refs[8:11]
+    sent, near, lined = refs[11 : 11 + outs], refs[11 + outs + 1], refs[11 + outs + 2]
+    spectrum = refs[11 + outs]
     tiles = padded(blocks) // LANES
     mine = lax.axis_index("row")
     side = lax.axis_index("col")
-    parts = []
-    for piece in range(pieces):
-        block = field[piece, :stripe, :]
-        if piece:
-            head = block[:8] + field[piece - 1, stripe : stripe + 8, :]
-            block = head if stripe == 8 else jnp.concatenate([head, block[8:]], 0)
-        parts.append(block)
-    spill = field[pieces - 1, stripe : stripe + 8, :]
-    parts.append(spill)
-    source = jnp.concatenate(parts, 0)
+    arranged = pieces_of(fields, slots, pieces, side * cores + lax.axis_index("sub"))
+    lined[SUBN:, :] = jnp.zeros((8, lined.shape[1]), F32)
+    for place, field in arranged:
+        lined[pl.ds(pl.multiple_of(place * stripe, 8), stripe), :] = field[:stripe, :]
+    for place, field in arranged:
+        head = pl.ds(pl.multiple_of((place + 1) * stripe, 8), 8)
+        lined[head, :] = lined[head, :] + field[stripe:, :]
+    source = lined[...]
     across = dot_three(halves(source), (basis_high[...], basis_low[...]))
     driven = dot_three((drive_high[...], drive_low[...]), halves(across))
     response = driven * scale[...]
@@ -215,69 +264,67 @@
     near[:8, :] = jnp.where(mine > 0, rims[24:32], 0.0)
     near[8:, :] = jnp.where(mine < rows - 1, rims[32:40], 0.0)
     base = 8 * tiles
-    tail = sent.shape[1] - base - 8
+    tail = sent[0].shape[-2] - base - 8
     total = jnp.sum(source[:SUBN], 0, keepdims=True)
     place = iota((tail, LANES), 0)
     sums = jnp.zeros((tail, LANES), F32)
     for block in range(blocks):
         cut = slice(block * SUBN, (block + 1) * SUBN)
         sums = jnp.where(place == block, total[:, cut], sums)
-        sums = jnp.where(place == blocks + block, spill[:1, cut], sums)
+        sums = jnp.where(place == blocks + block, source[SUBN : SUBN + 1, cut], sums)
     for tile in range(tiles):
         cut = slice(tile * LANES, (tile + 1) * LANES)
         sums = jnp.where(place == 2 * blocks + tile, across[SUBN : SUBN + 1, cut], sums)
-    for target in range(rows):
-        sent[target, : base + 8, :] = jnp.zeros((base + 8, LANES), F32)
-        sent[target, base + 8 :, :] = sums
-
-    def put(target, rim, lines):
-        sent[target, base : base + 8, :] = rim
-        if lines is not None:
-            for tile in range(tiles):
-                sent[target, 8 * tile : 8 * tile + 8, :] = lines[:, tile * LANES : (tile + 1) * LANES]
-
-    @pl.when(mine >= 1)
-    def _():
-        put(mine - 1, rims[:8], across[:8])
-
-    @pl.when(mine >= 2)
-    def _():
-        put(mine - 2, rims[16:24], None)
-
-    @pl.when(mine + 1 < rows)
-    def _():
-        put(mine + 1, rims[8:16], across[SUBN - 8 : SUBN])
-
-    @pl.when(mine + 2 < rows)
-    def _():
-        put(mine + 2, rims[40:], None)
-
-
-def phase_kernel(
-    sizes, received, field, spectrum, near, back_high, back_low, halo_high, halo_low, out_high, out_low, scale,
-    coarse, phase, mean_flux, spot_size,
-):
-    stripe, pieces, blocks, rows = sizes
-    for piece in range(pieces):
-        where = slice(piece * stripe, (piece + 1) * stripe)
-        mean_flux[0, where, :] = field[piece, stripe + 8 :, :SUBN]
-        spot_size[0, where, :] = field[piece, stripe + 8 :, SUBN : 2 * SUBN]
+    for target, piece in pieces_of(sent, outs, rows, mine):
+        ahead = target - mine
+        rim = jnp.where(ahead == -1, rims[:8], 0.0)
+        rim = jnp.where(ahead == 1, rims[8:16], rim)
+        rim = jnp.where(ahead == -2, rims[16:24], rim)
+        rim = jnp.where(ahead == 2, rims[40:], rim)
+        for tile in range(tiles):
+            cut = slice(tile * LANES, (tile + 1) * LANES)
+            line = jnp.where(ahead == -1, across[:8, cut], across[SUBN - 8 : SUBN, cut])
+            piece[8 * tile : 8 * tile + 8, :] = line
+        piece[base : base + 8, :] = rim
+        piece[base + 8 :, :] = sums
+
+
+def phase_kernel(sizes, *refs):
+    stripe, pieces, blocks, cores, rows = sizes
+    slots = pieces if swapped(pieces) else 1
+    ins = rows if swapped(rows) else 1
+    received, extras, refs = refs[:ins], refs[ins : ins + slots], refs[ins + slots :]
+    spectrum, near, back_high, back_low, halo_high, halo_low, out_high, out_low, scale, coarse = refs[:10]
+    phase, mean_flux, spot_size = refs[10:]
     tiles = padded(blocks) // LANES
     mine = lax.axis_index("row")
     side = lax.axis_index("col")
+    for place, extra in pieces_of(extras, slots, pieces, side * cores + lax.axis_index("sub")):
+        where = pl.ds(pl.multiple_of(place * stripe, 8), stripe)
+        mean_flux[0, where, :] = extra[:stripe, :]
+        spot_size[0, where, :] = extra[stripe:, :]
     base = 8 * tiles
-    tail = received.shape[1] - base - 8
-    above = jnp.maximum(mine - 1, 0)
-    below = jnp.minimum(mine + 1, rows - 1)
-    has_above = mine > 0
-    has_below = mine < rows - 1
+    tail = received[0].shape[-2] - base - 8
+    arranged = pieces_of(received, ins, rows, mine)
+
+    def of_row(row, where):
+        if ins == 1:
+            inside = jnp.logical_and(row >= 0, row < rows)
+            return jnp.where(inside, received[0][jnp.clip(row, 0, rows - 1), where, :], 0.0)
+        total = jnp.zeros((where.stop - where.start, LANES), F32)
+        for origin, piece in arranged[1:]:
+            total = jnp.where(origin == row, piece[where, :], total)
+        return total
+
+    above = of_row(mine - 1, slice(0, received[0].shape[-2]))
+    below = of_row(mine + 1, slice(0, base + 8))
     first = iota((8, LANES), 0) == 0
     top, bottom, spilt = [], [], []
     for tile in range(tiles):
-        top.append(jnp.where(has_above, received[above, 8 * tile : 8 * tile + 8, :], 0.0))
-        bottom.append(jnp.where(has_below, received[below, 8 * tile : 8 * tile + 8, :], 0.0))
-        line = received[above, pl.ds(base + 8 + 2 * blocks + tile, 1), :]
-        spilt.append(jnp.where(jnp.logical_and(first, has_above), line, 0.0))
+        top.append(above[8 * tile : 8 * tile + 8])
+        bottom.append(below[8 * tile : 8 * tile + 8])
+        start = base + 8 + 2 * blocks + tile
+        spilt.append(jnp.where(first, above[start : start + 1], 0.0))
     across = jnp.concatenate(
         [jnp.concatenate(top, 1), jnp.concatenate(spilt, 1), jnp.concatenate(bottom, 1)], 0
     )
@@ -286,18 +333,15 @@
     reach = dot_three(halves(response), (back_high[side], back_low[side]))
     solved = dot_three((out_high[...], out_low[...]), halves(reach))
     weighted = jnp.zeros((tail, coarse.shape[2]), F32)
-    for origin in range(rows):
-        count = jnp.sum(received[origin, base + 8 :, :], 1, keepdims=True)
+    for origin, piece in arranged:
+        count = jnp.sum(piece[base + 8 :, :], 1, keepdims=True)
         weighted = weighted + count * coarse[origin]
     own = iota(weighted.shape, 1) == mine * blocks + side
     level = jnp.sum(jnp.where(own, weighted, 0.0), keepdims=True)
     solved = solved + level
-    head = near[:8, :] + jnp.where(has_above, received[above, base : base + 8, :], 0.0)
-    head = head + jnp.where(mine > 1, received[jnp.maximum(mine - 2, 0), base : base + 8, :], 0.0)
-    foot = near[8:, :] + jnp.where(has_below, received[below, base : base + 8, :], 0.0)
-    foot = foot + jnp.where(
-        mine < rows - 2, received[jnp.minimum(mine + 2, rows - 1), base : base + 8, :], 0.0
-    )
+    rim = slice(base, base + 8)
+    head = near[:8, :] + above[rim] + of_row(mine - 2, rim)
+    foot = near[8:, :] + below[rim] + of_row(mine + 2, rim)
     phase[0, :8, :] = solved[:8] + head
     phase[0, 8 : SUBN - 8, :] = solved[8 : SUBN - 8]
     phase[0, SUBN - 8 :, :] = solved[SUBN - 8 :] + foot
@@ -333,11 +377,13 @@
     pieces = blocks * cores
     assert frames == cores and width == blocks * SUBN and stripe * pieces == SUBN
 
-    field = pl.pallas_call(
+    field_shapes = piece_shapes(pieces, (stripe + 8, width))
+    extra_shapes = piece_shapes(pieces, (2 * stripe, SUBN))
+    made = pl.pallas_call(
         functools.partial(moments_kernel, (frames, stripe, blocks, cores, rows * pieces)),
-        out_shape=jax.ShapeDtypeStruct((pieces, 2 * stripe + 8, width), F32),
+        out_shape=field_shapes + extra_shapes,
         in_specs=[pl.BlockSpec(memory_space=pltpu.HBM)],
-        out_specs=pl.BlockSpec(memory_space=pltpu.VMEM),
+        out_specs=in_vmem(len(field_shapes + extra_shapes)),
         scratch_shapes=[
             pltpu.VMEM((frames, pixel_rows, pixel_cols), BF16),
             pltpu.SemaphoreType.DMA((frames, blocks)),
@@ -345,8 +391,8 @@
         compiler_params=PARAMS,
         name="moments",
     )(pltpu.with_memory_space_constraint(pixels, pltpu.HBM))
-
-    field = lax.all_to_all(field, ("col", "sub"), split_axis=0, concat_axis=0, tiled=True)
+    fields = exchange(made[: len(field_shapes)], ("col", "sub"), pieces)
+    extras = exchange(made[len(field_shapes) :], ("col", "sub"), pieces)
 
     vectors, scale = sine_basis()
     basis = column_basis(blocks)
@@ -361,20 +407,19 @@
     tail = -(-(2 * blocks + tiles) // 8) * 8
     height = 8 * tiles + 8 + tail
 
-    sent, spectrum, near = pl.pallas_call(
-        functools.partial(rims_kernel, (stripe, pieces, blocks, rows)),
-        out_shape=(
-            jax.ShapeDtypeStruct((rows, height, LANES), F32),
-            jax.ShapeDtypeStruct((WIN, full), F32),
-            jax.ShapeDtypeStruct((16, SUBN), F32),
-        ),
-        in_specs=in_vmem(12),
-        out_specs=tuple(in_vmem(3)),
+    row_shapes = piece_shapes(rows, (height, LANES))
+    sizes = (stripe, pieces, blocks, cores, rows)
+    *sent, spectrum, near = pl.pallas_call(
+        functools.partial(rims_kernel, sizes),
+        out_shape=row_shapes
+        + [jax.ShapeDtypeStruct((WIN, full), F32), jax.ShapeDtypeStruct((16, SUBN), F32)],
+        in_specs=in_vmem(len(fields) + 11),
+        out_specs=in_vmem(len(row_shapes) + 2),
+        scratch_shapes=[pltpu.VMEM((SUBN + 8, width), F32)],
         compiler_params=PARAMS,
         name="rims",
-    )(field, *basis_pair, *back_pair, *drive_pair, *edge_pair, scale_wide, *side_tables)
-
-    received = lax.all_to_all(sent, "row", split_axis=0, concat_axis=0, tiled=True)
+    )(*fields, *basis_pair, *back_pair, *drive_pair, *edge_pair, scale_wide, *side_tables)
+    received = exchange(sent, ("row",), rows)
 
     halo = np.zeros((WIN, 24))
     halo[:, :9] = vectors[:, :9]
@@ -382,16 +427,17 @@
     halo_pair = constant_pair(halo)
     out_pair = constant_pair(vectors[MARGIN : MARGIN + SUBN])
     return pl.pallas_call(
-        functools.partial(phase_kernel, (stripe, pieces, blocks, rows)),
-        out_shape=(jax.ShapeDtypeStruct((1, SUBN, SUBN), F32),) * 3,
-        in_specs=in_vmem(12),
-        out_specs=tuple(in_vmem(3)),
+        functools.partial(phase_kernel, sizes),
+        out_shape=[jax.ShapeDtypeStruct((1, SUBN, SUBN), F32)] * 3,
+        in_specs=in_vmem(len(received) + len(extras) + 10),
+        out_specs=in_vmem(3),
         compiler_params=PARAMS,
         name="phase",
     )(
-        received, field, spectrum, near, *back_pair, *halo_pair, *out_pair, scale_wide,
+        *received, *extras, spectrum, near, *back_pair, *halo_pair, *out_pair, scale_wide,
         jnp.asarray(coarse_table(rows, blocks, tail)),
     )
+
 
 def solution(mesh):
     placed = P(("groups", "sub"), "row", "col")

time: 26.9 us -> 22.4 us (0.83)
  blocking collectives: 20.9 us -> 0 us
  starting transfers between devices: 0 us -> 9.68 us
  waiting for transfers between devices: 0 us -> 6.73 us
    all_to_all x2 -> x0, blocking collectives: 20.9 us -> none  [the longest x1 10.5 us: body(): lax.all_to_all(sent, 'row', split_axis=0, concat_axis=0, tiled=True)]
    ppermute x0 -> x9, starting transfers between devices: none -> 9.68 us  [exchange(): lax.ppermute(pieces[k], axes, [(i, i ^ k) for i in range(count)])]
    ppermute x0 -> x9, waiting for transfers between devices: none -> 6.73 us  [exchange(): lax.ppermute(pieces[k], axes, [(i, i ^ k) for i in range(count)])]
  transfers between devices with their start and end apart: 0 -> 9, of which waited for: 0 -> 3; matrix products, arithmetic and copies ran while one was open for 0% -> 0% of each run, Pallas kernels for 0% -> 4%
where the time goes in v5:
time: 22.4 us; the launch traced here: 22.3 us
  starting transfers between devices  9.68 us (43%)
  waiting for transfers between devices  6.73 us (30%)
  Pallas kernels  4.88 us (22%)
  between operations  0.87 us (4%)
    ppermute x9, starting transfers between devices, exchange(): lax.ppermute(pieces[k], axes, [(i, i ^ k) for i in range(count)])  9.68 us
    ppermute x9, waiting for transfers between devices, exchange(): lax.ppermute(pieces[k], axes, [(i, i ^ k) for i in range(count)])  6.73 us
    pallas_call x1, Pallas kernels, body(): pl.pallas_call(functools.partial(moments_kernel, (frames, stripe, blocks,...  2.64 us
    pallas_call x1, Pallas kernels, body(): pl.pallas_call(functools.partial(phase_kernel, sizes), out_shape=[jax.Sha...  1.34 us
    pallas_call x1, Pallas kernels, body(): pl.pallas_call(functools.partial(rims_kernel, sizes), out_shape=row_shape...  0.9 us
  transfers between devices with their start and end apart: 9, of which 3 were waited for; matrix products, arithmetic and copies ran while one was open for 0% of the time, Pallas kernels for 4%

profile of v5, /device:TPU:0, one launch (start us, length us, event | category | flops | bytes accessed | tf_op | source)
XLA Modules:
  0.0 22.3 jit_solution(18089346924878886455)
XLA Ops:
  0.6 0.0 copy-start
  0.6 0.0 copy-start.1
  0.7 0.0 copy-start.2
  0.7 0.0 copy-start.4
  0.7 0.0 copy-start.14
  0.7 0.0 copy-start.15
  0.7 0.0 copy-start.7
  0.7 0.0 copy-start.5
  0.8 0.0 copy-start.6
  0.8 2.6 %moments.1 = (f32[40,256]{1,0:T(8,128)S(1)}, f32[40,256]{1,0:T(8,128)S(1)}, f32[40,256]{1,0:T(8,128)S(1)}, f32[40,256]{1,0:T(8,128)S(1)}, f32[64,128]{1,0:T(8,12...) custom-call(bf16[2,256,2048]{2,1,0:T(8,128)(2,1)} %pixels.1), custom_call_target="tpu_custom_call" | custom-call | tf_op jit(solution)/shard_map/moments/pallas_call | solution.py:382
  3.5 0.5 %collective-permute-start = (f32[40,256]{1,0:T(8,128)S(1)}, f32[40,256]{1,0:T(8,128)S(1)}, u32[]{:S(2)}, u32[]{:S(2)}) collective-permute-start(f32[40,256]{1,0:T(8,128)S(1)} %get-tuple-element.18), channel_id=1, source_target_pairs={{0,1},{1,0},{2,3},{3,2},{4,5},{5,4},{6,7},{7,6},{8,9},{9,8},{10,11... | collective-permute-start | bytes 122888 | tf_op jit(solution)/shard_map/ppermute | solution.py:124
  4.0 2.6 %collective-permute-start.1 = (f32[40,256]{1,0:T(8,128)S(1)}, f32[40,256]{1,0:T(8,128)S(1)}, u32[]{:S(2)}, u32[]{:S(2)}) collective-permute-start(f32[40,256]{1,0:T(8,128)S(1)} %get-tuple-element.19), channel_id=1, source_target_pairs={{0,2},{1,3},{2,0},{3,1},{4,6},{5,7},{6,4},{7,5},{8,10},{9,11},{10,... | collective-permute-start | bytes 122888 | tf_op jit(solution)/shard_map/ppermute | solution.py:124
  6.6 0.1 collective-permute-start.2
  6.6 0.1 collective-permute-start.6
  6.8 1.9 %collective-permute-start.7 = (f32[64,128]{1,0:T(8,128)S(1)}, f32[64,128]{1,0:T(8,128)S(1)}, u32[]{:S(2)}, u32[]{:S(2)}) collective-permute-start(f32[64,128]{1,0:T(8,128)S(1)} %get-tuple-element.27), channel_id=1, source_target_pairs={{0,2},{1,3},{2,0},{3,1},{4,6},{5,7},{6,4},{7,5},{8,10},{9,11},{10,... | collective-permute-start | bytes 98312 | tf_op jit(solution)/shard_map/ppermute | solution.py:124
  8.7 0.0 collective-permute-done.1.refs_2_
  8.7 1.4 %collective-permute-done.2.refs_3_ = f32[40,256]{1,0:T(8,128)S(1)} collective-permute-done((f32[40,256]{1,0:T(8,128)S(1)}, f32[40,256]{1,0:T(8,128)S(1)}, u32[]{:S(2)}, u32[]{:S(2)}) %collective-permute-start.2) | collective-permute-done | bytes 40992 | tf_op jit(solution)/shard_map/ppermute | solution.py:124
  10.2 0.9 %rims.1 = (f32[40,128]{1,0:T(8,128)S(1)}, f32[40,128]{1,0:T(8,128)S(1)}, f32[40,128]{1,0:T(8,128)S(1)}, f32[40,128]{1,0:T(8,128)S(1)}, f32[144,384]{1,0:T(8,128)S(1)}, /*index=5*/f32[16,128]{1,0:T(8,128)S(1)}) custom-call(f32[40,256]{1,0:T(8,128)S(1)} %get-tuple-element.17.refs_0_, f32[40,256]{1,0:T(8,128)S(1)} %collective-permute-done.refs_1_, ...), custom_call_target="tpu_custom_call" | custom-call | tf_op jit(solution)/shard_map/rims/pallas_call | solution.py:412
  11.1 1.6 %collective-permute-start.3 = (f32[40,128]{1,0:T(8,128)S(1)}, f32[40,128]{1,0:T(8,128)S(1)}, u32[]{:S(2)}, u32[]{:S(2)}) collective-permute-start(f32[40,128]{1,0:T(8,128)S(1)} %get-tuple-element.22), channel_id=1, source_target_pairs={{0,4},{4,0},{8,12},{12,8},{1,5},{5,1},{9,13},{13,9},{2,6},{6,2},{1... | collective-permute-start | bytes 61448 | tf_op jit(solution)/shard_map/ppermute | solution.py:124
  12.7 2.6 %collective-permute-start.4 = (f32[40,128]{1,0:T(8,128)S(1)}, f32[40,128]{1,0:T(8,128)S(1)}, u32[]{:S(2)}, u32[]{:S(2)}) collective-permute-start(f32[40,128]{1,0:T(8,128)S(1)} %get-tuple-element.23), channel_id=1, source_target_pairs={{0,8},{4,12},{8,0},{12,4},{1,9},{5,13},{9,1},{13,5},{2,10},{6,14},... | collective-permute-start | bytes 61448 | tf_op jit(solution)/shard_map/ppermute | solution.py:124
  15.3 0.2 %collective-permute-start.5 = (f32[40,128]{1,0:T(8,128)S(1)}, f32[40,128]{1,0:T(8,128)S(1)}, u32[]{:S(2)}, u32[]{:S(2)}) collective-permute-start(f32[40,128]{1,0:T(8,128)S(1)} %get-tuple-element.24), channel_id=1, source_target_pairs={{0,12},{4,8},{8,4},{12,0},{1,13},{5,9},{9,5},{13,1},{2,14},{6,10},... | collective-permute-start | bytes 61448 | tf_op jit(solution)/shard_map/ppermute | solution.py:124
  15.5 2.0 %collective-permute-done.4.refs_2_ = f32[40,128]{1,0:T(8,128)S(1)} collective-permute-done((f32[40,128]{1,0:T(8,128)S(1)}, f32[40,128]{1,0:T(8,128)S(1)}, u32[]{:S(2)}, u32[]{:S(2)}) %collective-permute-start.4) | collective-permute-done | bytes 20512 | tf_op jit(solution)/shard_map/ppermute | solution.py:124
  17.5 3.4 %collective-permute-done.5.refs_3_ = f32[40,128]{1,0:T(8,128)S(1)} collective-permute-done((f32[40,128]{1,0:T(8,128)S(1)}, f32[40,128]{1,0:T(8,128)S(1)}, u32[]{:S(2)}, u32[]{:S(2)}) %collective-permute-start.5) | collective-permute-done | bytes 20512 | tf_op jit(solution)/shard_map/ppermute | solution.py:124
  20.9 1.3 %phase.1 = (f32[1,128,128]{2,1,0:T(8,128)}, f32[1,128,128]{2,1,0:T(8,128)}, f32[1,128,128]{2,1,0:T(8,128)}) custom-call(f32[40,128]{1,0:T(8,128)S(1)} %get-tuple-element.21.refs_0_, f32[40,128]{1,0:T(8,128)S(1)} %collective-permute-done.3.refs_1_, f32[40,128]{1,0:T(8,128)S(1)} %collective-permute-done.4.refs_2_, ...), custom_call_target="tpu_custom_call" | custom-call | tf_op jit(solution)/shard_map/phase/pallas_call | solution.py:429
  (29 shorter events, 0.1 us)
Async XLA Ops:
  0.6 9.5 %copy-start = (f32[144,384]{1,0:T(8,128)S(1)}, f32[144,384]{1,0:T(8,128)}, u32[]{:S(2)}) copy-start(f32[144,384]{1,0:T(8,128)} %constant.36.clone.refs_12_.refs_16_) | copy-start | bytes 663556
  0.6 9.4 %copy-start.1 = (bf16[2,384,128]{2,1,0:T(8,128)(2,1)S(1)}, bf16[2,384,128]{2,1,0:T(8,128)(2,1)}, u32[]{:S(2)}) copy-start(bf16[2,384,128]{2,1,0:T(8,128)(2,1)} %constant.35.clone.refs_7_.refs_11_) | copy-start | bytes 589828
  0.7 9.4 %copy-start.2 = (bf16[2,384,128]{2,1,0:T(8,128)(2,1)S(1)}, bf16[2,384,128]{2,1,0:T(8,128)(2,1)}, u32[]{:S(2)}) copy-start(bf16[2,384,128]{2,1,0:T(8,128)(2,1)} %constant.34.clone.refs_6_.refs_10_) | copy-start | bytes 589828
  0.7 9.4 %copy-start.3 = (f32[9,16,384]{2,1,0:T(8,128)S(1)}, f32[9,16,384]{2,1,0:T(8,128)}, u32[]{:S(2)}) copy-start(f32[9,16,384]{2,1,0:T(8,128)} %constant.42.clone.refs_14_) | copy-start | bytes 663556
  0.7 9.4 %copy-start.4 = (f32[8,16,384]{2,1,0:T(8,128)S(1)}, f32[8,16,384]{2,1,0:T(8,128)}, u32[]{:S(2)}) copy-start(f32[8,16,384]{2,1,0:T(8,128)} %constant.41.clone.refs_13_) | copy-start | bytes 589828
  0.7 9.4 %copy-start.14 = (bf16[16,144]{1,0:T(8,128)(2,1)S(1)}, bf16[16,144]{1,0:T(8,128)(2,1)}, u32[]{:S(2)}) copy-start(bf16[16,144]{1,0:T(8,128)(2,1)} %constant.40.clone.refs_11_) | copy-start | bytes 13828
  0.7 9.4 %copy-start.15 = (bf16[16,144]{1,0:T(8,128)(2,1)S(1)}, bf16[16,144]{1,0:T(8,128)(2,1)}, u32[]{:S(2)}) copy-start(bf16[16,144]{1,0:T(8,128)(2,1)} %constant.39.clone.refs_10_) | copy-start | bytes 13828
  0.7 9.4 %copy-start.7 = (bf16[144,136]{1,0:T(8,128)(2,1)S(1)}, bf16[144,136]{1,0:T(8,128)(2,1)}, u32[]{:S(2)}) copy-start(bf16[144,136]{1,0:T(8,128)(2,1)} %constant.38.clone.refs_9_) | copy-start | bytes 117508
  0.7 9.4 %copy-start.8 = (bf16[144,136]{1,0:T(8,128)(2,1)S(1)}, bf16[144,136]{1,0:T(8,128)(2,1)}, u32[]{:S(2)}) copy-start(bf16[144,136]{1,0:T(8,128)(2,1)} %constant.37.clone.refs_8_) | copy-start | bytes 117508
  0.7 9.4 %copy-start.5 = (bf16[256,384]{1,0:T(8,128)(2,1)S(1)}, bf16[256,384]{1,0:T(8,128)(2,1)}, u32[]{:S(2)}) copy-start(bf16[256,384]{1,0:T(8,128)(2,1)} %constant.33.clone.refs_5_) | copy-start | bytes 589828
  0.8 20.1 %copy-start.13 = (f32[4,8,128]{2,1,0:T(8,128)S(1)}, f32[4,8,128]{2,1,0:T(8,128)}, u32[]{:S(2)}) copy-start(f32[4,8,128]{2,1,0:T(8,128)} %constant.47.clone.refs_17_) | copy-start | bytes 49156
  0.8 20.1 %copy-start.9 = (bf16[128,144]{1,0:T(8,128)(2,1)S(1)}, bf16[128,144]{1,0:T(8,128)(2,1)}, u32[]{:S(2)}) copy-start(bf16[128,144]{1,0:T(8,128)(2,1)} %constant.46.clone.refs_15_) | copy-start | bytes 110596
  0.8 20.1 %copy-start.10 = (bf16[128,144]{1,0:T(8,128)(2,1)S(1)}, bf16[128,144]{1,0:T(8,128)(2,1)}, u32[]{:S(2)}) copy-start(bf16[128,144]{1,0:T(8,128)(2,1)} %constant.45.clone.refs_14_) | copy-start | bytes 110596
  0.8 20.1 %copy-start.11 = (bf16[144,24]{1,0:T(8,128)(2,1)S(1)}, bf16[144,24]{1,0:T(8,128)(2,1)}, u32[]{:S(2)}) copy-start(bf16[144,24]{1,0:T(8,128)(2,1)} %constant.44.clone.refs_13_) | copy-start | bytes 20740
  0.8 20.1 %copy-start.12 = (bf16[144,24]{1,0:T(8,128)(2,1)S(1)}, bf16[144,24]{1,0:T(8,128)(2,1)}, u32[]{:S(2)}) copy-start(bf16[144,24]{1,0:T(8,128)(2,1)} %constant.43.clone.refs_12_) | copy-start | bytes 20740
  3.5 5.2 %collective-permute-start = (f32[40,256]{1,0:T(8,128)S(1)}, f32[40,256]{1,0:T(8,128)S(1)}, u32[]{:S(2)}, u32[]{:S(2)}) collective-permute-start(f32[40,256]{1,0:T(8,128)S(1)} %get-tuple-element.18), channel_id=1, source_target_pairs={{0,1},{1,0},{2,3},{3,2},{4,5},{5,4},{6,7},{7,6},{8,9},{9,8},{10,11... | collective-permute-start | bytes 122888 | tf_op jit(solution)/shard_map/ppermute | solution.py:124
  4.0 4.7 %collective-permute-start.1 = (f32[40,256]{1,0:T(8,128)S(1)}, f32[40,256]{1,0:T(8,128)S(1)}, u32[]{:S(2)}, u32[]{:S(2)}) collective-permute-start(f32[40,256]{1,0:T(8,128)S(1)} %get-tuple-element.19), channel_id=1, source_target_pairs={{0,2},{1,3},{2,0},{3,1},{4,6},{5,7},{6,4},{7,5},{8,10},{9,11},{10,... | collective-permute-start | bytes 122888 | tf_op jit(solution)/shard_map/ppermute | solution.py:124
  6.6 3.5 %collective-permute-start.2 = (f32[40,256]{1,0:T(8,128)S(1)}, f32[40,256]{1,0:T(8,128)S(1)}, u32[]{:S(2)}, u32[]{:S(2)}) collective-permute-start(f32[40,256]{1,0:T(8,128)S(1)} %get-tuple-element.20), channel_id=1, source_target_pairs={{0,3},{1,2},{2,1},{3,0},{4,7},{5,6},{6,5},{7,4},{8,11},{9,10},{10,... | collective-permute-start | bytes 122888 | tf_op jit(solution)/shard_map/ppermute | solution.py:124
  6.6 8.7 %collective-permute-start.6 = (f32[64,128]{1,0:T(8,128)S(1)}, f32[64,128]{1,0:T(8,128)S(1)}, u32[]{:S(2)}, u32[]{:S(2)}) collective-permute-start(f32[64,128]{1,0:T(8,128)S(1)} %get-tuple-element.26), channel_id=1, source_target_pairs={{0,1},{1,0},{2,3},{3,2},{4,5},{5,4},{6,7},{7,6},{8,9},{9,8},{10,11... | collective-permute-start | bytes 98312 | tf_op jit(solution)/shard_map/ppermute | solution.py:124
  6.8 8.8 %collective-permute-start.7 = (f32[64,128]{1,0:T(8,128)S(1)}, f32[64,128]{1,0:T(8,128)S(1)}, u32[]{:S(2)}, u32[]{:S(2)}) collective-permute-start(f32[64,128]{1,0:T(8,128)S(1)} %get-tuple-element.27), channel_id=1, source_target_pairs={{0,2},{1,3},{2,0},{3,1},{4,6},{5,7},{6,4},{7,5},{8,10},{9,11},{10,... | collective-permute-start | bytes 98312 | tf_op jit(solution)/shard_map/ppermute | solution.py:124
  8.7 6.8 %collective-permute-start.8 = (f32[64,128]{1,0:T(8,128)S(1)}, f32[64,128]{1,0:T(8,128)S(1)}, u32[]{:S(2)}, u32[]{:S(2)}) collective-permute-start(f32[64,128]{1,0:T(8,128)S(1)} %get-tuple-element.28), channel_id=1, source_target_pairs={{0,3},{1,2},{2,1},{3,0},{4,7},{5,6},{6,5},{7,4},{8,11},{9,10},{10,... | collective-permute-start | bytes 98312 | tf_op jit(solution)/shard_map/ppermute | solution.py:124
  11.1 4.5 %collective-permute-start.3 = (f32[40,128]{1,0:T(8,128)S(1)}, f32[40,128]{1,0:T(8,128)S(1)}, u32[]{:S(2)}, u32[]{:S(2)}) collective-permute-start(f32[40,128]{1,0:T(8,128)S(1)} %get-tuple-element.22), channel_id=1, source_target_pairs={{0,4},{4,0},{8,12},{12,8},{1,5},{5,1},{9,13},{13,9},{2,6},{6,2},{1... | collective-permute-start | bytes 61448 | tf_op jit(solution)/shard_map/ppermute | solution.py:124
  12.7 4.8 %collective-permute-start.4 = (f32[40,128]{1,0:T(8,128)S(1)}, f32[40,128]{1,0:T(8,128)S(1)}, u32[]{:S(2)}, u32[]{:S(2)}) collective-permute-start(f32[40,128]{1,0:T(8,128)S(1)} %get-tuple-element.23), channel_id=1, source_target_pairs={{0,8},{4,12},{8,0},{12,4},{1,9},{5,13},{9,1},{13,5},{2,10},{6,14},... | collective-permute-start | bytes 61448 | tf_op jit(solution)/shard_map/ppermute | solution.py:124
  15.3 5.6 %collective-permute-start.5 = (f32[40,128]{1,0:T(8,128)S(1)}, f32[40,128]{1,0:T(8,128)S(1)}, u32[]{:S(2)}, u32[]{:S(2)}) collective-permute-start(f32[40,128]{1,0:T(8,128)S(1)} %get-tuple-element.24), channel_id=1, source_target_pairs={{0,12},{4,8},{8,4},{12,0},{1,13},{5,9},{9,5},{13,1},{2,14},{6,10},... | collective-permute-start | bytes 61448 | tf_op jit(solution)/shard_map/ppermute | solution.py:124
  (1 other events, 9.4 us)

commit v6 on v5

--- a/solution.py
+++ b/solution.py
@@ -113,15 +113,18 @@
     return jnp.where(hit, power(offset_of(place), kind), 0.0).astype(BF16)
 
 
+ORDER = {1: (), 2: (1,), 4: (2, 3, 1)}
+
+
 def swapped(count):
-    return count <= 4 and count & (count - 1) == 0
+    return count in ORDER
 
 
 def exchange(pieces, axes, count):
     if not swapped(count):
         return [lax.all_to_all(pieces[0], axes, split_axis=0, concat_axis=0, tiled=True)]
     return [pieces[0]] + [
-        lax.ppermute(pieces[k], axes, [(i, i ^ k) for i in range(count)]) for k in range(1, count)
+        lax.ppermute(pieces[k], axes, [(i, i ^ k) for i in range(count)]) for k in ORDER[count]
     ]
 
 
@@ -224,9 +227,9 @@
         extra[stripe:, :] = spot
 
 
-def pieces_of(refs, slots, count, mine):
+def pieces_of(refs, slots, count, mine, order):
     if slots > 1:
-        return [(mine ^ step, refs[step]) for step in range(count)]
+        return [(mine ^ step, ref) for step, ref in zip((0,) + tuple(order), refs)]
     return [(step, refs[0].at[step]) for step in range(count)]
 
 
@@ -242,7 +245,8 @@
     tiles = padded(blocks) // LANES
     mine = lax.axis_index("row")
     side = lax.axis_index("col")
-    arranged = pieces_of(fields, slots, pieces, side * cores + lax.axis_index("sub"))
+    slot = side * cores + lax.axis_index("sub")
+    arranged = pieces_of(fields, slots, pieces, slot, ORDER.get(pieces))
     lined[SUBN:, :] = jnp.zeros((8, lined.shape[1]), F32)
     for place, field in arranged:
         lined[pl.ds(pl.multiple_of(place * stripe, 8), stripe), :] = field[:stripe, :]
@@ -275,7 +279,7 @@
     for tile in range(tiles):
         cut = slice(tile * LANES, (tile + 1) * LANES)
         sums = jnp.where(place == 2 * blocks + tile, across[SUBN : SUBN + 1, cut], sums)
-    for target, piece in pieces_of(sent, outs, rows, mine):
+    for target, piece in pieces_of(sent, outs, rows, mine, range(1, rows)):
         ahead = target - mine
         rim = jnp.where(ahead == -1, rims[:8], 0.0)
         rim = jnp.where(ahead == 1, rims[8:16], rim)
@@ -299,13 +303,14 @@
     tiles = padded(blocks) // LANES
     mine = lax.axis_index("row")
     side = lax.axis_index("col")
-    for place, extra in pieces_of(extras, slots, pieces, side * cores + lax.axis_index("sub")):
+    slot = side * cores + lax.axis_index("sub")
+    for place, extra in pieces_of(extras, slots, pieces, slot, ORDER.get(pieces)):
         where = pl.ds(pl.multiple_of(place * stripe, 8), stripe)
         mean_flux[0, where, :] = extra[:stripe, :]
         spot_size[0, where, :] = extra[stripe:, :]
     base = 8 * tiles
     tail = received[0].shape[-2] - base - 8
-    arranged = pieces_of(received, ins, rows, mine)
+    arranged = pieces_of(received, ins, rows, mine, ORDER.get(rows))
 
     def of_row(row, where):
         if ins == 1:

time: 22.4 us -> 20.9 us (0.933)
  waiting for transfers between devices: 6.73 us -> 5.27 us
    ppermute x9, waiting for transfers between devices: 6.73 us -> 5.27 us  [exchange(): lax.ppermute(pieces[k], axes, [(i, i ^ k) for i in range(count)])]
where the time goes in v6:
time: 20.9 us; the launch traced here: 20.7 us
  starting transfers between devices  9.56 us (46%)
  waiting for transfers between devices  5.27 us (25%)
  Pallas kernels  4.88 us (23%)
  between operations  0.88 us (4%)
    ppermute x9, starting transfers between devices, exchange(): lax.ppermute(pieces[k], axes, [(i, i ^ k) for i in range(count)])  9.56 us
    ppermute x9, waiting for transfers between devices, exchange(): lax.ppermute(pieces[k], axes, [(i, i ^ k) for i in range(count)])  5.27 us
    pallas_call x1, Pallas kernels, body(): pl.pallas_call(functools.partial(moments_kernel, (frames, stripe, blocks,...  2.64 us
    pallas_call x1, Pallas kernels, body(): pl.pallas_call(functools.partial(phase_kernel, sizes), out_shape=[jax.Sha...  1.34 us
    pallas_call x1, Pallas kernels, body(): pl.pallas_call(functools.partial(rims_kernel, sizes), out_shape=row_shape...  0.91 us
  transfers between devices with their start and end apart: 9, of which 3 were waited for; matrix products, arithmetic and copies ran while one was open for 0% of the time, Pallas kernels for 4%

profile of v6, /device:TPU:0, one launch (start us, length us, event | category | flops | bytes accessed | tf_op | source)
XLA Modules:
  0.0 20.7 jit_solution(15002440411866220076)
XLA Ops:
  0.6 0.0 copy-start
  0.6 0.0 copy-start.1
  0.7 0.0 copy-start.2
  0.7 0.0 copy-start.3
  0.7 0.0 copy-start.14
  0.7 0.0 copy-start.15
  0.7 0.0 copy-start.7
  0.7 0.0 copy-start.8
  0.8 0.0 copy-start.6
  0.8 0.0 copy-start.13
  0.8 0.0 copy-start.9
  0.8 2.6 %moments.1 = (f32[40,256]{1,0:T(8,128)S(1)}, f32[40,256]{1,0:T(8,128)S(1)}, f32[40,256]{1,0:T(8,128)S(1)}, f32[40,256]{1,0:T(8,128)S(1)}, f32[64,128]{1,0:T(8,12...) custom-call(bf16[2,256,2048]{2,1,0:T(8,128)(2,1)} %pixels.1), custom_call_target="tpu_custom_call" | custom-call | tf_op jit(solution)/shard_map/moments/pallas_call | solution.py:387
  3.5 3.0 %collective-permute-start = (f32[40,256]{1,0:T(8,128)S(1)}, f32[40,256]{1,0:T(8,128)S(1)}, u32[]{:S(2)}, u32[]{:S(2)}) collective-permute-start(f32[40,256]{1,0:T(8,128)S(1)} %get-tuple-element.18), channel_id=1, source_target_pairs={{0,2},{1,3},{2,0},{3,1},{4,6},{5,7},{6,4},{7,5},{8,10},{9,11},{10,... | collective-permute-start | bytes 122888 | tf_op jit(solution)/shard_map/ppermute | solution.py:127
  6.5 0.2 collective-permute-start.2
  6.7 1.9 %collective-permute-start.6 = (f32[64,128]{1,0:T(8,128)S(1)}, f32[64,128]{1,0:T(8,128)S(1)}, u32[]{:S(2)}, u32[]{:S(2)}) collective-permute-start(f32[64,128]{1,0:T(8,128)S(1)} %get-tuple-element.26), channel_id=1, source_target_pairs={{0,2},{1,3},{2,0},{3,1},{4,6},{5,7},{6,4},{7,5},{8,10},{9,11},{10,... | collective-permute-start | bytes 98312 | tf_op jit(solution)/shard_map/ppermute | solution.py:127
  8.6 0.2 collective-permute-start.8
  8.8 1.3 %collective-permute-done.1.refs_2_ = f32[40,256]{1,0:T(8,128)S(1)} collective-permute-done((f32[40,256]{1,0:T(8,128)S(1)}, f32[40,256]{1,0:T(8,128)S(1)}, u32[]{:S(2)}, u32[]{:S(2)}) %collective-permute-start.1) | collective-permute-done | bytes 40992 | tf_op jit(solution)/shard_map/ppermute | solution.py:127
  10.2 0.9 %rims.1 = (f32[40,128]{1,0:T(8,128)S(1)}, f32[40,128]{1,0:T(8,128)S(1)}, f32[40,128]{1,0:T(8,128)S(1)}, f32[40,128]{1,0:T(8,128)S(1)}, f32[144,384]{1,0:T(8,128)S(1)}, /*index=5*/f32[16,128]{1,0:T(8,128)S(1)}) custom-call(f32[40,256]{1,0:T(8,128)S(1)} %get-tuple-element.17.refs_0_, f32[40,256]{1,0:T(8,128)S(1)} %collective-permute-done.refs_1_, ...), custom_call_target="tpu_custom_call" | custom-call | tf_op jit(solution)/shard_map/rims/pallas_call | solution.py:417
  11.1 2.6 %collective-permute-start.3 = (f32[40,128]{1,0:T(8,128)S(1)}, f32[40,128]{1,0:T(8,128)S(1)}, u32[]{:S(2)}, u32[]{:S(2)}) collective-permute-start(f32[40,128]{1,0:T(8,128)S(1)} %get-tuple-element.22), channel_id=1, source_target_pairs={{0,8},{4,12},{8,0},{12,4},{1,9},{5,13},{9,1},{13,5},{2,10},{6,14},... | collective-permute-start | bytes 61448 | tf_op jit(solution)/shard_map/ppermute | solution.py:127
  13.7 1.3 %collective-permute-start.4 = (f32[40,128]{1,0:T(8,128)S(1)}, f32[40,128]{1,0:T(8,128)S(1)}, u32[]{:S(2)}, u32[]{:S(2)}) collective-permute-start(f32[40,128]{1,0:T(8,128)S(1)} %get-tuple-element.23), channel_id=1, source_target_pairs={{0,12},{4,8},{8,4},{12,0},{1,13},{5,9},{9,5},{13,1},{2,14},{6,10},... | collective-permute-start | bytes 61448 | tf_op jit(solution)/shard_map/ppermute | solution.py:127
  15.1 0.2 %collective-permute-start.5 = (f32[40,128]{1,0:T(8,128)S(1)}, f32[40,128]{1,0:T(8,128)S(1)}, u32[]{:S(2)}, u32[]{:S(2)}) collective-permute-start(f32[40,128]{1,0:T(8,128)S(1)} %get-tuple-element.24), channel_id=1, source_target_pairs={{0,4},{4,0},{8,12},{12,8},{1,5},{5,1},{9,13},{13,9},{2,6},{6,2},{1... | collective-permute-start | bytes 61448 | tf_op jit(solution)/shard_map/ppermute | solution.py:127
  15.3 0.6 %collective-permute-done.3.refs_1_ = f32[40,128]{1,0:T(8,128)S(1)} collective-permute-done((f32[40,128]{1,0:T(8,128)S(1)}, f32[40,128]{1,0:T(8,128)S(1)}, u32[]{:S(2)}, u32[]{:S(2)}) %collective-permute-start.3) | collective-permute-done | bytes 20512 | tf_op jit(solution)/shard_map/ppermute | solution.py:127
  16.0 3.4 %collective-permute-done.4.refs_2_ = f32[40,128]{1,0:T(8,128)S(1)} collective-permute-done((f32[40,128]{1,0:T(8,128)S(1)}, f32[40,128]{1,0:T(8,128)S(1)}, u32[]{:S(2)}, u32[]{:S(2)}) %collective-permute-start.4) | collective-permute-done | bytes 20512 | tf_op jit(solution)/shard_map/ppermute | solution.py:127
  19.4 1.3 %phase.1 = (f32[1,128,128]{2,1,0:T(8,128)}, f32[1,128,128]{2,1,0:T(8,128)}, f32[1,128,128]{2,1,0:T(8,128)}) custom-call(f32[40,128]{1,0:T(8,128)S(1)} %get-tuple-element.21.refs_0_, f32[40,128]{1,0:T(8,128)S(1)} %collective-permute-done.3.refs_1_, f32[40,128]{1,0:T(8,128)S(1)} %collective-permute-done.4.refs_2_, ...), custom_call_target="tpu_custom_call" | custom-call | tf_op jit(solution)/shard_map/phase/pallas_call | solution.py:434
  (29 shorter events, 0.1 us)
Async XLA Ops:
  0.6 9.5 %copy-start = (f32[144,384]{1,0:T(8,128)S(1)}, f32[144,384]{1,0:T(8,128)}, u32[]{:S(2)}) copy-start(f32[144,384]{1,0:T(8,128)} %constant.36.clone.refs_12_.refs_16_) | copy-start | bytes 663556
  0.6 9.4 %copy-start.1 = (bf16[2,384,128]{2,1,0:T(8,128)(2,1)S(1)}, bf16[2,384,128]{2,1,0:T(8,128)(2,1)}, u32[]{:S(2)}) copy-start(bf16[2,384,128]{2,1,0:T(8,128)(2,1)} %constant.35.clone.refs_7_.refs_11_) | copy-start | bytes 589828
  0.7 9.4 %copy-start.2 = (bf16[2,384,128]{2,1,0:T(8,128)(2,1)S(1)}, bf16[2,384,128]{2,1,0:T(8,128)(2,1)}, u32[]{:S(2)}) copy-start(bf16[2,384,128]{2,1,0:T(8,128)(2,1)} %constant.34.clone.refs_6_.refs_10_) | copy-start | bytes 589828
  0.7 9.4 %copy-start.3 = (f32[9,16,384]{2,1,0:T(8,128)S(1)}, f32[9,16,384]{2,1,0:T(8,128)}, u32[]{:S(2)}) copy-start(f32[9,16,384]{2,1,0:T(8,128)} %constant.42.clone.refs_14_) | copy-start | bytes 663556
  0.7 9.4 %copy-start.4 = (f32[8,16,384]{2,1,0:T(8,128)S(1)}, f32[8,16,384]{2,1,0:T(8,128)}, u32[]{:S(2)}) copy-start(f32[8,16,384]{2,1,0:T(8,128)} %constant.41.clone.refs_13_) | copy-start | bytes 589828
  0.7 9.4 %copy-start.14 = (bf16[16,144]{1,0:T(8,128)(2,1)S(1)}, bf16[16,144]{1,0:T(8,128)(2,1)}, u32[]{:S(2)}) copy-start(bf16[16,144]{1,0:T(8,128)(2,1)} %constant.40.clone.refs_11_) | copy-start | bytes 13828
  0.7 9.4 %copy-start.15 = (bf16[16,144]{1,0:T(8,128)(2,1)S(1)}, bf16[16,144]{1,0:T(8,128)(2,1)}, u32[]{:S(2)}) copy-start(bf16[16,144]{1,0:T(8,128)(2,1)} %constant.39.clone.refs_10_) | copy-start | bytes 13828
  0.7 9.4 %copy-start.7 = (bf16[144,136]{1,0:T(8,128)(2,1)S(1)}, bf16[144,136]{1,0:T(8,128)(2,1)}, u32[]{:S(2)}) copy-start(bf16[144,136]{1,0:T(8,128)(2,1)} %constant.38.clone.refs_9_) | copy-start | bytes 117508
  0.7 9.4 %copy-start.8 = (bf16[144,136]{1,0:T(8,128)(2,1)S(1)}, bf16[144,136]{1,0:T(8,128)(2,1)}, u32[]{:S(2)}) copy-start(bf16[144,136]{1,0:T(8,128)(2,1)} %constant.37.clone.refs_8_) | copy-start | bytes 117508
  0.7 9.4 %copy-start.5 = (bf16[256,384]{1,0:T(8,128)(2,1)S(1)}, bf16[256,384]{1,0:T(8,128)(2,1)}, u32[]{:S(2)}) copy-start(bf16[256,384]{1,0:T(8,128)(2,1)} %constant.33.clone.refs_5_) | copy-start | bytes 589828
  0.8 18.6 %copy-start.13 = (f32[4,8,128]{2,1,0:T(8,128)S(1)}, f32[4,8,128]{2,1,0:T(8,128)}, u32[]{:S(2)}) copy-start(f32[4,8,128]{2,1,0:T(8,128)} %constant.47.clone.refs_17_) | copy-start | bytes 49156
  0.8 18.6 %copy-start.9 = (bf16[128,144]{1,0:T(8,128)(2,1)S(1)}, bf16[128,144]{1,0:T(8,128)(2,1)}, u32[]{:S(2)}) copy-start(bf16[128,144]{1,0:T(8,128)(2,1)} %constant.46.clone.refs_15_) | copy-start | bytes 110596
  0.8 18.5 %copy-start.10 = (bf16[128,144]{1,0:T(8,128)(2,1)S(1)}, bf16[128,144]{1,0:T(8,128)(2,1)}, u32[]{:S(2)}) copy-start(bf16[128,144]{1,0:T(8,128)(2,1)} %constant.45.clone.refs_14_) | copy-start | bytes 110596
  0.8 18.5 %copy-start.11 = (bf16[144,24]{1,0:T(8,128)(2,1)S(1)}, bf16[144,24]{1,0:T(8,128)(2,1)}, u32[]{:S(2)}) copy-start(bf16[144,24]{1,0:T(8,128)(2,1)} %constant.44.clone.refs_13_) | copy-start | bytes 20740
  0.8 18.5 %copy-start.12 = (bf16[144,24]{1,0:T(8,128)(2,1)S(1)}, bf16[144,24]{1,0:T(8,128)(2,1)}, u32[]{:S(2)}) copy-start(bf16[144,24]{1,0:T(8,128)(2,1)} %constant.43.clone.refs_12_) | copy-start | bytes 20740
  3.5 5.2 %collective-permute-start = (f32[40,256]{1,0:T(8,128)S(1)}, f32[40,256]{1,0:T(8,128)S(1)}, u32[]{:S(2)}, u32[]{:S(2)}) collective-permute-start(f32[40,256]{1,0:T(8,128)S(1)} %get-tuple-element.18), channel_id=1, source_target_pairs={{0,2},{1,3},{2,0},{3,1},{4,6},{5,7},{6,4},{7,5},{8,10},{9,11},{10,... | collective-permute-start | bytes 122888 | tf_op jit(solution)/shard_map/ppermute | solution.py:127
  6.5 3.6 %collective-permute-start.1 = (f32[40,256]{1,0:T(8,128)S(1)}, f32[40,256]{1,0:T(8,128)S(1)}, u32[]{:S(2)}, u32[]{:S(2)}) collective-permute-start(f32[40,256]{1,0:T(8,128)S(1)} %get-tuple-element.19), channel_id=1, source_target_pairs={{0,3},{1,2},{2,1},{3,0},{4,7},{5,6},{6,5},{7,4},{8,11},{9,10},{10,... | collective-permute-start | bytes 122888 | tf_op jit(solution)/shard_map/ppermute | solution.py:127
  6.5 3.6 %collective-permute-start.2 = (f32[40,256]{1,0:T(8,128)S(1)}, f32[40,256]{1,0:T(8,128)S(1)}, u32[]{:S(2)}, u32[]{:S(2)}) collective-permute-start(f32[40,256]{1,0:T(8,128)S(1)} %get-tuple-element.20), channel_id=1, source_target_pairs={{0,1},{1,0},{2,3},{3,2},{4,5},{5,4},{6,7},{7,6},{8,9},{9,8},{10,11... | collective-permute-start | bytes 122888 | tf_op jit(solution)/shard_map/ppermute | solution.py:127
  6.7 8.4 %collective-permute-start.6 = (f32[64,128]{1,0:T(8,128)S(1)}, f32[64,128]{1,0:T(8,128)S(1)}, u32[]{:S(2)}, u32[]{:S(2)}) collective-permute-start(f32[64,128]{1,0:T(8,128)S(1)} %get-tuple-element.26), channel_id=1, source_target_pairs={{0,2},{1,3},{2,0},{3,1},{4,6},{5,7},{6,4},{7,5},{8,10},{9,11},{10,... | collective-permute-start | bytes 98312 | tf_op jit(solution)/shard_map/ppermute | solution.py:127
  8.6 6.7 %collective-permute-start.7 = (f32[64,128]{1,0:T(8,128)S(1)}, f32[64,128]{1,0:T(8,128)S(1)}, u32[]{:S(2)}, u32[]{:S(2)}) collective-permute-start(f32[64,128]{1,0:T(8,128)S(1)} %get-tuple-element.27), channel_id=1, source_target_pairs={{0,3},{1,2},{2,1},{3,0},{4,7},{5,6},{6,5},{7,4},{8,11},{9,10},{10,... | collective-permute-start | bytes 98312 | tf_op jit(solution)/shard_map/ppermute | solution.py:127
  8.6 6.7 %collective-permute-start.8 = (f32[64,128]{1,0:T(8,128)S(1)}, f32[64,128]{1,0:T(8,128)S(1)}, u32[]{:S(2)}, u32[]{:S(2)}) collective-permute-start(f32[64,128]{1,0:T(8,128)S(1)} %get-tuple-element.28), channel_id=1, source_target_pairs={{0,1},{1,0},{2,3},{3,2},{4,5},{5,4},{6,7},{7,6},{8,9},{9,8},{10,11... | collective-permute-start | bytes 98312 | tf_op jit(solution)/shard_map/ppermute | solution.py:127
  11.1 4.9 %collective-permute-start.3 = (f32[40,128]{1,0:T(8,128)S(1)}, f32[40,128]{1,0:T(8,128)S(1)}, u32[]{:S(2)}, u32[]{:S(2)}) collective-permute-start(f32[40,128]{1,0:T(8,128)S(1)} %get-tuple-element.22), channel_id=1, source_target_pairs={{0,8},{4,12},{8,0},{12,4},{1,9},{5,13},{9,1},{13,5},{2,10},{6,14},... | collective-permute-start | bytes 61448 | tf_op jit(solution)/shard_map/ppermute | solution.py:127
  13.7 5.6 %collective-permute-start.4 = (f32[40,128]{1,0:T(8,128)S(1)}, f32[40,128]{1,0:T(8,128)S(1)}, u32[]{:S(2)}, u32[]{:S(2)}) collective-permute-start(f32[40,128]{1,0:T(8,128)S(1)} %get-tuple-element.23), channel_id=1, source_target_pairs={{0,12},{4,8},{8,4},{12,0},{1,13},{5,9},{9,5},{13,1},{2,14},{6,10},... | collective-permute-start | bytes 61448 | tf_op jit(solution)/shard_map/ppermute | solution.py:127
  15.1 4.2 %collective-permute-start.5 = (f32[40,128]{1,0:T(8,128)S(1)}, f32[40,128]{1,0:T(8,128)S(1)}, u32[]{:S(2)}, u32[]{:S(2)}) collective-permute-start(f32[40,128]{1,0:T(8,128)S(1)} %get-tuple-element.24), channel_id=1, source_target_pairs={{0,4},{4,0},{8,12},{12,8},{1,5},{5,1},{9,13},{13,9},{2,6},{6,2},{1... | collective-permute-start | bytes 61448 | tf_op jit(solution)/shard_map/ppermute | solution.py:127
  (1 other events, 9.4 us)

commit v7 on v6

--- a/solution.py
+++ b/solution.py
@@ -83,6 +83,19 @@
 
 def dot_three(left, right):
     return dot(left[0], right[0]) + (dot(left[0], right[1]) + dot(left[1], right[0]))
+
+
+def stacked_left(values, depth):
+    wide = np.zeros((values.shape[0], depth))
+    wide[:, : values.shape[1]] = values
+    high = wide.astype(jnp.bfloat16)
+    low = (wide - high.astype(np.float64)).astype(jnp.bfloat16)
+    return jnp.asarray(np.concatenate([high, high, low], 1))
+
+
+def dot_stacked(left, right):
+    high, low = halves(right)
+    return dot(left, jnp.concatenate([high, low, high], 0))
 
 
 def iota(shape, axis):
@@ -238,16 +251,16 @@
     slots = pieces if swapped(pieces) else 1
     outs = rows if swapped(rows) else 1
     fields, refs = refs[:slots], refs[slots:]
-    basis_high, basis_low, back_high, back_low, drive_high, drive_low, edge_high, edge_low = refs[:8]
-    scale, above_table, below_table = refs[8:11]
-    sent, near, lined = refs[11 : 11 + outs], refs[11 + outs + 1], refs[11 + outs + 2]
-    spectrum = refs[11 + outs]
+    basis_high, basis_low, back_high, back_low, drive, edge = refs[:6]
+    scale, above_table, below_table = refs[6:9]
+    sent, near, lined = refs[9 : 9 + outs], refs[9 + outs + 1], refs[9 + outs + 2]
+    spectrum = refs[9 + outs]
     tiles = padded(blocks) // LANES
     mine = lax.axis_index("row")
     side = lax.axis_index("col")
     slot = side * cores + lax.axis_index("sub")
     arranged = pieces_of(fields, slots, pieces, slot, ORDER.get(pieces))
-    lined[SUBN:, :] = jnp.zeros((8, lined.shape[1]), F32)
+    lined[SUBN:, :] = jnp.zeros((16, lined.shape[1]), F32)
     for place, field in arranged:
         lined[pl.ds(pl.multiple_of(place * stripe, 8), stripe), :] = field[:stripe, :]
     for place, field in arranged:
@@ -255,10 +268,10 @@
         lined[head, :] = lined[head, :] + field[stripe:, :]
     source = lined[...]
     across = dot_three(halves(source), (basis_high[...], basis_low[...]))
-    driven = dot_three((drive_high[...], drive_low[...]), halves(across))
+    driven = dot_stacked(drive[...], across)
     response = driven * scale[...]
     spectrum[...] = response
-    edges = [dot_three((edge_high[...], edge_low[...]), halves(response))]
+    edges = [dot_stacked(edge[...], response)]
     for table, start, count in ((above_table, 0, 8), (below_table, SUBN - 8, 9)):
         total = across[start : start + 1] * table[0]
         for step in range(1, count):
@@ -298,8 +311,8 @@
     slots = pieces if swapped(pieces) else 1
     ins = rows if swapped(rows) else 1
     received, extras, refs = refs[:ins], refs[ins : ins + slots], refs[ins + slots :]
-    spectrum, near, back_high, back_low, halo_high, halo_low, out_high, out_low, scale, coarse = refs[:10]
-    phase, mean_flux, spot_size = refs[10:]
+    spectrum, near, back_high, back_low, halo, out, scale, coarse = refs[:8]
+    phase, mean_flux, spot_size = refs[8:]
     tiles = padded(blocks) // LANES
     mine = lax.axis_index("row")
     side = lax.axis_index("col")
@@ -325,18 +338,19 @@
     below = of_row(mine + 1, slice(0, base + 8))
     first = iota((8, LANES), 0) == 0
     top, bottom, spilt = [], [], []
+    empty = [jnp.zeros((8, LANES), F32)] * tiles
     for tile in range(tiles):
         top.append(above[8 * tile : 8 * tile + 8])
         bottom.append(below[8 * tile : 8 * tile + 8])
         start = base + 8 + 2 * blocks + tile
         spilt.append(jnp.where(first, above[start : start + 1], 0.0))
     across = jnp.concatenate(
-        [jnp.concatenate(top, 1), jnp.concatenate(spilt, 1), jnp.concatenate(bottom, 1)], 0
+        [jnp.concatenate(part, 1) for part in (top, spilt, bottom, empty)], 0
     )
-    driven = dot_three((halo_high[...], halo_low[...]), halves(across))
+    driven = dot_stacked(halo[...], across)
     response = spectrum[...] + driven * scale[...]
     reach = dot_three(halves(response), (back_high[side], back_low[side]))
-    solved = dot_three((out_high[...], out_low[...]), halves(reach))
+    solved = dot_stacked(out[...], reach)
     weighted = jnp.zeros((tail, coarse.shape[2]), F32)
     for origin, piece in arranged:
         count = jnp.sum(piece[base + 8 :, :], 1, keepdims=True)
@@ -406,8 +420,8 @@
     basis_pair = constant_pair(basis)
     back_pair = constant_pair(basis.T.reshape(full, blocks, SUBN).transpose(1, 0, 2))
     scale_wide = jnp.asarray(widened(scale, blocks))
-    drive_pair = constant_pair(vectors[:, MARGIN:])
-    edge_pair = constant_pair(np.concatenate([vectors[:8], vectors[WIN - 8 :]], 0))
+    drive = stacked_left(vectors[:, MARGIN:], WIN)
+    edge = stacked_left(np.concatenate([vectors[:8], vectors[WIN - 8 :]], 0), WIN)
     side_tables = [jnp.asarray(widened(table, blocks)) for table in edge_tables()]
     tail = -(-(2 * blocks + tiles) // 8) * 8
     height = 8 * tiles + 8 + tail
@@ -418,28 +432,28 @@
         functools.partial(rims_kernel, sizes),
         out_shape=row_shapes
         + [jax.ShapeDtypeStruct((WIN, full), F32), jax.ShapeDtypeStruct((16, SUBN), F32)],
-        in_specs=in_vmem(len(fields) + 11),
+        in_specs=in_vmem(len(fields) + 9),
         out_specs=in_vmem(len(row_shapes) + 2),
-        scratch_shapes=[pltpu.VMEM((SUBN + 8, width), F32)],
+        scratch_shapes=[pltpu.VMEM((SUBN + 16, width), F32)],
         compiler_params=PARAMS,
         name="rims",
-    )(*fields, *basis_pair, *back_pair, *drive_pair, *edge_pair, scale_wide, *side_tables)
+    )(*fields, *basis_pair, *back_pair, drive, edge, scale_wide, *side_tables)
     received = exchange(sent, ("row",), rows)
 
     halo = np.zeros((WIN, 24))
     halo[:, :9] = vectors[:, :9]
     halo[:, 16:] = vectors[:, WIN - 8 :]
-    halo_pair = constant_pair(halo)
-    out_pair = constant_pair(vectors[MARGIN : MARGIN + SUBN])
+    halo = stacked_left(halo, 32)
+    out = stacked_left(vectors[MARGIN : MARGIN + SUBN], WIN)
     return pl.pallas_call(
         functools.partial(phase_kernel, sizes),
         out_shape=[jax.ShapeDtypeStruct((1, SUBN, SUBN), F32)] * 3,
-        in_specs=in_vmem(len(received) + len(extras) + 10),
+        in_specs=in_vmem(len(received) + len(extras) + 8),
         out_specs=in_vmem(3),
         compiler_params=PARAMS,
         name="phase",
     )(
-        *received, *extras, spectrum, near, *back_pair, *halo_pair, *out_pair, scale_wide,
+        *received, *extras, spectrum, near, *back_pair, halo, out, scale_wide,
         jnp.asarray(coarse_table(rows, blocks, tail)),
     )
 

time: 20.9 us -> 20.6 us (0.986)
  no operation moved by 1% of the time
where the time goes in v7:
time: 20.6 us; the launch traced here: 20.5 us
  starting transfers between devices  9.58 us (47%)
  waiting for transfers between devices  5.26 us (26%)
  Pallas kernels  4.73 us (23%)
  between operations  0.82 us (4%)
    ppermute x9, starting transfers between devices, exchange(): lax.ppermute(pieces[k], axes, [(i, i ^ k) for i in range(count)])  9.58 us
    ppermute x9, waiting for transfers between devices, exchange(): lax.ppermute(pieces[k], axes, [(i, i ^ k) for i in range(count)])  5.26 us
    pallas_call x1, Pallas kernels, body(): pl.pallas_call(functools.partial(moments_kernel, (frames, stripe, blocks,...  2.61 us
    pallas_call x1, Pallas kernels, body(): pl.pallas_call(functools.partial(phase_kernel, sizes), out_shape=[jax.Sha...  1.24 us
    pallas_call x1, Pallas kernels, body(): pl.pallas_call(functools.partial(rims_kernel, sizes), out_shape=row_shape...  0.88 us
  transfers between devices with their start and end apart: 9, of which 3 were waited for; matrix products, arithmetic and copies ran while one was open for 0% of the time, Pallas kernels for 4%

profile of v7, /device:TPU:0, one launch (start us, length us, event | category | flops | bytes accessed | tf_op | source)
XLA Modules:
  0.0 20.5 jit_solution(2140567796446347790)
XLA Ops:
  0.6 0.0 copy-start
  0.6 0.0 copy-start.1
  0.7 0.0 copy-start.2
  0.7 0.0 copy-start.3
  0.7 0.0 copy-start.4
  0.7 0.0 copy-start.7
  0.7 0.0 copy-start.5
  0.7 0.0 copy-start.6
  0.7 0.0 copy-start.10
  0.8 0.0 copy-start.8
  0.8 0.0 copy-start.9
  0.8 2.6 %moments.1 = (f32[40,256]{1,0:T(8,128)S(1)}, f32[40,256]{1,0:T(8,128)S(1)}, f32[40,256]{1,0:T(8,128)S(1)}, f32[40,256]{1,0:T(8,128)S(1)}, f32[64,128]{1,0:T(8,12...) custom-call(bf16[2,256,2048]{2,1,0:T(8,128)(2,1)} %pixels.1), custom_call_target="tpu_custom_call" | custom-call | tf_op jit(solution)/shard_map/moments/pallas_call | solution.py:401
  3.4 3.0 %collective-permute-start = (f32[40,256]{1,0:T(8,128)S(1)}, f32[40,256]{1,0:T(8,128)S(1)}, u32[]{:S(2)}, u32[]{:S(2)}) collective-permute-start(f32[40,256]{1,0:T(8,128)S(1)} %get-tuple-element.18), channel_id=1, source_target_pairs={{0,2},{1,3},{2,0},{3,1},{4,6},{5,7},{6,4},{7,5},{8,10},{9,11},{10,... | collective-permute-start | bytes 122888 | tf_op jit(solution)/shard_map/ppermute | solution.py:140
  6.4 0.2 collective-permute-start.2
  6.6 1.9 %collective-permute-start.6 = (f32[64,128]{1,0:T(8,128)S(1)}, f32[64,128]{1,0:T(8,128)S(1)}, u32[]{:S(2)}, u32[]{:S(2)}) collective-permute-start(f32[64,128]{1,0:T(8,128)S(1)} %get-tuple-element.26), channel_id=1, source_target_pairs={{0,2},{1,3},{2,0},{3,1},{4,6},{5,7},{6,4},{7,5},{8,10},{9,11},{10,... | collective-permute-start | bytes 98312 | tf_op jit(solution)/shard_map/ppermute | solution.py:140
  8.6 0.2 collective-permute-start.8
  8.7 1.3 %collective-permute-done.1.refs_2_ = f32[40,256]{1,0:T(8,128)S(1)} collective-permute-done((f32[40,256]{1,0:T(8,128)S(1)}, f32[40,256]{1,0:T(8,128)S(1)}, u32[]{:S(2)}, u32[]{:S(2)}) %collective-permute-start.1) | collective-permute-done | bytes 40992 | tf_op jit(solution)/shard_map/ppermute | solution.py:140
  10.1 0.9 %rims.1 = (f32[40,128]{1,0:T(8,128)S(1)}, f32[40,128]{1,0:T(8,128)S(1)}, f32[40,128]{1,0:T(8,128)S(1)}, f32[40,128]{1,0:T(8,128)S(1)}, f32[144,384]{1,0:T(8,128)S(1)}, /*index=5*/f32[16,128]{1,0:T(8,128)S(1)}) custom-call(f32[40,256]{1,0:T(8,128)S(1)} %get-tuple-element.17.refs_0_, f32[40,256]{1,0:T(8,128)S(1)} %collective-permute-done.refs_1_, ...), custom_call_target="tpu_custom_call" | custom-call | tf_op jit(solution)/shard_map/rims/pallas_call | solution.py:431
  11.0 2.7 %collective-permute-start.3 = (f32[40,128]{1,0:T(8,128)S(1)}, f32[40,128]{1,0:T(8,128)S(1)}, u32[]{:S(2)}, u32[]{:S(2)}) collective-permute-start(f32[40,128]{1,0:T(8,128)S(1)} %get-tuple-element.22), channel_id=1, source_target_pairs={{0,8},{4,12},{8,0},{12,4},{1,9},{5,13},{9,1},{13,5},{2,10},{6,14},... | collective-permute-start | bytes 61448 | tf_op jit(solution)/shard_map/ppermute | solution.py:140
  13.6 1.4 %collective-permute-start.4 = (f32[40,128]{1,0:T(8,128)S(1)}, f32[40,128]{1,0:T(8,128)S(1)}, u32[]{:S(2)}, u32[]{:S(2)}) collective-permute-start(f32[40,128]{1,0:T(8,128)S(1)} %get-tuple-element.23), channel_id=1, source_target_pairs={{0,12},{4,8},{8,4},{12,0},{1,13},{5,9},{9,5},{13,1},{2,14},{6,10},... | collective-permute-start | bytes 61448 | tf_op jit(solution)/shard_map/ppermute | solution.py:140
  15.0 0.2 %collective-permute-start.5 = (f32[40,128]{1,0:T(8,128)S(1)}, f32[40,128]{1,0:T(8,128)S(1)}, u32[]{:S(2)}, u32[]{:S(2)}) collective-permute-start(f32[40,128]{1,0:T(8,128)S(1)} %get-tuple-element.24), channel_id=1, source_target_pairs={{0,4},{4,0},{8,12},{12,8},{1,5},{5,1},{9,13},{13,9},{2,6},{6,2},{1... | collective-permute-start | bytes 61448 | tf_op jit(solution)/shard_map/ppermute | solution.py:140
  15.2 0.6 %collective-permute-done.3.refs_1_ = f32[40,128]{1,0:T(8,128)S(1)} collective-permute-done((f32[40,128]{1,0:T(8,128)S(1)}, f32[40,128]{1,0:T(8,128)S(1)}, u32[]{:S(2)}, u32[]{:S(2)}) %collective-permute-start.3) | collective-permute-done | bytes 20512 | tf_op jit(solution)/shard_map/ppermute | solution.py:140
  15.8 3.4 %collective-permute-done.4.refs_2_ = f32[40,128]{1,0:T(8,128)S(1)} collective-permute-done((f32[40,128]{1,0:T(8,128)S(1)}, f32[40,128]{1,0:T(8,128)S(1)}, u32[]{:S(2)}, u32[]{:S(2)}) %collective-permute-start.4) | collective-permute-done | bytes 20512 | tf_op jit(solution)/shard_map/ppermute | solution.py:140
  19.2 1.2 %phase.1 = (f32[1,128,128]{2,1,0:T(8,128)}, f32[1,128,128]{2,1,0:T(8,128)}, f32[1,128,128]{2,1,0:T(8,128)}) custom-call(f32[40,128]{1,0:T(8,128)S(1)} %get-tuple-element.21.refs_0_, f32[40,128]{1,0:T(8,128)S(1)} %collective-permute-done.3.refs_1_, f32[40,128]{1,0:T(8,128)S(1)} %collective-permute-done.4.refs_2_, ...), custom_call_target="tpu_custom_call" | custom-call | tf_op jit(solution)/shard_map/phase/pallas_call | solution.py:448
  (21 shorter events, 0.1 us)
Async XLA Ops:
  0.6 9.4 %copy-start = (f32[144,384]{1,0:T(8,128)S(1)}, f32[144,384]{1,0:T(8,128)}, u32[]{:S(2)}) copy-start(f32[144,384]{1,0:T(8,128)} %constant.28.clone.refs_10_.refs_14_) | copy-start | bytes 663556
  0.6 9.4 %copy-start.1 = (bf16[2,384,128]{2,1,0:T(8,128)(2,1)S(1)}, bf16[2,384,128]{2,1,0:T(8,128)(2,1)}, u32[]{:S(2)}) copy-start(bf16[2,384,128]{2,1,0:T(8,128)(2,1)} %constant.27.clone.refs_7_.refs_11_) | copy-start | bytes 589828
  0.7 9.4 %copy-start.2 = (bf16[2,384,128]{2,1,0:T(8,128)(2,1)S(1)}, bf16[2,384,128]{2,1,0:T(8,128)(2,1)}, u32[]{:S(2)}) copy-start(bf16[2,384,128]{2,1,0:T(8,128)(2,1)} %constant.26.clone.refs_6_.refs_10_) | copy-start | bytes 589828
  0.7 9.4 %copy-start.3 = (f32[9,16,384]{2,1,0:T(8,128)S(1)}, f32[9,16,384]{2,1,0:T(8,128)}, u32[]{:S(2)}) copy-start(f32[9,16,384]{2,1,0:T(8,128)} %constant.32.clone.refs_12_) | copy-start | bytes 663556
  0.7 9.4 %copy-start.4 = (f32[8,16,384]{2,1,0:T(8,128)S(1)}, f32[8,16,384]{2,1,0:T(8,128)}, u32[]{:S(2)}) copy-start(f32[8,16,384]{2,1,0:T(8,128)} %constant.31.clone.refs_11_) | copy-start | bytes 589828
  0.7 9.4 %copy-start.11 = (bf16[16,432]{1,0:T(8,128)(2,1)S(1)}, bf16[16,432]{1,0:T(8,128)(2,1)}, u32[]{:S(2)}) copy-start(bf16[16,432]{1,0:T(8,128)(2,1)} %constant.30.clone.refs_9_) | copy-start | bytes 41476
  0.7 9.4 %copy-start.7 = (bf16[144,432]{1,0:T(8,128)(2,1)S(1)}, bf16[144,432]{1,0:T(8,128)(2,1)}, u32[]{:S(2)}) copy-start(bf16[144,432]{1,0:T(8,128)(2,1)} %constant.29.clone.refs_8_) | copy-start | bytes 373252
  0.7 9.4 %copy-start.5 = (bf16[256,384]{1,0:T(8,128)(2,1)S(1)}, bf16[256,384]{1,0:T(8,128)(2,1)}, u32[]{:S(2)}) copy-start(bf16[256,384]{1,0:T(8,128)(2,1)} %constant.25.clone.refs_5_) | copy-start | bytes 589828
  0.7 9.3 %copy-start.6 = (bf16[256,384]{1,0:T(8,128)(2,1)S(1)}, bf16[256,384]{1,0:T(8,128)(2,1)}, u32[]{:S(2)}) copy-start(bf16[256,384]{1,0:T(8,128)(2,1)} %constant.24.clone.refs_4_) | copy-start | bytes 589828
  0.7 18.5 %copy-start.10 = (f32[4,8,128]{2,1,0:T(8,128)S(1)}, f32[4,8,128]{2,1,0:T(8,128)}, u32[]{:S(2)}) copy-start(f32[4,8,128]{2,1,0:T(8,128)} %constant.35.clone.refs_15_) | copy-start | bytes 49156
  0.8 18.5 %copy-start.8 = (bf16[128,432]{1,0:T(8,128)(2,1)S(1)}, bf16[128,432]{1,0:T(8,128)(2,1)}, u32[]{:S(2)}) copy-start(bf16[128,432]{1,0:T(8,128)(2,1)} %constant.34.clone.refs_13_) | copy-start | bytes 331780
  0.8 18.5 %copy-start.9 = (bf16[144,96]{1,0:T(8,128)(2,1)S(1)}, bf16[144,96]{1,0:T(8,128)(2,1)}, u32[]{:S(2)}) copy-start(bf16[144,96]{1,0:T(8,128)(2,1)} %constant.33.clone.refs_12_) | copy-start | bytes 82948
  3.4 5.2 %collective-permute-start = (f32[40,256]{1,0:T(8,128)S(1)}, f32[40,256]{1,0:T(8,128)S(1)}, u32[]{:S(2)}, u32[]{:S(2)}) collective-permute-start(f32[40,256]{1,0:T(8,128)S(1)} %get-tuple-element.18), channel_id=1, source_target_pairs={{0,2},{1,3},{2,0},{3,1},{4,6},{5,7},{6,4},{7,5},{8,10},{9,11},{10,... | collective-permute-start | bytes 122888 | tf_op jit(solution)/shard_map/ppermute | solution.py:140
  6.4 3.6 %collective-permute-start.1 = (f32[40,256]{1,0:T(8,128)S(1)}, f32[40,256]{1,0:T(8,128)S(1)}, u32[]{:S(2)}, u32[]{:S(2)}) collective-permute-start(f32[40,256]{1,0:T(8,128)S(1)} %get-tuple-element.19), channel_id=1, source_target_pairs={{0,3},{1,2},{2,1},{3,0},{4,7},{5,6},{6,5},{7,4},{8,11},{9,10},{10,... | collective-permute-start | bytes 122888 | tf_op jit(solution)/shard_map/ppermute | solution.py:140
  6.4 3.6 %collective-permute-start.2 = (f32[40,256]{1,0:T(8,128)S(1)}, f32[40,256]{1,0:T(8,128)S(1)}, u32[]{:S(2)}, u32[]{:S(2)}) collective-permute-start(f32[40,256]{1,0:T(8,128)S(1)} %get-tuple-element.20), channel_id=1, source_target_pairs={{0,1},{1,0},{2,3},{3,2},{4,5},{5,4},{6,7},{7,6},{8,9},{9,8},{10,11... | collective-permute-start | bytes 122888 | tf_op jit(solution)/shard_map/ppermute | solution.py:140
  6.6 8.4 %collective-permute-start.6 = (f32[64,128]{1,0:T(8,128)S(1)}, f32[64,128]{1,0:T(8,128)S(1)}, u32[]{:S(2)}, u32[]{:S(2)}) collective-permute-start(f32[64,128]{1,0:T(8,128)S(1)} %get-tuple-element.26), channel_id=1, source_target_pairs={{0,2},{1,3},{2,0},{3,1},{4,6},{5,7},{6,4},{7,5},{8,10},{9,11},{10,... | collective-permute-start | bytes 98312 | tf_op jit(solution)/shard_map/ppermute | solution.py:140
  8.5 6.7 %collective-permute-start.7 = (f32[64,128]{1,0:T(8,128)S(1)}, f32[64,128]{1,0:T(8,128)S(1)}, u32[]{:S(2)}, u32[]{:S(2)}) collective-permute-start(f32[64,128]{1,0:T(8,128)S(1)} %get-tuple-element.27), channel_id=1, source_target_pairs={{0,3},{1,2},{2,1},{3,0},{4,7},{5,6},{6,5},{7,4},{8,11},{9,10},{10,... | collective-permute-start | bytes 98312 | tf_op jit(solution)/shard_map/ppermute | solution.py:140
  8.6 6.7 %collective-permute-start.8 = (f32[64,128]{1,0:T(8,128)S(1)}, f32[64,128]{1,0:T(8,128)S(1)}, u32[]{:S(2)}, u32[]{:S(2)}) collective-permute-start(f32[64,128]{1,0:T(8,128)S(1)} %get-tuple-element.28), channel_id=1, source_target_pairs={{0,1},{1,0},{2,3},{3,2},{4,5},{5,4},{6,7},{7,6},{8,9},{9,8},{10,11... | collective-permute-start | bytes 98312 | tf_op jit(solution)/shard_map/ppermute | solution.py:140
  11.0 4.9 %collective-permute-start.3 = (f32[40,128]{1,0:T(8,128)S(1)}, f32[40,128]{1,0:T(8,128)S(1)}, u32[]{:S(2)}, u32[]{:S(2)}) collective-permute-start(f32[40,128]{1,0:T(8,128)S(1)} %get-tuple-element.22), channel_id=1, source_target_pairs={{0,8},{4,12},{8,0},{12,4},{1,9},{5,13},{9,1},{13,5},{2,10},{6,14},... | collective-permute-start | bytes 61448 | tf_op jit(solution)/shard_map/ppermute | solution.py:140
  13.6 5.6 %collective-permute-start.4 = (f32[40,128]{1,0:T(8,128)S(1)}, f32[40,128]{1,0:T(8,128)S(1)}, u32[]{:S(2)}, u32[]{:S(2)}) collective-permute-start(f32[40,128]{1,0:T(8,128)S(1)} %get-tuple-element.23), channel_id=1, source_target_pairs={{0,12},{4,8},{8,4},{12,0},{1,13},{5,9},{9,5},{13,1},{2,14},{6,10},... | collective-permute-start | bytes 61448 | tf_op jit(solution)/shard_map/ppermute | solution.py:140
  15.0 4.2 %collective-permute-start.5 = (f32[40,128]{1,0:T(8,128)S(1)}, f32[40,128]{1,0:T(8,128)S(1)}, u32[]{:S(2)}, u32[]{:S(2)}) collective-permute-start(f32[40,128]{1,0:T(8,128)S(1)} %get-tuple-element.24), channel_id=1, source_target_pairs={{0,4},{4,0},{8,12},{12,8},{1,5},{5,1},{9,13},{13,9},{2,6},{6,2},{1... | collective-permute-start | bytes 61448 | tf_op jit(solution)/shard_map/ppermute | solution.py:140

commit v8 on v7

--- a/solution.py
+++ b/solution.py
@@ -24,7 +24,7 @@
 def constant_pair(values):
     high = np.asarray(values).astype(jnp.bfloat16)
     low = (values - high.astype(np.float64)).astype(jnp.bfloat16)
-    return jnp.asarray(high), jnp.asarray(low)
+    return high, low
 
 
 def sine_basis():
@@ -90,7 +90,7 @@
     wide[:, : values.shape[1]] = values
     high = wide.astype(jnp.bfloat16)
     low = (wide - high.astype(np.float64)).astype(jnp.bfloat16)
-    return jnp.asarray(np.concatenate([high, high, low], 1))
+    return np.concatenate([high, high, low], 1)
 
 
 def dot_stacked(left, right):
@@ -152,6 +152,10 @@
     for step in range(len(values) - 1):
         total = jnp.where(index == step, values[step], total)
     return total
+
+
+def spill_rows(blocks):
+    return -(-blocks // 8) * 8
 
 
 def moments_kernel(sizes, pixels, *refs):
@@ -210,7 +214,11 @@
         left = jnp.where(column > 0, pltpu.roll(flow_x, 1, 1), 0.0)
         above = pltpu.roll(flow_y, 1, 0)
         source = left - flow_x + jnp.where(row > 0, above, 0.0) - flow_y
-        spill = jnp.where(row[:8] == 0, above[:8], 0.0)
+        spill = jnp.zeros((spill_rows(blocks), LANES), F32)
+        spot_row = iota(spill.shape, 0)
+        for block in range(blocks):
+            last = flow_y[stripe - 1 :, block * SUBN : (block + 1) * SUBN]
+            spill = jnp.where(spot_row == block, last, spill)
         fluxes = [mean_flux[:, block * SUBN : (block + 1) * SUBN] for block in range(blocks)]
         spots = [spot_size[:, block * SUBN : (block + 1) * SUBN] for block in range(blocks)]
         return source, spill, fluxes, spots
@@ -234,8 +242,9 @@
             source, spill, flux, spot = found[frame]
             flux, spot = flux[block], spot[block]
             field, extra = fields[0].at[piece], extras[0].at[piece]
-        field[:stripe, :] = source
-        field[stripe:, :] = spill
+        for block in range(blocks):
+            field[block * stripe : (block + 1) * stripe, :] = source[:, block * SUBN : (block + 1) * SUBN]
+        field[blocks * stripe :, :] = spill
         extra[:stripe, :] = flux
         extra[stripe:, :] = spot
 
@@ -246,15 +255,21 @@
     return [(step, refs[0].at[step]) for step in range(count)]
 
 
+def back_of(back, side, tiles):
+    depth = tiles * LANES
+    start = pl.multiple_of(side * (2 * depth), LANES)
+    return back[pl.ds(start, depth), :], back[pl.ds(start + depth, depth), :]
+
+
 def rims_kernel(sizes, *refs):
     stripe, pieces, blocks, cores, rows = sizes
+    width = blocks * SUBN
     slots = pieces if swapped(pieces) else 1
     outs = rows if swapped(rows) else 1
     fields, refs = refs[:slots], refs[slots:]
-    basis_high, basis_low, back_high, back_low, drive, edge = refs[:6]
-    scale, above_table, below_table = refs[6:9]
-    sent, near, lined = refs[9 : 9 + outs], refs[9 + outs + 1], refs[9 + outs + 2]
-    spectrum = refs[9 + outs]
+    basis, back, left, real = refs[:4]
+    sent, near, lined = refs[4 : 4 + outs], refs[4 + outs + 1], refs[4 + outs + 2]
+    spectrum = refs[4 + outs]
     tiles = padded(blocks) // LANES
     mine = lax.axis_index("row")
     side = lax.axis_index("col")
@@ -262,22 +277,29 @@
     arranged = pieces_of(fields, slots, pieces, slot, ORDER.get(pieces))
     lined[SUBN:, :] = jnp.zeros((16, lined.shape[1]), F32)
     for place, field in arranged:
-        lined[pl.ds(pl.multiple_of(place * stripe, 8), stripe), :] = field[:stripe, :]
+        for block in range(blocks):
+            where = pl.ds(pl.multiple_of(place * stripe, 8), stripe)
+            lined[where, block * SUBN : (block + 1) * SUBN] = field[block * stripe : (block + 1) * stripe, :]
+    first = iota((8, LANES), 0) == 0
     for place, field in arranged:
         head = pl.ds(pl.multiple_of((place + 1) * stripe, 8), 8)
-        lined[head, :] = lined[head, :] + field[stripe:, :]
+        for block in range(blocks):
+            cut = slice(block * SUBN, (block + 1) * SUBN)
+            last = field[blocks * stripe + block : blocks * stripe + block + 1, :]
+            lined[head, cut] = lined[head, cut] + jnp.where(first, last, 0.0)
     source = lined[...]
-    across = dot_three(halves(source), (basis_high[...], basis_low[...]))
-    driven = dot_stacked(drive[...], across)
-    response = driven * scale[...]
+    across = dot_three(halves(source), (basis[:width, :], basis[width:, :]))
+    driven = dot_stacked(left[:WIN, :], across)
+    response = driven * real[:WIN, :]
     spectrum[...] = response
-    edges = [dot_stacked(edge[...], response)]
-    for table, start, count in ((above_table, 0, 8), (below_table, SUBN - 8, 9)):
-        total = across[start : start + 1] * table[0]
+    edges = [dot_stacked(left[WIN : WIN + 16, :], response)]
+    for place, start, count in ((WIN, 0, 8), (WIN + 8 * 16, SUBN - 8, 9)):
+        total = across[start : start + 1] * real[place : place + 16, :]
         for step in range(1, count):
-            total = total + across[start + step : start + step + 1] * table[step]
+            table = real[place + 16 * step : place + 16 * step + 16, :]
+            total = total + across[start + step : start + step + 1] * table
         edges.append(total)
-    rims = dot_three(halves(jnp.concatenate(edges, 0)), (back_high[side], back_low[side]))
+    rims = dot_three(halves(jnp.concatenate(edges, 0)), back_of(back, side, tiles))
     near[:8, :] = jnp.where(mine > 0, rims[24:32], 0.0)
     near[8:, :] = jnp.where(mine < rows - 1, rims[32:40], 0.0)
     base = 8 * tiles
@@ -311,8 +333,8 @@
     slots = pieces if swapped(pieces) else 1
     ins = rows if swapped(rows) else 1
     received, extras, refs = refs[:ins], refs[ins : ins + slots], refs[ins + slots :]
-    spectrum, near, back_high, back_low, halo, out, scale, coarse = refs[:8]
-    phase, mean_flux, spot_size = refs[8:]
+    spectrum, near, back, left, real = refs[:5]
+    phase, mean_flux, spot_size = refs[5:]
     tiles = padded(blocks) // LANES
     mine = lax.axis_index("row")
     side = lax.axis_index("col")
@@ -347,14 +369,16 @@
     across = jnp.concatenate(
         [jnp.concatenate(part, 1) for part in (top, spilt, bottom, empty)], 0
     )
-    driven = dot_stacked(halo[...], across)
-    response = spectrum[...] + driven * scale[...]
-    reach = dot_three(halves(response), (back_high[side], back_low[side]))
-    solved = dot_stacked(out[...], reach)
-    weighted = jnp.zeros((tail, coarse.shape[2]), F32)
+    halo = left[WIN + 16 + SUBN :, : 3 * across.shape[0]]
+    driven = dot_stacked(halo, across)
+    response = spectrum[...] + driven * real[:WIN, :]
+    reach = dot_three(halves(response), back_of(back, side, tiles))
+    solved = dot_stacked(left[WIN + 16 : WIN + 16 + SUBN, :], reach)
+    coarse = WIN + 17 * 16
+    weighted = jnp.zeros((tail, real.shape[1]), F32)
     for origin, piece in arranged:
         count = jnp.sum(piece[base + 8 :, :], 1, keepdims=True)
-        weighted = weighted + count * coarse[origin]
+        weighted = weighted + count * real[pl.ds(pl.multiple_of(coarse + origin * tail, 8), tail), :]
     own = iota(weighted.shape, 1) == mine * blocks + side
     level = jnp.sum(jnp.where(own, weighted, 0.0), keepdims=True)
     solved = solved + level
@@ -396,7 +420,7 @@
     pieces = blocks * cores
     assert frames == cores and width == blocks * SUBN and stripe * pieces == SUBN
 
-    field_shapes = piece_shapes(pieces, (stripe + 8, width))
+    field_shapes = piece_shapes(pieces, (blocks * stripe + spill_rows(blocks), LANES))
     extra_shapes = piece_shapes(pieces, (2 * stripe, SUBN))
     made = pl.pallas_call(
         functools.partial(moments_kernel, (frames, stripe, blocks, cores, rows * pieces)),
@@ -417,14 +441,25 @@
     basis = column_basis(blocks)
     full = padded(blocks)
     tiles = full // LANES
-    basis_pair = constant_pair(basis)
-    back_pair = constant_pair(basis.T.reshape(full, blocks, SUBN).transpose(1, 0, 2))
-    scale_wide = jnp.asarray(widened(scale, blocks))
-    drive = stacked_left(vectors[:, MARGIN:], WIN)
-    edge = stacked_left(np.concatenate([vectors[:8], vectors[WIN - 8 :]], 0), WIN)
-    side_tables = [jnp.asarray(widened(table, blocks)) for table in edge_tables()]
     tail = -(-(2 * blocks + tiles) // 8) * 8
     height = 8 * tiles + 8 + tail
+    halo = np.zeros((WIN, 24))
+    halo[:, :9] = vectors[:, :9]
+    halo[:, 16:] = vectors[:, WIN - 8 :]
+    lefts = [
+        stacked_left(vectors[:, MARGIN:], WIN),
+        stacked_left(np.concatenate([vectors[:8], vectors[WIN - 8 :]], 0), WIN),
+        stacked_left(vectors[MARGIN : MARGIN + SUBN], WIN),
+        np.pad(stacked_left(halo, 32), ((0, 0), (0, 3 * WIN - 96))),
+    ]
+    back = constant_pair(basis.T.reshape(full, blocks, SUBN).transpose(1, 0, 2))
+    tables = [widened(table, blocks).reshape(-1, full) for table in (scale,) + edge_tables()]
+    coarse = coarse_table(rows, blocks, tail)
+    tables.append(np.pad(coarse, ((0, 0), (0, 0), (0, full - coarse.shape[2]))).reshape(-1, full))
+    wide = jnp.asarray(np.concatenate(constant_pair(basis), 0))
+    back = jnp.asarray(np.concatenate(back, 1).reshape(-1, SUBN))
+    left = jnp.asarray(np.concatenate(lefts, 0))
+    real = jnp.asarray(np.concatenate(tables, 0).astype(np.float32))
 
     row_shapes = piece_shapes(rows, (height, LANES))
     sizes = (stripe, pieces, blocks, cores, rows)
@@ -432,30 +467,22 @@
         functools.partial(rims_kernel, sizes),
         out_shape=row_shapes
         + [jax.ShapeDtypeStruct((WIN, full), F32), jax.ShapeDtypeStruct((16, SUBN), F32)],
-        in_specs=in_vmem(len(fields) + 9),
+        in_specs=in_vmem(len(fields) + 4),
         out_specs=in_vmem(len(row_shapes) + 2),
         scratch_shapes=[pltpu.VMEM((SUBN + 16, width), F32)],
         compiler_params=PARAMS,
         name="rims",
-    )(*fields, *basis_pair, *back_pair, drive, edge, scale_wide, *side_tables)
+    )(*fields, wide, back, left, real)
     received = exchange(sent, ("row",), rows)
 
-    halo = np.zeros((WIN, 24))
-    halo[:, :9] = vectors[:, :9]
-    halo[:, 16:] = vectors[:, WIN - 8 :]
-    halo = stacked_left(halo, 32)
-    out = stacked_left(vectors[MARGIN : MARGIN + SUBN], WIN)
     return pl.pallas_call(
         functools.partial(phase_kernel, sizes),
         out_shape=[jax.ShapeDtypeStruct((1, SUBN, SUBN), F32)] * 3,
-        in_specs=in_vmem(len(received) + len(extras) + 8),
+        in_specs=in_vmem(len(received) + len(extras) + 5),
         out_specs=in_vmem(3),
         compiler_params=PARAMS,
         name="phase",
-    )(
-        *received, *extras, spectrum, near, *back_pair, halo, out, scale_wide,
-        jnp.asarray(coarse_table(rows, blocks, tail)),
-    )
+    )(*received, *extras, spectrum, near, back, left, real)
 
 
 def solution(mesh):

time: 20.6 us -> 20.3 us (0.985)
  no operation moved by 1% of the time
where the time goes in v8:
time: 20.3 us; the launch traced here: 20.1 us
  starting transfers between devices  9.57 us (47%)
  waiting for transfers between devices  5.17 us (25%)
  Pallas kernels  4.67 us (23%)
  between operations  0.7 us (3%)
    ppermute x9, starting transfers between devices, exchange(): lax.ppermute(pieces[k], axes, [(i, i ^ k) for i in range(count)])  9.57 us
    ppermute x9, waiting for transfers between devices, exchange(): lax.ppermute(pieces[k], axes, [(i, i ^ k) for i in range(count)])  5.17 us
    pallas_call x1, Pallas kernels, body(): pl.pallas_call(functools.partial(moments_kernel, (frames, stripe, blocks,...  2.56 us
    pallas_call x1, Pallas kernels, body(): pl.pallas_call(functools.partial(phase_kernel, sizes), out_shape=[jax.Sha...  1.23 us
    pallas_call x1, Pallas kernels, body(): pl.pallas_call(functools.partial(rims_kernel, sizes), out_shape=row_shape...  0.87 us
  transfers between devices with their start and end apart: 9, of which 3 were waited for; matrix products, arithmetic and copies ran while one was open for 0% of the time, Pallas kernels for 4%

profile of v8, /device:TPU:0, one launch (start us, length us, event | category | flops | bytes accessed | tf_op | source)
XLA Modules:
  0.0 20.1 jit_solution(16020120931131543988)
XLA Ops:
  0.6 0.0 copy-start
  0.6 0.0 copy-start.1
  0.7 0.0 copy-start.2
  0.7 0.0 copy-start.3
  0.7 2.6 %moments.1 = (f32[72,128]{1,0:T(8,128)S(1)}, f32[72,128]{1,0:T(8,128)S(1)}, f32[72,128]{1,0:T(8,128)S(1)}, f32[72,128]{1,0:T(8,128)S(1)}, f32[64,128]{1,0:T(8,12...) custom-call(bf16[2,256,2048]{2,1,0:T(8,128)(2,1)} %pixels.1), custom_call_target="tpu_custom_call" | custom-call | tf_op jit(solution)/shard_map/moments/pallas_call | solution.py:425
  3.3 3.0 %collective-permute-start = (f32[72,128]{1,0:T(8,128)S(1)}, f32[72,128]{1,0:T(8,128)S(1)}, u32[]{:S(2)}, u32[]{:S(2)}) collective-permute-start(f32[72,128]{1,0:T(8,128)S(1)} %get-tuple-element.18), channel_id=1, source_target_pairs={{0,2},{1,3},{2,0},{3,1},{4,6},{5,7},{6,4},{7,5},{8,10},{9,11},{10,... | collective-permute-start | bytes 110600 | tf_op jit(solution)/shard_map/ppermute | solution.py:140
  6.3 0.0 collective-permute-start.1
  6.3 0.2 collective-permute-start.2
  6.4 1.9 %collective-permute-start.6 = (f32[64,128]{1,0:T(8,128)S(1)}, f32[64,128]{1,0:T(8,128)S(1)}, u32[]{:S(2)}, u32[]{:S(2)}) collective-permute-start(f32[64,128]{1,0:T(8,128)S(1)} %get-tuple-element.26), channel_id=1, source_target_pairs={{0,2},{1,3},{2,0},{3,1},{4,6},{5,7},{6,4},{7,5},{8,10},{9,11},{10,... | collective-permute-start | bytes 98312 | tf_op jit(solution)/shard_map/ppermute | solution.py:140
  8.4 0.0 collective-permute-start.7
  8.4 0.0 collective-permute-done.refs_1_
  8.4 0.2 collective-permute-start.8
  8.6 1.2 %collective-permute-done.1.refs_2_ = f32[72,128]{1,0:T(8,128)S(1)} collective-permute-done((f32[72,128]{1,0:T(8,128)S(1)}, f32[72,128]{1,0:T(8,128)S(1)}, u32[]{:S(2)}, u32[]{:S(2)}) %collective-permute-start.1) | collective-permute-done | bytes 36896 | tf_op jit(solution)/shard_map/ppermute | solution.py:140
  9.8 0.0 collective-permute-done.2.refs_3_
  9.8 0.9 %rims.1 = (f32[40,128]{1,0:T(8,128)S(1)}, f32[40,128]{1,0:T(8,128)S(1)}, f32[40,128]{1,0:T(8,128)S(1)}, f32[40,128]{1,0:T(8,128)S(1)}, f32[144,384]{1,0:T(8,128)S(1)}, /*index=5*/f32[16,128]{1,0:T(8,128)S(1)}) custom-call(f32[72,128]{1,0:T(8,128)S(1)} %get-tuple-element.17.refs_0_, f32[72,128]{1,0:T(8,128)S(1)} %collective-permute-done.refs_1_, ...), custom_call_target="tpu_custom_call" | custom-call | tf_op jit(solution)/shard_map/rims/pallas_call | solution.py:466
  10.7 2.7 %collective-permute-start.3 = (f32[40,128]{1,0:T(8,128)S(1)}, f32[40,128]{1,0:T(8,128)S(1)}, u32[]{:S(2)}, u32[]{:S(2)}) collective-permute-start(f32[40,128]{1,0:T(8,128)S(1)} %get-tuple-element.22), channel_id=1, source_target_pairs={{0,8},{4,12},{8,0},{12,4},{1,9},{5,13},{9,1},{13,5},{2,10},{6,14},... | collective-permute-start | bytes 61448 | tf_op jit(solution)/shard_map/ppermute | solution.py:140
  13.3 1.3 %collective-permute-start.4 = (f32[40,128]{1,0:T(8,128)S(1)}, f32[40,128]{1,0:T(8,128)S(1)}, u32[]{:S(2)}, u32[]{:S(2)}) collective-permute-start(f32[40,128]{1,0:T(8,128)S(1)} %get-tuple-element.23), channel_id=1, source_target_pairs={{0,12},{4,8},{8,4},{12,0},{1,13},{5,9},{9,5},{13,1},{2,14},{6,10},... | collective-permute-start | bytes 61448 | tf_op jit(solution)/shard_map/ppermute | solution.py:140
  14.7 0.0 collective-permute-done.6.refs_5_
  14.7 0.2 %collective-permute-start.5 = (f32[40,128]{1,0:T(8,128)S(1)}, f32[40,128]{1,0:T(8,128)S(1)}, u32[]{:S(2)}, u32[]{:S(2)}) collective-permute-start(f32[40,128]{1,0:T(8,128)S(1)} %get-tuple-element.24), channel_id=1, source_target_pairs={{0,4},{4,0},{8,12},{12,8},{1,5},{5,1},{9,13},{13,9},{2,6},{6,2},{1... | collective-permute-start | bytes 61448 | tf_op jit(solution)/shard_map/ppermute | solution.py:140
  14.9 0.0 collective-permute-done.7.refs_6_
  14.9 0.0 collective-permute-done.8.refs_7_
  14.9 0.6 %collective-permute-done.3.refs_1_ = f32[40,128]{1,0:T(8,128)S(1)} collective-permute-done((f32[40,128]{1,0:T(8,128)S(1)}, f32[40,128]{1,0:T(8,128)S(1)}, u32[]{:S(2)}, u32[]{:S(2)}) %collective-permute-start.3) | collective-permute-done | bytes 20512 | tf_op jit(solution)/shard_map/ppermute | solution.py:140
  15.5 3.4 %collective-permute-done.4.refs_2_ = f32[40,128]{1,0:T(8,128)S(1)} collective-permute-done((f32[40,128]{1,0:T(8,128)S(1)}, f32[40,128]{1,0:T(8,128)S(1)}, u32[]{:S(2)}, u32[]{:S(2)}) %collective-permute-start.4) | collective-permute-done | bytes 20512 | tf_op jit(solution)/shard_map/ppermute | solution.py:140
  18.9 1.2 %phase.1 = (f32[1,128,128]{2,1,0:T(8,128)}, f32[1,128,128]{2,1,0:T(8,128)}, f32[1,128,128]{2,1,0:T(8,128)}) custom-call(f32[40,128]{1,0:T(8,128)S(1)} %get-tuple-element.21.refs_0_, f32[40,128]{1,0:T(8,128)S(1)} %collective-permute-done.3.refs_1_, f32[40,128]{1,0:T(8,128)S(1)} %collective-permute-done.4.refs_2_, ...), custom_call_target="tpu_custom_call" | custom-call | tf_op jit(solution)/shard_map/phase/pallas_call | solution.py:478
  (5 shorter events, 0.0 us)
Async XLA Ops:
  0.6 9.1 %copy-start = (f32[448,384]{1,0:T(8,128)S(1)}, f32[448,384]{1,0:T(8,128)}, u32[]{:S(2)}) copy-start(f32[448,384]{1,0:T(8,128)} %constant.11.clone.refs_7_.refs_12_) | copy-start | bytes 2064388
  0.6 9.1 %copy-start.1 = (bf16[432,432]{1,0:T(8,128)(2,1)S(1)}, bf16[432,432]{1,0:T(8,128)(2,1)}, u32[]{:S(2)}) copy-start(bf16[432,432]{1,0:T(8,128)(2,1)} %constant.10.clone.refs_6_.refs_11_) | copy-start | bytes 1119748
  0.7 9.1 %copy-start.2 = (bf16[1536,128]{1,0:T(8,128)(2,1)S(1)}, bf16[1536,128]{1,0:T(8,128)(2,1)}, u32[]{:S(2)}) copy-start(bf16[1536,128]{1,0:T(8,128)(2,1)} %constant.9.clone.refs_5_.refs_10_) | copy-start | bytes 1179652
  0.7 9.1 %copy-start.3 = (bf16[512,384]{1,0:T(8,128)(2,1)S(1)}, bf16[512,384]{1,0:T(8,128)(2,1)}, u32[]{:S(2)}) copy-start(bf16[512,384]{1,0:T(8,128)(2,1)} %constant.8.clone.refs_4_) | copy-start | bytes 1179652
  3.3 5.2 %collective-permute-start = (f32[72,128]{1,0:T(8,128)S(1)}, f32[72,128]{1,0:T(8,128)S(1)}, u32[]{:S(2)}, u32[]{:S(2)}) collective-permute-start(f32[72,128]{1,0:T(8,128)S(1)} %get-tuple-element.18), channel_id=1, source_target_pairs={{0,2},{1,3},{2,0},{3,1},{4,6},{5,7},{6,4},{7,5},{8,10},{9,11},{10,... | collective-permute-start | bytes 110600 | tf_op jit(solution)/shard_map/ppermute | solution.py:140
  6.3 3.5 %collective-permute-start.1 = (f32[72,128]{1,0:T(8,128)S(1)}, f32[72,128]{1,0:T(8,128)S(1)}, u32[]{:S(2)}, u32[]{:S(2)}) collective-permute-start(f32[72,128]{1,0:T(8,128)S(1)} %get-tuple-element.19), channel_id=1, source_target_pairs={{0,3},{1,2},{2,1},{3,0},{4,7},{5,6},{6,5},{7,4},{8,11},{9,10},{10,... | collective-permute-start | bytes 110600 | tf_op jit(solution)/shard_map/ppermute | solution.py:140
  6.3 3.5 %collective-permute-start.2 = (f32[72,128]{1,0:T(8,128)S(1)}, f32[72,128]{1,0:T(8,128)S(1)}, u32[]{:S(2)}, u32[]{:S(2)}) collective-permute-start(f32[72,128]{1,0:T(8,128)S(1)} %get-tuple-element.20), channel_id=1, source_target_pairs={{0,1},{1,0},{2,3},{3,2},{4,5},{5,4},{6,7},{7,6},{8,9},{9,8},{10,11... | collective-permute-start | bytes 110600 | tf_op jit(solution)/shard_map/ppermute | solution.py:140
  6.4 8.2 %collective-permute-start.6 = (f32[64,128]{1,0:T(8,128)S(1)}, f32[64,128]{1,0:T(8,128)S(1)}, u32[]{:S(2)}, u32[]{:S(2)}) collective-permute-start(f32[64,128]{1,0:T(8,128)S(1)} %get-tuple-element.26), channel_id=1, source_target_pairs={{0,2},{1,3},{2,0},{3,1},{4,6},{5,7},{6,4},{7,5},{8,10},{9,11},{10,... | collective-permute-start | bytes 98312 | tf_op jit(solution)/shard_map/ppermute | solution.py:140
  8.4 6.5 %collective-permute-start.7 = (f32[64,128]{1,0:T(8,128)S(1)}, f32[64,128]{1,0:T(8,128)S(1)}, u32[]{:S(2)}, u32[]{:S(2)}) collective-permute-start(f32[64,128]{1,0:T(8,128)S(1)} %get-tuple-element.27), channel_id=1, source_target_pairs={{0,3},{1,2},{2,1},{3,0},{4,7},{5,6},{6,5},{7,4},{8,11},{9,10},{10,... | collective-permute-start | bytes 98312 | tf_op jit(solution)/shard_map/ppermute | solution.py:140
  8.4 6.5 %collective-permute-start.8 = (f32[64,128]{1,0:T(8,128)S(1)}, f32[64,128]{1,0:T(8,128)S(1)}, u32[]{:S(2)}, u32[]{:S(2)}) collective-permute-start(f32[64,128]{1,0:T(8,128)S(1)} %get-tuple-element.28), channel_id=1, source_target_pairs={{0,1},{1,0},{2,3},{3,2},{4,5},{5,4},{6,7},{7,6},{8,9},{9,8},{10,11... | collective-permute-start | bytes 98312 | tf_op jit(solution)/shard_map/ppermute | solution.py:140
  10.7 4.8 %collective-permute-start.3 = (f32[40,128]{1,0:T(8,128)S(1)}, f32[40,128]{1,0:T(8,128)S(1)}, u32[]{:S(2)}, u32[]{:S(2)}) collective-permute-start(f32[40,128]{1,0:T(8,128)S(1)} %get-tuple-element.22), channel_id=1, source_target_pairs={{0,8},{4,12},{8,0},{12,4},{1,9},{5,13},{9,1},{13,5},{2,10},{6,14},... | collective-permute-start | bytes 61448 | tf_op jit(solution)/shard_map/ppermute | solution.py:140
  13.3 5.6 %collective-permute-start.4 = (f32[40,128]{1,0:T(8,128)S(1)}, f32[40,128]{1,0:T(8,128)S(1)}, u32[]{:S(2)}, u32[]{:S(2)}) collective-permute-start(f32[40,128]{1,0:T(8,128)S(1)} %get-tuple-element.23), channel_id=1, source_target_pairs={{0,12},{4,8},{8,4},{12,0},{1,13},{5,9},{9,5},{13,1},{2,14},{6,10},... | collective-permute-start | bytes 61448 | tf_op jit(solution)/shard_map/ppermute | solution.py:140
  14.7 4.2 %collective-permute-start.5 = (f32[40,128]{1,0:T(8,128)S(1)}, f32[40,128]{1,0:T(8,128)S(1)}, u32[]{:S(2)}, u32[]{:S(2)}) collective-permute-start(f32[40,128]{1,0:T(8,128)S(1)} %get-tuple-element.24), channel_id=1, source_target_pairs={{0,4},{4,0},{8,12},{12,8},{1,5},{5,1},{9,13},{13,9},{2,6},{6,2},{1... | collective-permute-start | bytes 61448 | tf_op jit(solution)/shard_map/ppermute | solution.py:140

commit v9 on v8

--- a/solution.py
+++ b/solution.py
@@ -328,21 +328,27 @@
         piece[base + 8 :, :] = sums
 
 
+def outputs_kernel(sizes, *refs):
+    stripe, pieces, blocks, cores, rows = sizes
+    slots = pieces if swapped(pieces) else 1
+    extras, (mean_flux, spot_size) = refs[:slots], refs[slots:]
+    slot = lax.axis_index("col") * cores + lax.axis_index("sub")
+    for place, extra in pieces_of(extras, slots, pieces, slot, ORDER.get(pieces)):
+        where = pl.ds(pl.multiple_of(place * stripe, 8), stripe)
+        mean_flux[0, where, :] = extra[:stripe, :]
+        spot_size[0, where, :] = extra[stripe:, :]
+
+
 def phase_kernel(sizes, *refs):
     stripe, pieces, blocks, cores, rows = sizes
     slots = pieces if swapped(pieces) else 1
     ins = rows if swapped(rows) else 1
-    received, extras, refs = refs[:ins], refs[ins : ins + slots], refs[ins + slots :]
+    received, refs = refs[:ins], refs[ins:]
     spectrum, near, back, left, real = refs[:5]
-    phase, mean_flux, spot_size = refs[5:]
+    phase = refs[5]
     tiles = padded(blocks) // LANES
     mine = lax.axis_index("row")
     side = lax.axis_index("col")
-    slot = side * cores + lax.axis_index("sub")
-    for place, extra in pieces_of(extras, slots, pieces, slot, ORDER.get(pieces)):
-        where = pl.ds(pl.multiple_of(place * stripe, 8), stripe)
-        mean_flux[0, where, :] = extra[:stripe, :]
-        spot_size[0, where, :] = extra[stripe:, :]
     base = 8 * tiles
     tail = received[0].shape[-2] - base - 8
     arranged = pieces_of(received, ins, rows, mine, ORDER.get(rows))
@@ -475,14 +481,23 @@
     )(*fields, wide, back, left, real)
     received = exchange(sent, ("row",), rows)
 
-    return pl.pallas_call(
+    mean_flux, spot_size = pl.pallas_call(
+        functools.partial(outputs_kernel, sizes),
+        out_shape=[jax.ShapeDtypeStruct((1, SUBN, SUBN), F32)] * 2,
+        in_specs=in_vmem(len(extras)),
+        out_specs=in_vmem(2),
+        compiler_params=PARAMS,
+        name="outputs",
+    )(*extras)
+    phase = pl.pallas_call(
         functools.partial(phase_kernel, sizes),
-        out_shape=[jax.ShapeDtypeStruct((1, SUBN, SUBN), F32)] * 3,
-        in_specs=in_vmem(len(received) + len(extras) + 5),
-        out_specs=in_vmem(3),
+        out_shape=jax.ShapeDtypeStruct((1, SUBN, SUBN), F32),
+        in_specs=in_vmem(len(received) + 5),
+        out_specs=pl.BlockSpec(memory_space=pltpu.VMEM),
         compiler_params=PARAMS,
         name="phase",
-    )(*received, *extras, spectrum, near, back, left, real)
+    )(*received, spectrum, near, back, left, real)
+    return phase, mean_flux, spot_size
 
 
 def solution(mesh):

time: 20.3 us -> 20.3 us (level)
  waiting for transfers between devices: 5.17 us -> 4.51 us
  Pallas kernels: 4.67 us -> 5.32 us
    ppermute x9, waiting for transfers between devices: 5.17 us -> 4.51 us  [exchange(): lax.ppermute(pieces[k], axes, [(i, i ^ k) for i in range(count)])]
    pallas_call x1 -> x2, Pallas kernels: 1.23 us -> 1.89 us  [the longest x1 1.22 us: body(): pl.pallas_call(functools.partial(phase_kernel, sizes), out_shape=jax.Shap...]
  transfers between devices with their start and end apart: 9 -> 9, of which waited for: 3 -> 2; matrix products, arithmetic and copies ran while one was open for 0% -> 0% of each run, Pallas kernels for 4% -> 8%
where the time goes in v9:
time: 20.3 us; the launch traced here: 20.1 us
  starting transfers between devices  9.57 us (47%)
  Pallas kernels  5.32 us (26%)
  waiting for transfers between devices  4.51 us (22%)
  between operations  0.71 us (3%)
    ppermute x9, starting transfers between devices, exchange(): lax.ppermute(pieces[k], axes, [(i, i ^ k) for i in range(count)])  9.57 us
    ppermute x9, waiting for transfers between devices, exchange(): lax.ppermute(pieces[k], axes, [(i, i ^ k) for i in range(count)])  4.51 us
    pallas_call x1, Pallas kernels, body(): pl.pallas_call(functools.partial(moments_kernel, (frames, stripe, blocks,...  2.56 us
    pallas_call x1, Pallas kernels, body(): pl.pallas_call(functools.partial(phase_kernel, sizes), out_shape=jax.Shap...  1.22 us
    pallas_call x1, Pallas kernels, body(): pl.pallas_call(functools.partial(rims_kernel, sizes), out_shape=row_shape...  0.87 us
    pallas_call x1, Pallas kernels, body(): pl.pallas_call(functools.partial(outputs_kernel, sizes), out_shape=[jax.S...  0.67 us
  transfers between devices with their start and end apart: 9, of which 2 were waited for; matrix products, arithmetic and copies ran while one was open for 0% of the time, Pallas kernels for 8%

profile of v9, /device:TPU:0, one launch (start us, length us, event | category | flops | bytes accessed | tf_op | source)
XLA Modules:
  0.0 20.1 jit_solution(17483528793725774221)
XLA Ops:
  0.6 0.0 copy-start
  0.6 0.0 copy-start.1
  0.7 0.0 copy-start.2
  0.7 0.0 copy-start.3
  0.7 2.6 %moments.1 = (f32[72,128]{1,0:T(8,128)S(1)}, f32[72,128]{1,0:T(8,128)S(1)}, f32[72,128]{1,0:T(8,128)S(1)}, f32[72,128]{1,0:T(8,128)S(1)}, f32[64,128]{1,0:T(8,12...) custom-call(bf16[2,256,2048]{2,1,0:T(8,128)(2,1)} %pixels.1), custom_call_target="tpu_custom_call" | custom-call | tf_op jit(solution)/shard_map/moments/pallas_call | solution.py:431
  3.3 3.0 %collective-permute-start = (f32[72,128]{1,0:T(8,128)S(1)}, f32[72,128]{1,0:T(8,128)S(1)}, u32[]{:S(2)}, u32[]{:S(2)}) collective-permute-start(f32[72,128]{1,0:T(8,128)S(1)} %get-tuple-element.20), channel_id=1, source_target_pairs={{0,2},{1,3},{2,0},{3,1},{4,6},{5,7},{6,4},{7,5},{8,10},{9,11},{10,... | collective-permute-start | bytes 110600 | tf_op jit(solution)/shard_map/ppermute | solution.py:140
  6.3 0.0 collective-permute-start.1
  6.3 0.2 collective-permute-start.2
  6.4 1.9 %collective-permute-start.6 = (f32[64,128]{1,0:T(8,128)S(1)}, f32[64,128]{1,0:T(8,128)S(1)}, u32[]{:S(2)}, u32[]{:S(2)}) collective-permute-start(f32[64,128]{1,0:T(8,128)S(1)} %get-tuple-element.30), channel_id=1, source_target_pairs={{0,2},{1,3},{2,0},{3,1},{4,6},{5,7},{6,4},{7,5},{8,10},{9,11},{10,... | collective-permute-start | bytes 98312 | tf_op jit(solution)/shard_map/ppermute | solution.py:140
  8.4 0.0 collective-permute-start.7
  8.4 0.0 collective-permute-done.refs_1_
  8.4 0.2 collective-permute-start.8
  8.6 1.2 %collective-permute-done.1.refs_2_ = f32[72,128]{1,0:T(8,128)S(1)} collective-permute-done((f32[72,128]{1,0:T(8,128)S(1)}, f32[72,128]{1,0:T(8,128)S(1)}, u32[]{:S(2)}, u32[]{:S(2)}) %collective-permute-start.1) | collective-permute-done | bytes 36896 | tf_op jit(solution)/shard_map/ppermute | solution.py:140
  9.8 0.0 collective-permute-done.2.refs_3_
  9.8 0.9 %rims.1 = (f32[40,128]{1,0:T(8,128)S(1)}, f32[40,128]{1,0:T(8,128)S(1)}, f32[40,128]{1,0:T(8,128)S(1)}, f32[40,128]{1,0:T(8,128)S(1)}, f32[144,384]{1,0:T(8,128)S(1)}, /*index=5*/f32[16,128]{1,0:T(8,128)S(1)}) custom-call(f32[72,128]{1,0:T(8,128)S(1)} %get-tuple-element.19.refs_0_, f32[72,128]{1,0:T(8,128)S(1)} %collective-permute-done.refs_1_, ...), custom_call_target="tpu_custom_call" | custom-call | tf_op jit(solution)/shard_map/rims/pallas_call | solution.py:472
  10.7 2.7 %collective-permute-start.3 = (f32[40,128]{1,0:T(8,128)S(1)}, f32[40,128]{1,0:T(8,128)S(1)}, u32[]{:S(2)}, u32[]{:S(2)}) collective-permute-start(f32[40,128]{1,0:T(8,128)S(1)} %get-tuple-element.24), channel_id=1, source_target_pairs={{0,8},{4,12},{8,0},{12,4},{1,9},{5,13},{9,1},{13,5},{2,10},{6,14},... | collective-permute-start | bytes 61448 | tf_op jit(solution)/shard_map/ppermute | solution.py:140
  13.3 1.3 %collective-permute-start.4 = (f32[40,128]{1,0:T(8,128)S(1)}, f32[40,128]{1,0:T(8,128)S(1)}, u32[]{:S(2)}, u32[]{:S(2)}) collective-permute-start(f32[40,128]{1,0:T(8,128)S(1)} %get-tuple-element.25), channel_id=1, source_target_pairs={{0,12},{4,8},{8,4},{12,0},{1,13},{5,9},{9,5},{13,1},{2,14},{6,10},... | collective-permute-start | bytes 61448 | tf_op jit(solution)/shard_map/ppermute | solution.py:140
  14.7 0.0 collective-permute-done.6.refs_1_
  14.7 0.2 %collective-permute-start.5 = (f32[40,128]{1,0:T(8,128)S(1)}, f32[40,128]{1,0:T(8,128)S(1)}, u32[]{:S(2)}, u32[]{:S(2)}) collective-permute-start(f32[40,128]{1,0:T(8,128)S(1)} %get-tuple-element.26), channel_id=1, source_target_pairs={{0,4},{4,0},{8,12},{12,8},{1,5},{5,1},{9,13},{13,9},{2,6},{6,2},{1... | collective-permute-start | bytes 61448 | tf_op jit(solution)/shard_map/ppermute | solution.py:140
  14.9 0.0 collective-permute-done.7.refs_2_
  14.9 0.0 collective-permute-done.8.refs_3_
  14.9 0.7 %outputs.1 = (f32[1,128,128]{2,1,0:T(8,128)}, f32[1,128,128]{2,1,0:T(8,128)}) custom-call(f32[64,128]{1,0:T(8,128)S(1)} %get-tuple-element.29.refs_0_, f32[64,128]{1,0:T(8,128)S(1)} %collective-permute-done.6.refs_1_, f32[64,128]{1,0:T(8,128)S(1)} %collective-permute-done.7.refs_2_, f32[64,128]{1,0:T(8,128)S(1)} %collective-permute-done.8.refs_3_), custom_call_target="tpu_custom_call" | custom-call | tf_op jit(solution)/shard_map/outputs/pallas_call | solution.py:484
  15.6 3.3 %collective-permute-done.4.refs_2_ = f32[40,128]{1,0:T(8,128)S(1)} collective-permute-done((f32[40,128]{1,0:T(8,128)S(1)}, f32[40,128]{1,0:T(8,128)S(1)}, u32[]{:S(2)}, u32[]{:S(2)}) %collective-permute-start.4) | collective-permute-done | bytes 20512 | tf_op jit(solution)/shard_map/ppermute | solution.py:140
  18.9 1.2 %phase.1 = f32[1,128,128]{2,1,0:T(8,128)} custom-call(f32[40,128]{1,0:T(8,128)S(1)} %get-tuple-element.23.refs_0_, f32[40,128]{1,0:T(8,128)S(1)} %collective-permute-done.3.refs_1_, f32[40,128]{1,0:T(8,128)S(1)} %collective-permute-done.4.refs_2_, f32[40,128]{1,0:T(8,128)S(1)} %collective-permute-done.5.refs_3_, f32[144,384]{1,0:T(8,128)S(1)} %get-tuple-element.27.refs_4_, ...), custom_call_target="tpu_custom_call" | custom-call | tf_op jit(solution)/shard_map/phase/pallas_call | solution.py:492
  (6 shorter events, 0.0 us)
Async XLA Ops:
  0.6 9.1 %copy-start = (f32[448,384]{1,0:T(8,128)S(1)}, f32[448,384]{1,0:T(8,128)}, u32[]{:S(2)}) copy-start(f32[448,384]{1,0:T(8,128)} %constant.11.clone.refs_7_.refs_8_) | copy-start | bytes 2064388
  0.6 9.1 %copy-start.1 = (bf16[432,432]{1,0:T(8,128)(2,1)S(1)}, bf16[432,432]{1,0:T(8,128)(2,1)}, u32[]{:S(2)}) copy-start(bf16[432,432]{1,0:T(8,128)(2,1)} %constant.10.clone.refs_6_.refs_7_) | copy-start | bytes 1119748
  0.7 9.1 %copy-start.2 = (bf16[1536,128]{1,0:T(8,128)(2,1)S(1)}, bf16[1536,128]{1,0:T(8,128)(2,1)}, u32[]{:S(2)}) copy-start(bf16[1536,128]{1,0:T(8,128)(2,1)} %constant.9.clone.refs_5_.refs_6_) | copy-start | bytes 1179652
  0.7 9.1 %copy-start.3 = (bf16[512,384]{1,0:T(8,128)(2,1)S(1)}, bf16[512,384]{1,0:T(8,128)(2,1)}, u32[]{:S(2)}) copy-start(bf16[512,384]{1,0:T(8,128)(2,1)} %constant.8.clone.refs_4_) | copy-start | bytes 1179652
  3.3 5.2 %collective-permute-start = (f32[72,128]{1,0:T(8,128)S(1)}, f32[72,128]{1,0:T(8,128)S(1)}, u32[]{:S(2)}, u32[]{:S(2)}) collective-permute-start(f32[72,128]{1,0:T(8,128)S(1)} %get-tuple-element.20), channel_id=1, source_target_pairs={{0,2},{1,3},{2,0},{3,1},{4,6},{5,7},{6,4},{7,5},{8,10},{9,11},{10,... | collective-permute-start | bytes 110600 | tf_op jit(solution)/shard_map/ppermute | solution.py:140
  6.3 3.5 %collective-permute-start.1 = (f32[72,128]{1,0:T(8,128)S(1)}, f32[72,128]{1,0:T(8,128)S(1)}, u32[]{:S(2)}, u32[]{:S(2)}) collective-permute-start(f32[72,128]{1,0:T(8,128)S(1)} %get-tuple-element.21), channel_id=1, source_target_pairs={{0,3},{1,2},{2,1},{3,0},{4,7},{5,6},{6,5},{7,4},{8,11},{9,10},{10,... | collective-permute-start | bytes 110600 | tf_op jit(solution)/shard_map/ppermute | solution.py:140
  6.3 3.5 %collective-permute-start.2 = (f32[72,128]{1,0:T(8,128)S(1)}, f32[72,128]{1,0:T(8,128)S(1)}, u32[]{:S(2)}, u32[]{:S(2)}) collective-permute-start(f32[72,128]{1,0:T(8,128)S(1)} %get-tuple-element.22), channel_id=1, source_target_pairs={{0,1},{1,0},{2,3},{3,2},{4,5},{5,4},{6,7},{7,6},{8,9},{9,8},{10,11... | collective-permute-start | bytes 110600 | tf_op jit(solution)/shard_map/ppermute | solution.py:140
  6.4 8.2 %collective-permute-start.6 = (f32[64,128]{1,0:T(8,128)S(1)}, f32[64,128]{1,0:T(8,128)S(1)}, u32[]{:S(2)}, u32[]{:S(2)}) collective-permute-start(f32[64,128]{1,0:T(8,128)S(1)} %get-tuple-element.30), channel_id=1, source_target_pairs={{0,2},{1,3},{2,0},{3,1},{4,6},{5,7},{6,4},{7,5},{8,10},{9,11},{10,... | collective-permute-start | bytes 98312 | tf_op jit(solution)/shard_map/ppermute | solution.py:140
  8.4 6.5 %collective-permute-start.7 = (f32[64,128]{1,0:T(8,128)S(1)}, f32[64,128]{1,0:T(8,128)S(1)}, u32[]{:S(2)}, u32[]{:S(2)}) collective-permute-start(f32[64,128]{1,0:T(8,128)S(1)} %get-tuple-element.31), channel_id=1, source_target_pairs={{0,3},{1,2},{2,1},{3,0},{4,7},{5,6},{6,5},{7,4},{8,11},{9,10},{10,... | collective-permute-start | bytes 98312 | tf_op jit(solution)/shard_map/ppermute | solution.py:140
  8.4 6.5 %collective-permute-start.8 = (f32[64,128]{1,0:T(8,128)S(1)}, f32[64,128]{1,0:T(8,128)S(1)}, u32[]{:S(2)}, u32[]{:S(2)}) collective-permute-start(f32[64,128]{1,0:T(8,128)S(1)} %get-tuple-element.32), channel_id=1, source_target_pairs={{0,1},{1,0},{2,3},{3,2},{4,5},{5,4},{6,7},{7,6},{8,9},{9,8},{10,11... | collective-permute-start | bytes 98312 | tf_op jit(solution)/shard_map/ppermute | solution.py:140
  10.7 4.9 %collective-permute-start.3 = (f32[40,128]{1,0:T(8,128)S(1)}, f32[40,128]{1,0:T(8,128)S(1)}, u32[]{:S(2)}, u32[]{:S(2)}) collective-permute-start(f32[40,128]{1,0:T(8,128)S(1)} %get-tuple-element.24), channel_id=1, source_target_pairs={{0,8},{4,12},{8,0},{12,4},{1,9},{5,13},{9,1},{13,5},{2,10},{6,14},... | collective-permute-start | bytes 61448 | tf_op jit(solution)/shard_map/ppermute | solution.py:140
  13.3 5.6 %collective-permute-start.4 = (f32[40,128]{1,0:T(8,128)S(1)}, f32[40,128]{1,0:T(8,128)S(1)}, u32[]{:S(2)}, u32[]{:S(2)}) collective-permute-start(f32[40,128]{1,0:T(8,128)S(1)} %get-tuple-element.25), channel_id=1, source_target_pairs={{0,12},{4,8},{8,4},{12,0},{1,13},{5,9},{9,5},{13,1},{2,14},{6,10},... | collective-permute-start | bytes 61448 | tf_op jit(solution)/shard_map/ppermute | solution.py:140
  14.7 4.2 %collective-permute-start.5 = (f32[40,128]{1,0:T(8,128)S(1)}, f32[40,128]{1,0:T(8,128)S(1)}, u32[]{:S(2)}, u32[]{:S(2)}) collective-permute-start(f32[40,128]{1,0:T(8,128)S(1)} %get-tuple-element.26), channel_id=1, source_target_pairs={{0,4},{4,0},{8,12},{12,8},{1,5},{5,1},{9,13},{13,9},{2,6},{6,2},{1... | collective-permute-start | bytes 61448 | tf_op jit(solution)/shard_map/ppermute | solution.py:140

commit v10 on v9

--- a/solution.py
+++ b/solution.py
@@ -127,17 +127,18 @@
 
 
 ORDER = {1: (), 2: (1,), 4: (2, 3, 1)}
+CELL_ORDER = {1: (), 2: (1,), 4: (2, 1, 3)}
 
 
 def swapped(count):
     return count in ORDER
 
 
-def exchange(pieces, axes, count):
+def exchange(pieces, axes, count, orders):
     if not swapped(count):
         return [lax.all_to_all(pieces[0], axes, split_axis=0, concat_axis=0, tiled=True)]
     return [pieces[0]] + [
-        lax.ppermute(pieces[k], axes, [(i, i ^ k) for i in range(count)]) for k in ORDER[count]
+        lax.ppermute(pieces[k], axes, [(i, i ^ k) for i in range(count)]) for k in orders[count]
     ]
 
 
@@ -274,7 +275,7 @@
     mine = lax.axis_index("row")
     side = lax.axis_index("col")
     slot = side * cores + lax.axis_index("sub")
-    arranged = pieces_of(fields, slots, pieces, slot, ORDER.get(pieces))
+    arranged = pieces_of(fields, slots, pieces, slot, CELL_ORDER.get(pieces))
     lined[SUBN:, :] = jnp.zeros((16, lined.shape[1]), F32)
     for place, field in arranged:
         for block in range(blocks):
@@ -333,7 +334,7 @@
     slots = pieces if swapped(pieces) else 1
     extras, (mean_flux, spot_size) = refs[:slots], refs[slots:]
     slot = lax.axis_index("col") * cores + lax.axis_index("sub")
-    for place, extra in pieces_of(extras, slots, pieces, slot, ORDER.get(pieces)):
+    for place, extra in pieces_of(extras, slots, pieces, slot, CELL_ORDER.get(pieces)):
         where = pl.ds(pl.multiple_of(place * stripe, 8), stripe)
         mean_flux[0, where, :] = extra[:stripe, :]
         spot_size[0, where, :] = extra[stripe:, :]
@@ -440,8 +441,8 @@
         compiler_params=PARAMS,
         name="moments",
     )(pltpu.with_memory_space_constraint(pixels, pltpu.HBM))
-    fields = exchange(made[: len(field_shapes)], ("col", "sub"), pieces)
-    extras = exchange(made[len(field_shapes) :], ("col", "sub"), pieces)
+    fields = exchange(made[: len(field_shapes)], ("col", "sub"), pieces, CELL_ORDER)
+    extras = exchange(made[len(field_shapes) :], ("col", "sub"), pieces, CELL_ORDER)
 
     vectors, scale = sine_basis()
     basis = column_basis(blocks)
@@ -479,7 +480,7 @@
         compiler_params=PARAMS,
         name="rims",
     )(*fields, wide, back, left, real)
-    received = exchange(sent, ("row",), rows)
+    received = exchange(sent, ("row",), rows, ORDER)
 
     mean_flux, spot_size = pl.pallas_call(
         functools.partial(outputs_kernel, sizes),

time: 20.3 us -> 20.2 us (level)
  no operation moved by 1% of the time
where the time goes in v10:
time: 20.2 us; the launch traced here: 20.1 us
  starting transfers between devices  9.58 us (47%)
  Pallas kernels  5.32 us (26%)
  waiting for transfers between devices  4.43 us (22%)
  between operations  0.7 us (3%)
    ppermute x9, starting transfers between devices, exchange(): lax.ppermute(pieces[k], axes, [(i, i ^ k) for i in range(count)])  9.58 us
    ppermute x9, waiting for transfers between devices, exchange(): lax.ppermute(pieces[k], axes, [(i, i ^ k) for i in range(count)])  4.43 us
    pallas_call x1, Pallas kernels, body(): pl.pallas_call(functools.partial(moments_kernel, (frames, stripe, blocks,...  2.56 us
    pallas_call x1, Pallas kernels, body(): pl.pallas_call(functools.partial(phase_kernel, sizes), out_shape=jax.Shap...  1.22 us
    pallas_call x1, Pallas kernels, body(): pl.pallas_call(functools.partial(rims_kernel, sizes), out_shape=row_shape...  0.87 us
    pallas_call x1, Pallas kernels, body(): pl.pallas_call(functools.partial(outputs_kernel, sizes), out_shape=[jax.S...  0.67 us
  transfers between devices with their start and end apart: 9, of which 2 were waited for; matrix products, arithmetic and copies ran while one was open for 0% of the time, Pallas kernels for 8%

profile of v10, /device:TPU:0, one launch (start us, length us, event | category | flops | bytes accessed | tf_op | source)
XLA Modules:
  0.0 20.1 jit_solution(15728255414517395433)
XLA Ops:
  0.6 0.0 copy-start
  0.6 0.0 copy-start.1
  0.7 0.0 copy-start.2
  0.7 0.0 copy-start.3
  0.7 2.6 %moments.1 = (f32[72,128]{1,0:T(8,128)S(1)}, f32[72,128]{1,0:T(8,128)S(1)}, f32[72,128]{1,0:T(8,128)S(1)}, f32[72,128]{1,0:T(8,128)S(1)}, f32[64,128]{1,0:T(8,12...) custom-call(bf16[2,256,2048]{2,1,0:T(8,128)(2,1)} %pixels.1), custom_call_target="tpu_custom_call" | custom-call | tf_op jit(solution)/shard_map/moments/pallas_call | solution.py:432
  3.3 3.0 %collective-permute-start = (f32[72,128]{1,0:T(8,128)S(1)}, f32[72,128]{1,0:T(8,128)S(1)}, u32[]{:S(2)}, u32[]{:S(2)}) collective-permute-start(f32[72,128]{1,0:T(8,128)S(1)} %get-tuple-element.20), channel_id=1, source_target_pairs={{0,2},{1,3},{2,0},{3,1},{4,6},{5,7},{6,4},{7,5},{8,10},{9,11},{10,... | collective-permute-start | bytes 110600 | tf_op jit(solution)/shard_map/ppermute | solution.py:141
  6.3 0.0 collective-permute-start.1
  6.3 0.2 %collective-permute-start.2 = (f32[72,128]{1,0:T(8,128)S(1)}, f32[72,128]{1,0:T(8,128)S(1)}, u32[]{:S(2)}, u32[]{:S(2)}) collective-permute-start(f32[72,128]{1,0:T(8,128)S(1)} %get-tuple-element.22), channel_id=1, source_target_pairs={{0,3},{1,2},{2,1},{3,0},{4,7},{5,6},{6,5},{7,4},{8,11},{9,10},{10,... | collective-permute-start | bytes 110600 | tf_op jit(solution)/shard_map/ppermute | solution.py:141
  6.5 1.9 %collective-permute-start.6 = (f32[64,128]{1,0:T(8,128)S(1)}, f32[64,128]{1,0:T(8,128)S(1)}, u32[]{:S(2)}, u32[]{:S(2)}) collective-permute-start(f32[64,128]{1,0:T(8,128)S(1)} %get-tuple-element.30), channel_id=1, source_target_pairs={{0,2},{1,3},{2,0},{3,1},{4,6},{5,7},{6,4},{7,5},{8,10},{9,11},{10,... | collective-permute-start | bytes 98312 | tf_op jit(solution)/shard_map/ppermute | solution.py:141
  8.4 0.0 collective-permute-start.7
  8.4 0.0 collective-permute-done.refs_1_
  8.4 0.2 %collective-permute-start.8 = (f32[64,128]{1,0:T(8,128)S(1)}, f32[64,128]{1,0:T(8,128)S(1)}, u32[]{:S(2)}, u32[]{:S(2)}) collective-permute-start(f32[64,128]{1,0:T(8,128)S(1)} %get-tuple-element.32), channel_id=1, source_target_pairs={{0,3},{1,2},{2,1},{3,0},{4,7},{5,6},{6,5},{7,4},{8,11},{9,10},{10,... | collective-permute-start | bytes 98312 | tf_op jit(solution)/shard_map/ppermute | solution.py:141
  8.6 0.0 collective-permute-done.1.refs_2_
  8.6 1.0 %collective-permute-done.2.refs_3_ = f32[72,128]{1,0:T(8,128)S(1)} collective-permute-done((f32[72,128]{1,0:T(8,128)S(1)}, f32[72,128]{1,0:T(8,128)S(1)}, u32[]{:S(2)}, u32[]{:S(2)}) %collective-permute-start.2) | collective-permute-done | bytes 36896 | tf_op jit(solution)/shard_map/ppermute | solution.py:141
  9.7 0.9 %rims.1 = (f32[40,128]{1,0:T(8,128)S(1)}, f32[40,128]{1,0:T(8,128)S(1)}, f32[40,128]{1,0:T(8,128)S(1)}, f32[40,128]{1,0:T(8,128)S(1)}, f32[144,384]{1,0:T(8,128)S(1)}, /*index=5*/f32[16,128]{1,0:T(8,128)S(1)}) custom-call(f32[72,128]{1,0:T(8,128)S(1)} %get-tuple-element.19.refs_0_, f32[72,128]{1,0:T(8,128)S(1)} %collective-permute-done.refs_1_, ...), custom_call_target="tpu_custom_call" | custom-call | tf_op jit(solution)/shard_map/rims/pallas_call | solution.py:473
  10.5 2.7 %collective-permute-start.3 = (f32[40,128]{1,0:T(8,128)S(1)}, f32[40,128]{1,0:T(8,128)S(1)}, u32[]{:S(2)}, u32[]{:S(2)}) collective-permute-start(f32[40,128]{1,0:T(8,128)S(1)} %get-tuple-element.24), channel_id=1, source_target_pairs={{0,8},{4,12},{8,0},{12,4},{1,9},{5,13},{9,1},{13,5},{2,10},{6,14},... | collective-permute-start | bytes 61448 | tf_op jit(solution)/shard_map/ppermute | solution.py:141
  13.2 1.4 %collective-permute-start.4 = (f32[40,128]{1,0:T(8,128)S(1)}, f32[40,128]{1,0:T(8,128)S(1)}, u32[]{:S(2)}, u32[]{:S(2)}) collective-permute-start(f32[40,128]{1,0:T(8,128)S(1)} %get-tuple-element.25), channel_id=1, source_target_pairs={{0,12},{4,8},{8,4},{12,0},{1,13},{5,9},{9,5},{13,1},{2,14},{6,10},... | collective-permute-start | bytes 61448 | tf_op jit(solution)/shard_map/ppermute | solution.py:141
  14.5 0.2 %collective-permute-start.5 = (f32[40,128]{1,0:T(8,128)S(1)}, f32[40,128]{1,0:T(8,128)S(1)}, u32[]{:S(2)}, u32[]{:S(2)}) collective-permute-start(f32[40,128]{1,0:T(8,128)S(1)} %get-tuple-element.26), channel_id=1, source_target_pairs={{0,4},{4,0},{8,12},{12,8},{1,5},{5,1},{9,13},{13,9},{2,6},{6,2},{1... | collective-permute-start | bytes 61448 | tf_op jit(solution)/shard_map/ppermute | solution.py:141
  14.8 0.0 collective-permute-done.7.refs_2_
  14.8 0.0 collective-permute-done.8.refs_3_
  14.8 0.7 %outputs.1 = (f32[1,128,128]{2,1,0:T(8,128)}, f32[1,128,128]{2,1,0:T(8,128)}) custom-call(f32[64,128]{1,0:T(8,128)S(1)} %get-tuple-element.29.refs_0_, f32[64,128]{1,0:T(8,128)S(1)} %collective-permute-done.6.refs_1_, f32[64,128]{1,0:T(8,128)S(1)} %collective-permute-done.7.refs_2_, f32[64,128]{1,0:T(8,128)S(1)} %collective-permute-done.8.refs_3_), custom_call_target="tpu_custom_call" | custom-call | tf_op jit(solution)/shard_map/outputs/pallas_call | solution.py:485
  15.5 0.0 collective-permute-done.3.refs_1_
  15.5 3.4 %collective-permute-done.4.refs_2_ = f32[40,128]{1,0:T(8,128)S(1)} collective-permute-done((f32[40,128]{1,0:T(8,128)S(1)}, f32[40,128]{1,0:T(8,128)S(1)}, u32[]{:S(2)}, u32[]{:S(2)}) %collective-permute-start.4) | collective-permute-done | bytes 20512 | tf_op jit(solution)/shard_map/ppermute | solution.py:141
  18.8 1.2 %phase.1 = f32[1,128,128]{2,1,0:T(8,128)} custom-call(f32[40,128]{1,0:T(8,128)S(1)} %get-tuple-element.23.refs_0_, f32[40,128]{1,0:T(8,128)S(1)} %collective-permute-done.3.refs_1_, f32[40,128]{1,0:T(8,128)S(1)} %collective-permute-done.4.refs_2_, f32[40,128]{1,0:T(8,128)S(1)} %collective-permute-done.5.refs_3_, f32[144,384]{1,0:T(8,128)S(1)} %get-tuple-element.27.refs_4_, ...), custom_call_target="tpu_custom_call" | custom-call | tf_op jit(solution)/shard_map/phase/pallas_call | solution.py:493
  (6 shorter events, 0.0 us)
Async XLA Ops:
  0.6 9.0 %copy-start = (f32[448,384]{1,0:T(8,128)S(1)}, f32[448,384]{1,0:T(8,128)}, u32[]{:S(2)}) copy-start(f32[448,384]{1,0:T(8,128)} %constant.11.clone.refs_7_.refs_8_) | copy-start | bytes 2064388
  0.6 9.0 %copy-start.1 = (bf16[432,432]{1,0:T(8,128)(2,1)S(1)}, bf16[432,432]{1,0:T(8,128)(2,1)}, u32[]{:S(2)}) copy-start(bf16[432,432]{1,0:T(8,128)(2,1)} %constant.10.clone.refs_6_.refs_7_) | copy-start | bytes 1119748
  0.7 9.0 %copy-start.2 = (bf16[1536,128]{1,0:T(8,128)(2,1)S(1)}, bf16[1536,128]{1,0:T(8,128)(2,1)}, u32[]{:S(2)}) copy-start(bf16[1536,128]{1,0:T(8,128)(2,1)} %constant.9.clone.refs_5_.refs_6_) | copy-start | bytes 1179652
  0.7 9.0 %copy-start.3 = (bf16[512,384]{1,0:T(8,128)(2,1)S(1)}, bf16[512,384]{1,0:T(8,128)(2,1)}, u32[]{:S(2)}) copy-start(bf16[512,384]{1,0:T(8,128)(2,1)} %constant.8.clone.refs_4_) | copy-start | bytes 1179652
  3.3 5.2 %collective-permute-start = (f32[72,128]{1,0:T(8,128)S(1)}, f32[72,128]{1,0:T(8,128)S(1)}, u32[]{:S(2)}, u32[]{:S(2)}) collective-permute-start(f32[72,128]{1,0:T(8,128)S(1)} %get-tuple-element.20), channel_id=1, source_target_pairs={{0,2},{1,3},{2,0},{3,1},{4,6},{5,7},{6,4},{7,5},{8,10},{9,11},{10,... | collective-permute-start | bytes 110600 | tf_op jit(solution)/shard_map/ppermute | solution.py:141
  6.3 2.4 %collective-permute-start.1 = (f32[72,128]{1,0:T(8,128)S(1)}, f32[72,128]{1,0:T(8,128)S(1)}, u32[]{:S(2)}, u32[]{:S(2)}) collective-permute-start(f32[72,128]{1,0:T(8,128)S(1)} %get-tuple-element.21), channel_id=1, source_target_pairs={{0,1},{1,0},{2,3},{3,2},{4,5},{5,4},{6,7},{7,6},{8,9},{9,8},{10,11... | collective-permute-start | bytes 110600 | tf_op jit(solution)/shard_map/ppermute | solution.py:141
  6.3 3.4 %collective-permute-start.2 = (f32[72,128]{1,0:T(8,128)S(1)}, f32[72,128]{1,0:T(8,128)S(1)}, u32[]{:S(2)}, u32[]{:S(2)}) collective-permute-start(f32[72,128]{1,0:T(8,128)S(1)} %get-tuple-element.22), channel_id=1, source_target_pairs={{0,3},{1,2},{2,1},{3,0},{4,7},{5,6},{6,5},{7,4},{8,11},{9,10},{10,... | collective-permute-start | bytes 110600 | tf_op jit(solution)/shard_map/ppermute | solution.py:141
  6.5 8.1 %collective-permute-start.6 = (f32[64,128]{1,0:T(8,128)S(1)}, f32[64,128]{1,0:T(8,128)S(1)}, u32[]{:S(2)}, u32[]{:S(2)}) collective-permute-start(f32[64,128]{1,0:T(8,128)S(1)} %get-tuple-element.30), channel_id=1, source_target_pairs={{0,2},{1,3},{2,0},{3,1},{4,6},{5,7},{6,4},{7,5},{8,10},{9,11},{10,... | collective-permute-start | bytes 98312 | tf_op jit(solution)/shard_map/ppermute | solution.py:141
  8.4 6.4 %collective-permute-start.7 = (f32[64,128]{1,0:T(8,128)S(1)}, f32[64,128]{1,0:T(8,128)S(1)}, u32[]{:S(2)}, u32[]{:S(2)}) collective-permute-start(f32[64,128]{1,0:T(8,128)S(1)} %get-tuple-element.31), channel_id=1, source_target_pairs={{0,1},{1,0},{2,3},{3,2},{4,5},{5,4},{6,7},{7,6},{8,9},{9,8},{10,11... | collective-permute-start | bytes 98312 | tf_op jit(solution)/shard_map/ppermute | solution.py:141
  8.4 6.4 %collective-permute-start.8 = (f32[64,128]{1,0:T(8,128)S(1)}, f32[64,128]{1,0:T(8,128)S(1)}, u32[]{:S(2)}, u32[]{:S(2)}) collective-permute-start(f32[64,128]{1,0:T(8,128)S(1)} %get-tuple-element.32), channel_id=1, source_target_pairs={{0,3},{1,2},{2,1},{3,0},{4,7},{5,6},{6,5},{7,4},{8,11},{9,10},{10,... | collective-permute-start | bytes 98312 | tf_op jit(solution)/shard_map/ppermute | solution.py:141
  10.5 4.9 %collective-permute-start.3 = (f32[40,128]{1,0:T(8,128)S(1)}, f32[40,128]{1,0:T(8,128)S(1)}, u32[]{:S(2)}, u32[]{:S(2)}) collective-permute-start(f32[40,128]{1,0:T(8,128)S(1)} %get-tuple-element.24), channel_id=1, source_target_pairs={{0,8},{4,12},{8,0},{12,4},{1,9},{5,13},{9,1},{13,5},{2,10},{6,14},... | collective-permute-start | bytes 61448 | tf_op jit(solution)/shard_map/ppermute | solution.py:141
  13.2 5.6 %collective-permute-start.4 = (f32[40,128]{1,0:T(8,128)S(1)}, f32[40,128]{1,0:T(8,128)S(1)}, u32[]{:S(2)}, u32[]{:S(2)}) collective-permute-start(f32[40,128]{1,0:T(8,128)S(1)} %get-tuple-element.25), channel_id=1, source_target_pairs={{0,12},{4,8},{8,4},{12,0},{1,13},{5,9},{9,5},{13,1},{2,14},{6,10},... | collective-permute-start | bytes 61448 | tf_op jit(solution)/shard_map/ppermute | solution.py:141
  14.5 4.3 %collective-permute-start.5 = (f32[40,128]{1,0:T(8,128)S(1)}, f32[40,128]{1,0:T(8,128)S(1)}, u32[]{:S(2)}, u32[]{:S(2)}) collective-permute-start(f32[40,128]{1,0:T(8,128)S(1)} %get-tuple-element.26), channel_id=1, source_target_pairs={{0,4},{4,0},{8,12},{12,8},{1,5},{5,1},{9,13},{13,9},{2,6},{6,2},{1... | collective-permute-start | bytes 61448 | tf_op jit(solution)/shard_map/ppermute | solution.py:141

commit v11 on v10

--- a/solution.py
+++ b/solution.py
@@ -254,6 +254,10 @@
     if slots > 1:
         return [(mine ^ step, ref) for step, ref in zip((0,) + tuple(order), refs)]
     return [(step, refs[0].at[step]) for step in range(count)]
+
+
+def tail_rows(blocks):
+    return -(-(2 * blocks + padded(blocks) // LANES) // 8) * 8
 
 
 def back_of(back, side, tiles):
@@ -303,8 +307,7 @@
     rims = dot_three(halves(jnp.concatenate(edges, 0)), back_of(back, side, tiles))
     near[:8, :] = jnp.where(mine > 0, rims[24:32], 0.0)
     near[8:, :] = jnp.where(mine < rows - 1, rims[32:40], 0.0)
-    base = 8 * tiles
-    tail = sent[0].shape[-2] - base - 8
+    tail = tail_rows(blocks)
     total = jnp.sum(source[:SUBN], 0, keepdims=True)
     place = iota((tail, LANES), 0)
     sums = jnp.zeros((tail, LANES), F32)
@@ -321,12 +324,14 @@
         rim = jnp.where(ahead == 1, rims[8:16], rim)
         rim = jnp.where(ahead == -2, rims[16:24], rim)
         rim = jnp.where(ahead == 2, rims[40:], rim)
+        piece[:8, :] = rim
+        piece[8 : 8 + tail, :] = sums
+        if piece.shape[-2] == 8 + tail:
+            continue
         for tile in range(tiles):
             cut = slice(tile * LANES, (tile + 1) * LANES)
             line = jnp.where(ahead == -1, across[:8, cut], across[SUBN - 8 : SUBN, cut])
-            piece[8 * tile : 8 * tile + 8, :] = line
-        piece[base : base + 8, :] = rim
-        piece[base + 8 :, :] = sums
+            piece[8 + tail + 8 * tile : 16 + tail + 8 * tile, :] = line
 
 
 def outputs_kernel(sizes, *refs):
@@ -350,8 +355,7 @@
     tiles = padded(blocks) // LANES
     mine = lax.axis_index("row")
     side = lax.axis_index("col")
-    base = 8 * tiles
-    tail = received[0].shape[-2] - base - 8
+    tail = tail_rows(blocks)
     arranged = pieces_of(received, ins, rows, mine, ORDER.get(rows))
 
     def of_row(row, where):
@@ -360,18 +364,21 @@
             return jnp.where(inside, received[0][jnp.clip(row, 0, rows - 1), where, :], 0.0)
         total = jnp.zeros((where.stop - where.start, LANES), F32)
         for origin, piece in arranged[1:]:
+            if piece.shape[-2] < where.stop:
+                continue
             total = jnp.where(origin == row, piece[where, :], total)
         return total
 
-    above = of_row(mine - 1, slice(0, received[0].shape[-2]))
-    below = of_row(mine + 1, slice(0, base + 8))
+    above = of_row(mine - 1, slice(0, 8 + tail + 8 * tiles))
+    below = of_row(mine + 1, slice(0, 8 + tail + 8 * tiles))
     first = iota((8, LANES), 0) == 0
     top, bottom, spilt = [], [], []
     empty = [jnp.zeros((8, LANES), F32)] * tiles
     for tile in range(tiles):
-        top.append(above[8 * tile : 8 * tile + 8])
-        bottom.append(below[8 * tile : 8 * tile + 8])
-        start = base + 8 + 2 * blocks + tile
+        lines = slice(8 + tail + 8 * tile, 16 + tail + 8 * tile)
+        top.append(above[lines])
+        bottom.append(below[lines])
+        start = 8 + 2 * blocks + tile
         spilt.append(jnp.where(first, above[start : start + 1], 0.0))
     across = jnp.concatenate(
         [jnp.concatenate(part, 1) for part in (top, spilt, bottom, empty)], 0
@@ -384,12 +391,12 @@
     coarse = WIN + 17 * 16
     weighted = jnp.zeros((tail, real.shape[1]), F32)
     for origin, piece in arranged:
-        count = jnp.sum(piece[base + 8 :, :], 1, keepdims=True)
+        count = jnp.sum(piece[8 : 8 + tail, :], 1, keepdims=True)
         weighted = weighted + count * real[pl.ds(pl.multiple_of(coarse + origin * tail, 8), tail), :]
     own = iota(weighted.shape, 1) == mine * blocks + side
     level = jnp.sum(jnp.where(own, weighted, 0.0), keepdims=True)
     solved = solved + level
-    rim = slice(base, base + 8)
+    rim = slice(0, 8)
     head = near[:8, :] + above[rim] + of_row(mine - 2, rim)
     foot = near[8:, :] + below[rim] + of_row(mine + 2, rim)
     phase[0, :8, :] = solved[:8] + head
@@ -448,8 +455,8 @@
     basis = column_basis(blocks)
     full = padded(blocks)
     tiles = full // LANES
-    tail = -(-(2 * blocks + tiles) // 8) * 8
-    height = 8 * tiles + 8 + tail
+    tail = tail_rows(blocks)
+    short, height = 8 + tail, 8 + tail + 8 * tiles
     halo = np.zeros((WIN, 24))
     halo[:, :9] = vectors[:, :9]
     halo[:, 16:] = vectors[:, WIN - 8 :]
@@ -469,6 +476,9 @@
     real = jnp.asarray(np.concatenate(tables, 0).astype(np.float32))
 
     row_shapes = piece_shapes(rows, (height, LANES))
+    if swapped(rows):
+        touching = [any(abs((row ^ k) - row) == 1 for row in range(rows)) for k in range(rows)]
+        row_shapes = [jax.ShapeDtypeStruct((height if one else short, LANES), F32) for one in touching]
     sizes = (stripe, pieces, blocks, cores, rows)
     *sent, spectrum, near = pl.pallas_call(
         functools.partial(rims_kernel, sizes),

time: 20.2 us -> 20.1 us (level)
  waiting for transfers between devices: 4.43 us -> 4.14 us
  starting transfers between devices: 9.58 us -> 9.8 us
    ppermute x9, waiting for transfers between devices: 4.43 us -> 4.14 us  [exchange(): lax.ppermute(pieces[k], axes, [(i, i ^ k) for i in range(count)])]
    ppermute x9, starting transfers between devices: 9.58 us -> 9.8 us  [exchange(): lax.ppermute(pieces[k], axes, [(i, i ^ k) for i in range(count)])]
where the time goes in v11:
time: 20.1 us; the launch traced here: 20 us
  starting transfers between devices  9.8 us (49%)
  Pallas kernels  5.32 us (26%)
  waiting for transfers between devices  4.14 us (21%)
  between operations  0.7 us (3%)
    ppermute x9, starting transfers between devices, exchange(): lax.ppermute(pieces[k], axes, [(i, i ^ k) for i in range(count)])  9.8 us
    ppermute x9, waiting for transfers between devices, exchange(): lax.ppermute(pieces[k], axes, [(i, i ^ k) for i in range(count)])  4.14 us
    pallas_call x1, Pallas kernels, body(): pl.pallas_call(functools.partial(moments_kernel, (frames, stripe, blocks,...  2.56 us
    pallas_call x1, Pallas kernels, body(): pl.pallas_call(functools.partial(phase_kernel, sizes), out_shape=jax.Shap...  1.21 us
    pallas_call x1, Pallas kernels, body(): pl.pallas_call(functools.partial(rims_kernel, sizes), out_shape=row_shape...  0.87 us
    pallas_call x1, Pallas kernels, body(): pl.pallas_call(functools.partial(outputs_kernel, sizes), out_shape=[jax.S...  0.67 us
  transfers between devices with their start and end apart: 9, of which 2 were waited for; matrix products, arithmetic and copies ran while one was open for 0% of the time, Pallas kernels for 8%

profile of v11, /device:TPU:0, one launch (start us, length us, event | category | flops | bytes accessed | tf_op | source)
XLA Modules:
  0.0 20.0 jit_solution(18189906072951413346)
XLA Ops:
  0.6 0.0 copy-start
  0.6 0.0 copy-start.1
  0.7 0.0 copy-start.2
  0.7 0.0 copy-start.3
  0.7 2.6 %moments.1 = (f32[72,128]{1,0:T(8,128)S(1)}, f32[72,128]{1,0:T(8,128)S(1)}, f32[72,128]{1,0:T(8,128)S(1)}, f32[72,128]{1,0:T(8,128)S(1)}, f32[64,128]{1,0:T(8,12...) custom-call(bf16[2,256,2048]{2,1,0:T(8,128)(2,1)} %pixels.1), custom_call_target="tpu_custom_call" | custom-call | tf_op jit(solution)/shard_map/moments/pallas_call | solution.py:439
  3.3 3.0 %collective-permute-start = (f32[72,128]{1,0:T(8,128)S(1)}, f32[72,128]{1,0:T(8,128)S(1)}, u32[]{:S(2)}, u32[]{:S(2)}) collective-permute-start(f32[72,128]{1,0:T(8,128)S(1)} %get-tuple-element.20), channel_id=1, source_target_pairs={{0,2},{1,3},{2,0},{3,1},{4,6},{5,7},{6,4},{7,5},{8,10},{9,11},{10,... | collective-permute-start | bytes 110600 | tf_op jit(solution)/shard_map/ppermute | solution.py:141
  6.3 0.0 collective-permute-start.1
  6.3 0.2 %collective-permute-start.2 = (f32[72,128]{1,0:T(8,128)S(1)}, f32[72,128]{1,0:T(8,128)S(1)}, u32[]{:S(2)}, u32[]{:S(2)}) collective-permute-start(f32[72,128]{1,0:T(8,128)S(1)} %get-tuple-element.22), channel_id=1, source_target_pairs={{0,3},{1,2},{2,1},{3,0},{4,7},{5,6},{6,5},{7,4},{8,11},{9,10},{10,... | collective-permute-start | bytes 110600 | tf_op jit(solution)/shard_map/ppermute | solution.py:141
  6.5 1.9 %collective-permute-start.6 = (f32[64,128]{1,0:T(8,128)S(1)}, f32[64,128]{1,0:T(8,128)S(1)}, u32[]{:S(2)}, u32[]{:S(2)}) collective-permute-start(f32[64,128]{1,0:T(8,128)S(1)} %get-tuple-element.30), channel_id=1, source_target_pairs={{0,2},{1,3},{2,0},{3,1},{4,6},{5,7},{6,4},{7,5},{8,10},{9,11},{10,... | collective-permute-start | bytes 98312 | tf_op jit(solution)/shard_map/ppermute | solution.py:141
  8.4 0.0 collective-permute-start.7
  8.4 0.0 collective-permute-done.refs_1_
  8.4 0.2 %collective-permute-start.8 = (f32[64,128]{1,0:T(8,128)S(1)}, f32[64,128]{1,0:T(8,128)S(1)}, u32[]{:S(2)}, u32[]{:S(2)}) collective-permute-start(f32[64,128]{1,0:T(8,128)S(1)} %get-tuple-element.32), channel_id=1, source_target_pairs={{0,3},{1,2},{2,1},{3,0},{4,7},{5,6},{6,5},{7,4},{8,11},{9,10},{10,... | collective-permute-start | bytes 98312 | tf_op jit(solution)/shard_map/ppermute | solution.py:141
  8.6 0.0 collective-permute-done.1.refs_2_
  8.6 1.0 %collective-permute-done.2.refs_3_ = f32[72,128]{1,0:T(8,128)S(1)} collective-permute-done((f32[72,128]{1,0:T(8,128)S(1)}, f32[72,128]{1,0:T(8,128)S(1)}, u32[]{:S(2)}, u32[]{:S(2)}) %collective-permute-start.2) | collective-permute-done | bytes 36896 | tf_op jit(solution)/shard_map/ppermute | solution.py:141
  9.7 0.9 %rims.1 = (f32[16,128]{1,0:T(8,128)S(1)}, f32[40,128]{1,0:T(8,128)S(1)}, f32[16,128]{1,0:T(8,128)S(1)}, f32[40,128]{1,0:T(8,128)S(1)}, f32[144,384]{1,0:T(8,128)S(1)}, /*index=5*/f32[16,128]{1,0:T(8,128)S(1)}) custom-call(f32[72,128]{1,0:T(8,128)S(1)} %get-tuple-element.19.refs_0_, f32[72,128]{1,0:T(8,128)S(1)} %collective-permute-done.refs_1_, ...), custom_call_target="tpu_custom_call" | custom-call | tf_op jit(solution)/shard_map/rims/pallas_call | solution.py:483
  10.5 3.7 %collective-permute-start.4 = (f32[40,128]{1,0:T(8,128)S(1)}, f32[40,128]{1,0:T(8,128)S(1)}, u32[]{:S(2)}, u32[]{:S(2)}) collective-permute-start(f32[40,128]{1,0:T(8,128)S(1)} %get-tuple-element.25), channel_id=1, source_target_pairs={{0,12},{4,8},{8,4},{12,0},{1,13},{5,9},{9,5},{13,1},{2,14},{6,10},... | collective-permute-start | bytes 61448 | tf_op jit(solution)/shard_map/ppermute | solution.py:141
  14.2 0.0 collective-permute-start.5
  14.2 0.0 collective-permute-done.6.refs_1_
  14.2 0.8 %collective-permute-start.3 = (f32[16,128]{1,0:T(8,128)S(1)}, f32[16,128]{1,0:T(8,128)S(1)}, u32[]{:S(2)}, u32[]{:S(2)}) collective-permute-start(f32[16,128]{1,0:T(8,128)S(1)} %get-tuple-element.24), channel_id=1, source_target_pairs={{0,8},{4,12},{8,0},{12,4},{1,9},{5,13},{9,1},{13,5},{2,10},{6,14},... | collective-permute-start | bytes 24584 | tf_op jit(solution)/shard_map/ppermute | solution.py:141
  15.0 0.0 collective-permute-done.7.refs_2_
  15.0 0.0 collective-permute-done.8.refs_3_
  15.0 0.7 %outputs.1 = (f32[1,128,128]{2,1,0:T(8,128)}, f32[1,128,128]{2,1,0:T(8,128)}) custom-call(f32[64,128]{1,0:T(8,128)S(1)} %get-tuple-element.29.refs_0_, f32[64,128]{1,0:T(8,128)S(1)} %collective-permute-done.6.refs_1_, f32[64,128]{1,0:T(8,128)S(1)} %collective-permute-done.7.refs_2_, f32[64,128]{1,0:T(8,128)S(1)} %collective-permute-done.8.refs_3_), custom_call_target="tpu_custom_call" | custom-call | tf_op jit(solution)/shard_map/outputs/pallas_call | solution.py:495
  15.7 3.1 %collective-permute-done.3.refs_1_ = f32[16,128]{1,0:T(8,128)S(1)} collective-permute-done((f32[16,128]{1,0:T(8,128)S(1)}, f32[16,128]{1,0:T(8,128)S(1)}, u32[]{:S(2)}, u32[]{:S(2)}) %collective-permute-start.3) | collective-permute-done | bytes 8224 | tf_op jit(solution)/shard_map/ppermute | solution.py:141
  18.8 1.2 %phase.1 = f32[1,128,128]{2,1,0:T(8,128)} custom-call(f32[16,128]{1,0:T(8,128)S(1)} %get-tuple-element.23.refs_0_, f32[16,128]{1,0:T(8,128)S(1)} %collective-permute-done.3.refs_1_, f32[40,128]{1,0:T(8,128)S(1)} %collective-permute-done.4.refs_2_, f32[40,128]{1,0:T(8,128)S(1)} %collective-permute-done.5.refs_3_, f32[144,384]{1,0:T(8,128)S(1)} %get-tuple-element.27.refs_4_, ...), custom_call_target="tpu_custom_call" | custom-call | tf_op jit(solution)/shard_map/phase/pallas_call | solution.py:503
  (6 shorter events, 0.0 us)
Async XLA Ops:
  0.6 9.0 %copy-start = (f32[448,384]{1,0:T(8,128)S(1)}, f32[448,384]{1,0:T(8,128)}, u32[]{:S(2)}) copy-start(f32[448,384]{1,0:T(8,128)} %constant.11.clone.refs_7_.refs_8_) | copy-start | bytes 2064388
  0.6 9.0 %copy-start.1 = (bf16[432,432]{1,0:T(8,128)(2,1)S(1)}, bf16[432,432]{1,0:T(8,128)(2,1)}, u32[]{:S(2)}) copy-start(bf16[432,432]{1,0:T(8,128)(2,1)} %constant.10.clone.refs_6_.refs_7_) | copy-start | bytes 1119748
  0.7 9.0 %copy-start.2 = (bf16[1536,128]{1,0:T(8,128)(2,1)S(1)}, bf16[1536,128]{1,0:T(8,128)(2,1)}, u32[]{:S(2)}) copy-start(bf16[1536,128]{1,0:T(8,128)(2,1)} %constant.9.clone.refs_5_.refs_6_) | copy-start | bytes 1179652
  0.7 9.0 %copy-start.3 = (bf16[512,384]{1,0:T(8,128)(2,1)S(1)}, bf16[512,384]{1,0:T(8,128)(2,1)}, u32[]{:S(2)}) copy-start(bf16[512,384]{1,0:T(8,128)(2,1)} %constant.8.clone.refs_4_) | copy-start | bytes 1179652
  3.3 5.2 %collective-permute-start = (f32[72,128]{1,0:T(8,128)S(1)}, f32[72,128]{1,0:T(8,128)S(1)}, u32[]{:S(2)}, u32[]{:S(2)}) collective-permute-start(f32[72,128]{1,0:T(8,128)S(1)} %get-tuple-element.20), channel_id=1, source_target_pairs={{0,2},{1,3},{2,0},{3,1},{4,6},{5,7},{6,4},{7,5},{8,10},{9,11},{10,... | collective-permute-start | bytes 110600 | tf_op jit(solution)/shard_map/ppermute | solution.py:141
  6.3 2.4 %collective-permute-start.1 = (f32[72,128]{1,0:T(8,128)S(1)}, f32[72,128]{1,0:T(8,128)S(1)}, u32[]{:S(2)}, u32[]{:S(2)}) collective-permute-start(f32[72,128]{1,0:T(8,128)S(1)} %get-tuple-element.21), channel_id=1, source_target_pairs={{0,1},{1,0},{2,3},{3,2},{4,5},{5,4},{6,7},{7,6},{8,9},{9,8},{10,11... | collective-permute-start | bytes 110600 | tf_op jit(solution)/shard_map/ppermute | solution.py:141
  6.3 3.4 %collective-permute-start.2 = (f32[72,128]{1,0:T(8,128)S(1)}, f32[72,128]{1,0:T(8,128)S(1)}, u32[]{:S(2)}, u32[]{:S(2)}) collective-permute-start(f32[72,128]{1,0:T(8,128)S(1)} %get-tuple-element.22), channel_id=1, source_target_pairs={{0,3},{1,2},{2,1},{3,0},{4,7},{5,6},{6,5},{7,4},{8,11},{9,10},{10,... | collective-permute-start | bytes 110600 | tf_op jit(solution)/shard_map/ppermute | solution.py:141
  6.5 7.8 %collective-permute-start.6 = (f32[64,128]{1,0:T(8,128)S(1)}, f32[64,128]{1,0:T(8,128)S(1)}, u32[]{:S(2)}, u32[]{:S(2)}) collective-permute-start(f32[64,128]{1,0:T(8,128)S(1)} %get-tuple-element.30), channel_id=1, source_target_pairs={{0,2},{1,3},{2,0},{3,1},{4,6},{5,7},{6,4},{7,5},{8,10},{9,11},{10,... | collective-permute-start | bytes 98312 | tf_op jit(solution)/shard_map/ppermute | solution.py:141
  8.4 6.6 %collective-permute-start.7 = (f32[64,128]{1,0:T(8,128)S(1)}, f32[64,128]{1,0:T(8,128)S(1)}, u32[]{:S(2)}, u32[]{:S(2)}) collective-permute-start(f32[64,128]{1,0:T(8,128)S(1)} %get-tuple-element.31), channel_id=1, source_target_pairs={{0,1},{1,0},{2,3},{3,2},{4,5},{5,4},{6,7},{7,6},{8,9},{9,8},{10,11... | collective-permute-start | bytes 98312 | tf_op jit(solution)/shard_map/ppermute | solution.py:141
  8.4 6.6 %collective-permute-start.8 = (f32[64,128]{1,0:T(8,128)S(1)}, f32[64,128]{1,0:T(8,128)S(1)}, u32[]{:S(2)}, u32[]{:S(2)}) collective-permute-start(f32[64,128]{1,0:T(8,128)S(1)} %get-tuple-element.32), channel_id=1, source_target_pairs={{0,3},{1,2},{2,1},{3,0},{4,7},{5,6},{6,5},{7,4},{8,11},{9,10},{10,... | collective-permute-start | bytes 98312 | tf_op jit(solution)/shard_map/ppermute | solution.py:141
  10.5 8.2 %collective-permute-start.4 = (f32[40,128]{1,0:T(8,128)S(1)}, f32[40,128]{1,0:T(8,128)S(1)}, u32[]{:S(2)}, u32[]{:S(2)}) collective-permute-start(f32[40,128]{1,0:T(8,128)S(1)} %get-tuple-element.25), channel_id=1, source_target_pairs={{0,12},{4,8},{8,4},{12,0},{1,13},{5,9},{9,5},{13,1},{2,14},{6,10},... | collective-permute-start | bytes 61448 | tf_op jit(solution)/shard_map/ppermute | solution.py:141
  14.2 4.6 %collective-permute-start.5 = (f32[40,128]{1,0:T(8,128)S(1)}, f32[40,128]{1,0:T(8,128)S(1)}, u32[]{:S(2)}, u32[]{:S(2)}) collective-permute-start(f32[40,128]{1,0:T(8,128)S(1)} %get-tuple-element.26), channel_id=1, source_target_pairs={{0,4},{4,0},{8,12},{12,8},{1,5},{5,1},{9,13},{13,9},{2,6},{6,2},{1... | collective-permute-start | bytes 61448 | tf_op jit(solution)/shard_map/ppermute | solution.py:141
  14.2 4.6 %collective-permute-start.3 = (f32[16,128]{1,0:T(8,128)S(1)}, f32[16,128]{1,0:T(8,128)S(1)}, u32[]{:S(2)}, u32[]{:S(2)}) collective-permute-start(f32[16,128]{1,0:T(8,128)S(1)} %get-tuple-element.24), channel_id=1, source_target_pairs={{0,8},{4,12},{8,0},{12,4},{1,9},{5,13},{9,1},{13,5},{2,10},{6,14},... | collective-permute-start | bytes 24584 | tf_op jit(solution)/shard_map/ppermute | solution.py:141

commit v12 on v11

--- a/solution.py
+++ b/solution.py
@@ -126,7 +126,7 @@
     return jnp.where(hit, power(offset_of(place), kind), 0.0).astype(BF16)
 
 
-ORDER = {1: (), 2: (1,), 4: (2, 3, 1)}
+ORDER = {1: (), 2: (1,), 4: (3, 1, 2)}
 CELL_ORDER = {1: (), 2: (1,), 4: (2, 1, 3)}
 
 

time: 20.1 us -> 20.1 us (level)
  no operation moved by 1% of the time
where the time goes in v12:
time: 20.1 us; the launch traced here: 20 us
  starting transfers between devices  9.8 us (49%)
  Pallas kernels  5.32 us (26%)
  waiting for transfers between devices  4.14 us (21%)
  between operations  0.7 us (3%)
    ppermute x9, starting transfers between devices, exchange(): lax.ppermute(pieces[k], axes, [(i, i ^ k) for i in range(count)])  9.8 us
    ppermute x9, waiting for transfers between devices, exchange(): lax.ppermute(pieces[k], axes, [(i, i ^ k) for i in range(count)])  4.14 us
    pallas_call x1, Pallas kernels, body(): pl.pallas_call(functools.partial(moments_kernel, (frames, stripe, blocks,...  2.56 us
    pallas_call x1, Pallas kernels, body(): pl.pallas_call(functools.partial(phase_kernel, sizes), out_shape=jax.Shap...  1.21 us
    pallas_call x1, Pallas kernels, body(): pl.pallas_call(functools.partial(rims_kernel, sizes), out_shape=row_shape...  0.87 us
    pallas_call x1, Pallas kernels, body(): pl.pallas_call(functools.partial(outputs_kernel, sizes), out_shape=[jax.S...  0.67 us
  transfers between devices with their start and end apart: 9, of which 2 were waited for; matrix products, arithmetic and copies ran while one was open for 0% of the time, Pallas kernels for 8%

profile of v12, /device:TPU:0, one launch (start us, length us, event | category | flops | bytes accessed | tf_op | source)
XLA Modules:
  0.0 20.0 jit_solution(2719812622315196042)
XLA Ops:
  0.6 0.0 copy-start
  0.6 0.0 copy-start.1
  0.7 0.0 copy-start.2
  0.7 0.0 copy-start.3
  0.7 2.6 %moments.1 = (f32[72,128]{1,0:T(8,128)S(1)}, f32[72,128]{1,0:T(8,128)S(1)}, f32[72,128]{1,0:T(8,128)S(1)}, f32[72,128]{1,0:T(8,128)S(1)}, f32[64,128]{1,0:T(8,12...) custom-call(bf16[2,256,2048]{2,1,0:T(8,128)(2,1)} %pixels.1), custom_call_target="tpu_custom_call" | custom-call | tf_op jit(solution)/shard_map/moments/pallas_call | solution.py:439
  3.3 3.0 %collective-permute-start = (f32[72,128]{1,0:T(8,128)S(1)}, f32[72,128]{1,0:T(8,128)S(1)}, u32[]{:S(2)}, u32[]{:S(2)}) collective-permute-start(f32[72,128]{1,0:T(8,128)S(1)} %get-tuple-element.20), channel_id=1, source_target_pairs={{0,2},{1,3},{2,0},{3,1},{4,6},{5,7},{6,4},{7,5},{8,10},{9,11},{10,... | collective-permute-start | bytes 110600 | tf_op jit(solution)/shard_map/ppermute | solution.py:141
  6.3 0.0 collective-permute-start.1
  6.3 0.2 %collective-permute-start.2 = (f32[72,128]{1,0:T(8,128)S(1)}, f32[72,128]{1,0:T(8,128)S(1)}, u32[]{:S(2)}, u32[]{:S(2)}) collective-permute-start(f32[72,128]{1,0:T(8,128)S(1)} %get-tuple-element.22), channel_id=1, source_target_pairs={{0,3},{1,2},{2,1},{3,0},{4,7},{5,6},{6,5},{7,4},{8,11},{9,10},{10,... | collective-permute-start | bytes 110600 | tf_op jit(solution)/shard_map/ppermute | solution.py:141
  6.5 1.9 %collective-permute-start.6 = (f32[64,128]{1,0:T(8,128)S(1)}, f32[64,128]{1,0:T(8,128)S(1)}, u32[]{:S(2)}, u32[]{:S(2)}) collective-permute-start(f32[64,128]{1,0:T(8,128)S(1)} %get-tuple-element.30), channel_id=1, source_target_pairs={{0,2},{1,3},{2,0},{3,1},{4,6},{5,7},{6,4},{7,5},{8,10},{9,11},{10,... | collective-permute-start | bytes 98312 | tf_op jit(solution)/shard_map/ppermute | solution.py:141
  8.4 0.0 collective-permute-start.7
  8.4 0.0 collective-permute-done.refs_1_
  8.4 0.2 %collective-permute-start.8 = (f32[64,128]{1,0:T(8,128)S(1)}, f32[64,128]{1,0:T(8,128)S(1)}, u32[]{:S(2)}, u32[]{:S(2)}) collective-permute-start(f32[64,128]{1,0:T(8,128)S(1)} %get-tuple-element.32), channel_id=1, source_target_pairs={{0,3},{1,2},{2,1},{3,0},{4,7},{5,6},{6,5},{7,4},{8,11},{9,10},{10,... | collective-permute-start | bytes 98312 | tf_op jit(solution)/shard_map/ppermute | solution.py:141
  8.6 0.0 collective-permute-done.1.refs_2_
  8.6 1.0 %collective-permute-done.2.refs_3_ = f32[72,128]{1,0:T(8,128)S(1)} collective-permute-done((f32[72,128]{1,0:T(8,128)S(1)}, f32[72,128]{1,0:T(8,128)S(1)}, u32[]{:S(2)}, u32[]{:S(2)}) %collective-permute-start.2) | collective-permute-done | bytes 36896 | tf_op jit(solution)/shard_map/ppermute | solution.py:141
  9.7 0.9 %rims.1 = (f32[16,128]{1,0:T(8,128)S(1)}, f32[40,128]{1,0:T(8,128)S(1)}, f32[16,128]{1,0:T(8,128)S(1)}, f32[40,128]{1,0:T(8,128)S(1)}, f32[144,384]{1,0:T(8,128)S(1)}, /*index=5*/f32[16,128]{1,0:T(8,128)S(1)}) custom-call(f32[72,128]{1,0:T(8,128)S(1)} %get-tuple-element.19.refs_0_, f32[72,128]{1,0:T(8,128)S(1)} %collective-permute-done.refs_1_, ...), custom_call_target="tpu_custom_call" | custom-call | tf_op jit(solution)/shard_map/rims/pallas_call | solution.py:483
  10.5 3.7 %collective-permute-start.3 = (f32[40,128]{1,0:T(8,128)S(1)}, f32[40,128]{1,0:T(8,128)S(1)}, u32[]{:S(2)}, u32[]{:S(2)}) collective-permute-start(f32[40,128]{1,0:T(8,128)S(1)} %get-tuple-element.24), channel_id=1, source_target_pairs={{0,12},{4,8},{8,4},{12,0},{1,13},{5,9},{9,5},{13,1},{2,14},{6,10},... | collective-permute-start | bytes 61448 | tf_op jit(solution)/shard_map/ppermute | solution.py:141
  14.2 0.8 %collective-permute-start.5 = (f32[16,128]{1,0:T(8,128)S(1)}, f32[16,128]{1,0:T(8,128)S(1)}, u32[]{:S(2)}, u32[]{:S(2)}) collective-permute-start(f32[16,128]{1,0:T(8,128)S(1)} %get-tuple-element.26), channel_id=1, source_target_pairs={{0,8},{4,12},{8,0},{12,4},{1,9},{5,13},{9,1},{13,5},{2,10},{6,14},... | collective-permute-start | bytes 24584 | tf_op jit(solution)/shard_map/ppermute | solution.py:141
  15.0 0.0 collective-permute-done.7.refs_2_
  15.0 0.0 collective-permute-done.8.refs_3_
  15.0 0.7 %outputs.1 = (f32[1,128,128]{2,1,0:T(8,128)}, f32[1,128,128]{2,1,0:T(8,128)}) custom-call(f32[64,128]{1,0:T(8,128)S(1)} %get-tuple-element.29.refs_0_, f32[64,128]{1,0:T(8,128)S(1)} %collective-permute-done.6.refs_1_, f32[64,128]{1,0:T(8,128)S(1)} %collective-permute-done.7.refs_2_, f32[64,128]{1,0:T(8,128)S(1)} %collective-permute-done.8.refs_3_), custom_call_target="tpu_custom_call" | custom-call | tf_op jit(solution)/shard_map/outputs/pallas_call | solution.py:495
  15.7 3.1 %collective-permute-done.5.refs_3_ = f32[16,128]{1,0:T(8,128)S(1)} collective-permute-done((f32[16,128]{1,0:T(8,128)S(1)}, f32[16,128]{1,0:T(8,128)S(1)}, u32[]{:S(2)}, u32[]{:S(2)}) %collective-permute-start.5) | collective-permute-done | bytes 8224 | tf_op jit(solution)/shard_map/ppermute | solution.py:141
  18.8 0.0 collective-permute-done.3.refs_1_
  18.8 0.0 collective-permute-done.4.refs_2_
  18.8 1.2 %phase.1 = f32[1,128,128]{2,1,0:T(8,128)} custom-call(f32[16,128]{1,0:T(8,128)S(1)} %get-tuple-element.23.refs_0_, f32[40,128]{1,0:T(8,128)S(1)} %collective-permute-done.3.refs_1_, f32[40,128]{1,0:T(8,128)S(1)} %collective-permute-done.4.refs_2_, f32[16,128]{1,0:T(8,128)S(1)} %collective-permute-done.5.refs_3_, f32[144,384]{1,0:T(8,128)S(1)} %get-tuple-element.27.refs_4_, ...), custom_call_target="tpu_custom_call" | custom-call | tf_op jit(solution)/shard_map/phase/pallas_call | solution.py:503
  (6 shorter events, 0.0 us)
Async XLA Ops:
  0.6 9.0 %copy-start = (f32[448,384]{1,0:T(8,128)S(1)}, f32[448,384]{1,0:T(8,128)}, u32[]{:S(2)}) copy-start(f32[448,384]{1,0:T(8,128)} %constant.11.clone.refs_7_.refs_8_) | copy-start | bytes 2064388
  0.6 9.0 %copy-start.1 = (bf16[432,432]{1,0:T(8,128)(2,1)S(1)}, bf16[432,432]{1,0:T(8,128)(2,1)}, u32[]{:S(2)}) copy-start(bf16[432,432]{1,0:T(8,128)(2,1)} %constant.10.clone.refs_6_.refs_7_) | copy-start | bytes 1119748
  0.7 9.0 %copy-start.2 = (bf16[1536,128]{1,0:T(8,128)(2,1)S(1)}, bf16[1536,128]{1,0:T(8,128)(2,1)}, u32[]{:S(2)}) copy-start(bf16[1536,128]{1,0:T(8,128)(2,1)} %constant.9.clone.refs_5_.refs_6_) | copy-start | bytes 1179652
  0.7 9.0 %copy-start.3 = (bf16[512,384]{1,0:T(8,128)(2,1)S(1)}, bf16[512,384]{1,0:T(8,128)(2,1)}, u32[]{:S(2)}) copy-start(bf16[512,384]{1,0:T(8,128)(2,1)} %constant.8.clone.refs_4_) | copy-start | bytes 1179652
  3.3 5.2 %collective-permute-start = (f32[72,128]{1,0:T(8,128)S(1)}, f32[72,128]{1,0:T(8,128)S(1)}, u32[]{:S(2)}, u32[]{:S(2)}) collective-permute-start(f32[72,128]{1,0:T(8,128)S(1)} %get-tuple-element.20), channel_id=1, source_target_pairs={{0,2},{1,3},{2,0},{3,1},{4,6},{5,7},{6,4},{7,5},{8,10},{9,11},{10,... | collective-permute-start | bytes 110600 | tf_op jit(solution)/shard_map/ppermute | solution.py:141
  6.3 2.4 %collective-permute-start.1 = (f32[72,128]{1,0:T(8,128)S(1)}, f32[72,128]{1,0:T(8,128)S(1)}, u32[]{:S(2)}, u32[]{:S(2)}) collective-permute-start(f32[72,128]{1,0:T(8,128)S(1)} %get-tuple-element.21), channel_id=1, source_target_pairs={{0,1},{1,0},{2,3},{3,2},{4,5},{5,4},{6,7},{7,6},{8,9},{9,8},{10,11... | collective-permute-start | bytes 110600 | tf_op jit(solution)/shard_map/ppermute | solution.py:141
  6.3 3.4 %collective-permute-start.2 = (f32[72,128]{1,0:T(8,128)S(1)}, f32[72,128]{1,0:T(8,128)S(1)}, u32[]{:S(2)}, u32[]{:S(2)}) collective-permute-start(f32[72,128]{1,0:T(8,128)S(1)} %get-tuple-element.22), channel_id=1, source_target_pairs={{0,3},{1,2},{2,1},{3,0},{4,7},{5,6},{6,5},{7,4},{8,11},{9,10},{10,... | collective-permute-start | bytes 110600 | tf_op jit(solution)/shard_map/ppermute | solution.py:141
  6.5 7.8 %collective-permute-start.6 = (f32[64,128]{1,0:T(8,128)S(1)}, f32[64,128]{1,0:T(8,128)S(1)}, u32[]{:S(2)}, u32[]{:S(2)}) collective-permute-start(f32[64,128]{1,0:T(8,128)S(1)} %get-tuple-element.30), channel_id=1, source_target_pairs={{0,2},{1,3},{2,0},{3,1},{4,6},{5,7},{6,4},{7,5},{8,10},{9,11},{10,... | collective-permute-start | bytes 98312 | tf_op jit(solution)/shard_map/ppermute | solution.py:141
  8.4 6.6 %collective-permute-start.7 = (f32[64,128]{1,0:T(8,128)S(1)}, f32[64,128]{1,0:T(8,128)S(1)}, u32[]{:S(2)}, u32[]{:S(2)}) collective-permute-start(f32[64,128]{1,0:T(8,128)S(1)} %get-tuple-element.31), channel_id=1, source_target_pairs={{0,1},{1,0},{2,3},{3,2},{4,5},{5,4},{6,7},{7,6},{8,9},{9,8},{10,11... | collective-permute-start | bytes 98312 | tf_op jit(solution)/shard_map/ppermute | solution.py:141
  8.4 6.6 %collective-permute-start.8 = (f32[64,128]{1,0:T(8,128)S(1)}, f32[64,128]{1,0:T(8,128)S(1)}, u32[]{:S(2)}, u32[]{:S(2)}) collective-permute-start(f32[64,128]{1,0:T(8,128)S(1)} %get-tuple-element.32), channel_id=1, source_target_pairs={{0,3},{1,2},{2,1},{3,0},{4,7},{5,6},{6,5},{7,4},{8,11},{9,10},{10,... | collective-permute-start | bytes 98312 | tf_op jit(solution)/shard_map/ppermute | solution.py:141
  10.5 8.2 %collective-permute-start.3 = (f32[40,128]{1,0:T(8,128)S(1)}, f32[40,128]{1,0:T(8,128)S(1)}, u32[]{:S(2)}, u32[]{:S(2)}) collective-permute-start(f32[40,128]{1,0:T(8,128)S(1)} %get-tuple-element.24), channel_id=1, source_target_pairs={{0,12},{4,8},{8,4},{12,0},{1,13},{5,9},{9,5},{13,1},{2,14},{6,10},... | collective-permute-start | bytes 61448 | tf_op jit(solution)/shard_map/ppermute | solution.py:141
  14.2 4.6 %collective-permute-start.4 = (f32[40,128]{1,0:T(8,128)S(1)}, f32[40,128]{1,0:T(8,128)S(1)}, u32[]{:S(2)}, u32[]{:S(2)}) collective-permute-start(f32[40,128]{1,0:T(8,128)S(1)} %get-tuple-element.25), channel_id=1, source_target_pairs={{0,4},{4,0},{8,12},{12,8},{1,5},{5,1},{9,13},{13,9},{2,6},{6,2},{1... | collective-permute-start | bytes 61448 | tf_op jit(solution)/shard_map/ppermute | solution.py:141
  14.2 4.6 %collective-permute-start.5 = (f32[16,128]{1,0:T(8,128)S(1)}, f32[16,128]{1,0:T(8,128)S(1)}, u32[]{:S(2)}, u32[]{:S(2)}) collective-permute-start(f32[16,128]{1,0:T(8,128)S(1)} %get-tuple-element.26), channel_id=1, source_target_pairs={{0,8},{4,12},{8,0},{12,4},{1,9},{5,13},{9,1},{13,5},{2,10},{6,14},... | collective-permute-start | bytes 24584 | tf_op jit(solution)/shard_map/ppermute | solution.py:141
